TPU v7x, 256 devices: a whole 4x4x8 slice. The times are simulated.
256 devices in a mesh: seq: 32 (over y, z), chan: 8 (over x, core).
Axes of the slice: x: 4, y: 4, z: 8, core: 2. Of those that a mesh axis runs over, the one named last changes fastest.
Arguments:
- targets: int32 [32768], P('seq'), may hold values from 0 to 4
- resid: bfloat16 [32768, 2560], P('seq', 'chan'), may hold values from -6 to 6
- w_gate_in: bfloat16 [2560, 2560], P('seq', 'chan'), may hold values from -0.125 to 0.125
- w_x_in: bfloat16 [2560, 2560], P('seq', 'chan'), may hold values from -0.125 to 0.125
- conv_weight: float32 [4, 2560], P(None, 'chan'), may hold values from -3 to 3
- conv_bias: float32 [2560], P('chan'), may hold values from -3 to 3
- skip_d: float32 [40], P('chan'), may hold values from 0.5 to 2
- norm_gain: float32 [2560], P('chan'), may hold values from 0.1 to 1.9
- w_out: bfloat16 [2560, 2560], P('seq', 'chan'), may hold values from -0.125 to 0.125
- w_head: bfloat16 [2560, 16], P('chan'), may hold values from -0.375 to 0.375
Outputs:
- new_resid: bfloat16 [32768, 2560], P('seq', 'chan')
- grad_gate_in: float32 [2560, 2560], P('seq', 'chan')
- grad_x_in: float32 [2560, 2560], P('seq', 'chan')
- grad_out: float32 [2560, 2560], P('seq', 'chan')
- grad_head: float32 [2560, 16], P('chan')
- grad_conv_weight: float32 [4, 2560], P(None, 'chan')
- grad_conv_bias: float32 [2560], P('chan')
- grad_skip: float32 [40], P('chan')
- grad_gain: float32 [2560], P('chan')
All inputs are finite; a program needn't handle non-finite values.
Results may differ from a plain program's by a relative error of at most 0.035.
Values may be sent and summed in bfloat16 or wider, within the bound.
A program may use at most 128 MiB of HBM per device.

v0:
```python
import jax
import jax.numpy as jnp
from jax import lax
from jax.sharding import PartitionSpec as P

HEADDIM = 64
KERNEL = 4
VOCAB = 16
INNER = 2560


def shifted(array, axis, by):
    length = lax.axis_size(axis)
    pairs = [(i, i + by) for i in range(length) if 0 <= i + by < length]
    return lax.ppermute(array, axis, pairs)


def slope(value, sig):
    return sig * (1.0 + value * (1.0 - sig))


def inner_rows(left, right):
    return lax.dot_general(
        left, right, (((0,), (0,)), ((), ())), preferred_element_type=jnp.float32
    )


def per_device(
    targets, resid, w_gate_in, w_x_in, conv_weight, conv_bias, skip_d, norm_gain, w_out, w_head
):
    f32 = jnp.float32
    bf16 = jnp.bfloat16
    tok_rows = resid.shape[0]
    seq_count = lax.axis_size("seq")
    local_inner = w_gate_in.shape[1]
    halo_rows = KERNEL - 1
    features = lax.all_gather(resid, "chan", axis=1, tiled=True)
    gate_sum = jnp.dot(
        features, lax.all_gather(w_gate_in, "seq", axis=0, tiled=True), preferred_element_type=f32
    )
    x_sum = jnp.dot(
        features, lax.all_gather(w_x_in, "seq", axis=0, tiled=True), preferred_element_type=f32
    )
    gate_pre = gate_sum.astype(bf16)
    x_pre = x_sum.astype(bf16)
    before = shifted(x_pre[tok_rows - halo_rows :], "seq", 1)
    padded = jnp.concatenate([before, x_pre], axis=0).astype(f32)
    conv_out = jnp.zeros((tok_rows, local_inner), f32) + conv_bias
    for offset in range(KERNEL):
        conv_out = conv_out + conv_weight[offset] * padded[offset : offset + tok_rows]
    sig_conv = jax.nn.sigmoid(conv_out)
    active = conv_out * sig_conv
    gate_f32 = gate_pre.astype(f32)
    sig_gate = jax.nn.sigmoid(gate_f32)
    silu_gate = gate_f32 * sig_gate
    head_scale = jnp.repeat(skip_d, HEADDIM)
    gated = active * head_scale * silu_gate
    sq_sum = lax.psum(jnp.sum(gated * gated, axis=1), "chan")
    inverse = lax.rsqrt(sq_sum / INNER + 1e-05)
    normed = (gated * inverse[:, None] * norm_gain).astype(bf16)
    full_normed = lax.all_gather(normed, "chan", axis=1, tiled=True)
    out_cols = lax.all_gather(w_out, "seq", axis=0, tiled=True)
    new_resid = (
        resid.astype(f32) + jnp.dot(full_normed, out_cols, preferred_element_type=f32)
    ).astype(bf16)
    part_logits = jnp.dot(new_resid, w_head, preferred_element_type=f32)
    logits = lax.psum(part_logits.astype(jnp.bfloat16), "chan").astype(jnp.float32)
    raised = jnp.exp(logits)
    probs = raised / jnp.sum(raised, axis=1, keepdims=True)
    onehot = (targets[:, None] == jnp.arange(VOCAB, dtype=jnp.int32)[None, :]).astype(f32)
    loss_weight = 4.0 / jnp.sqrt(jnp.asarray(tok_rows * seq_count, f32))
    dlogit = (probs - onehot) * loss_weight
    head_local = jnp.dot(new_resid.astype(f32).T, dlogit, precision=lax.Precision.HIGHEST)
    dresid = jnp.dot(dlogit, w_head.astype(f32).T, precision=lax.Precision.HIGHEST).astype(bf16)
    summed = lax.psum(inner_rows(full_normed, dresid).astype(jnp.bfloat16), "seq").astype(
        jnp.float32
    )
    row_count = summed.shape[0] // seq_count
    grad_out = lax.dynamic_slice_in_dim(summed, lax.axis_index("seq") * row_count, row_count, 0)
    norm_term = jnp.dot(dresid, out_cols.T, preferred_element_type=f32)
    dnormed = lax.psum_scatter(
        norm_term.astype(jnp.bfloat16), "chan", scatter_dimension=1, tiled=True
    ).astype(jnp.float32)
    dot_gn = lax.psum(jnp.sum(gated * norm_gain * dnormed, axis=1), "chan")
    dgated = inverse[:, None] * norm_gain * dnormed - gated * (inverse**3 * dot_gn / INNER)[:, None]
    gain_local = jnp.sum(dnormed * gated * inverse[:, None], axis=0)
    skip_local = jnp.sum(dgated * active * silu_gate, axis=0).reshape(-1, HEADDIM).sum(axis=1)
    dgate = (dgated * active * head_scale * slope(gate_f32, sig_gate)).astype(bf16)
    dconv = dgated * head_scale * silu_gate * slope(conv_out, sig_conv)
    bias_local = jnp.sum(dconv, axis=0)
    taps_local = jnp.stack(
        [jnp.sum(dconv * padded[offset : offset + tok_rows], axis=0) for offset in range(KERNEL)]
    )
    future = shifted(dconv[:halo_rows], "seq", -1)
    dpadded = jnp.concatenate([dconv, future], axis=0)
    dx_sum = jnp.zeros((tok_rows, local_inner), f32)
    for offset in range(KERNEL):
        dx_sum = (
            dx_sum
            + conv_weight[offset] * dpadded[halo_rows - offset : halo_rows - offset + tok_rows]
        )
    dx_pre = dx_sum.astype(bf16)
    both_grads = jnp.concatenate([dgate, dx_pre], axis=1)
    grad_both = lax.psum_scatter(
        inner_rows(features, both_grads).astype(jnp.bfloat16),
        "seq",
        scatter_dimension=0,
        tiled=True,
    ).astype(jnp.float32)
    grad_gate_in = grad_both[:, :local_inner]
    grad_x_in = grad_both[:, local_inner:]
    grad_head, grad_conv_weight, grad_conv_bias, grad_skip, grad_gain = lax.psum(
        (head_local, taps_local, bias_local, skip_local, gain_local), "seq"
    )
    return (
        new_resid,
        grad_gate_in,
        grad_x_in,
        grad_out,
        grad_head,
        grad_conv_weight,
        grad_conv_bias,
        grad_skip,
        grad_gain,
    )


def solution(mesh):
    return jax.shard_map(
        per_device,
        mesh=mesh,
        in_specs=(
            P("seq"),
            P("seq", "chan"),
            P("seq", "chan"),
            P("seq", "chan"),
            P(None, "chan"),
            P("chan"),
            P("chan"),
            P("chan"),
            P("seq", "chan"),
            P("chan", None),
        ),
        out_specs=(
            P("seq", "chan"),
            P("seq", "chan"),
            P("seq", "chan"),
            P("seq", "chan"),
            P("chan", None),
            P(None, "chan"),
            P("chan"),
            P("chan"),
            P("chan"),
        ),
        check_vma=False,
    )
```

profile of v0, /device:TPU:1, one launch (start us, length us, event | category | flops | bytes accessed | tf_op | source)
XLA Modules:
  0.0 773.0 jit_solution(8640452376771448256)
XLA Ops:
  7.2 0.7 all-gather.8.cloned.1.call-update
  8.0 0.7 all-gather.6.cloned.1.call-update
  8.7 0.7 all-gather.10.cloned.1.call-update
  9.5 0.5 all-gather.14.cloned.1.call-update
  10.1 78.3 %all-gather.8.cloned.1.call-done = bf16[2560,320]{1,0:T(8,128)(2,1)} async-done(((bf16[80,320]{1,0:T(8,128)(2,1)}), bf16[2560,320]{1,0:T(8,128)(2,1)}) %all-gather.8.cloned.1.call-update) | async-done | bytes 1638416 | tf_op jit(solution)/shard_map/all_gather | solution.py:42
  88.3 42.4 %all-gather.6.cloned.1.call-done = bf16[1024,2560]{0,1:T(8,128)(2,1)} async-done(((bf16[1024,320]{0,1:T(8,128)(2,1)}), bf16[1024,2560]{0,1:T(8,128)(2,1)}) %all-gather.6.cloned.1.call-update) | async-done | bytes 5242896 | tf_op jit(solution)/shard_map/all_gather | solution.py:37
  130.8 5.0 convolution_convert_fusion.5
  135.8 0.1 slice.68
  135.9 3.2 collective-permute-start
  139.2 0.1 mul.217
  139.3 1.3 collective-permute-done
  140.6 0.3 maximum_convert_fusion
  140.9 66.1 %all-gather.10.cloned.1.call-done = bf16[2560,320]{1,0:T(8,128)(2,1)} async-done(((bf16[80,320]{1,0:T(8,128)(2,1)}), bf16[2560,320]{1,0:T(8,128)(2,1)}) %all-gather.10.cloned.1.call-update) | async-done | bytes 1638416 | tf_op jit(solution)/shard_map/all_gather | solution.py:39
  206.9 6.6 multiply_reduce_fusion.5
  213.5 16.3 %psum.63 = f32[1024]{0:T(1024)S(1)} all-reduce(f32[1024]{0:T(1024)S(1)} %get-tuple-element.55), channel_id=1, replica_groups=mesh['seq'=32,'chan'=8] {'chan'}, use_global_device_ids=true, to_apply=%region_1.0 | all-reduce | flops 1024 | bytes 8192 | tf_op jit(solution)/shard_map/psum | solution.py:58
  229.8 1.0 multiply_convert_fusion
  230.9 53.6 %all-gather.14.cloned.1.call-done = bf16[2560,320]{1,0:T(8,128)(2,1)} async-done(((bf16[80,320]{1,0:T(8,128)(2,1)}), bf16[2560,320]{1,0:T(8,128)(2,1)}) %all-gather.14.cloned.1.call-update) | async-done | bytes 1638416 | tf_op jit(solution)/shard_map/all_gather | solution.py:62
  284.4 42.9 %all-gather.12.cloned.1.call-done = bf16[1024,2560]{0,1:T(8,128)(2,1)} async-done(((bf16[1024,320]{0,1:T(8,128)(2,1)}), bf16[1024,2560]{0,1:T(8,128)(2,1)}) %all-gather.12.cloned.1.call-update) | async-done | bytes 5242896 | tf_op jit(solution)/shard_map/all_gather | solution.py:61
  327.3 5.1 fusion.1
  332.4 0.8 copy-done.1
  333.2 0.2 convolution_convert_fusion.6
  333.4 20.9 %psum.64 = bf16[1024,16]{0,1:T(8,128)(2,1)S(1)} all-reduce(bf16[1024,16]{0,1:T(8,128)(2,1)S(1)} %convolution_convert_fusion.6), channel_id=1, replica_groups=mesh['seq'=32,'chan'=8] {'chan'}, use_global_device_ids=true, to_apply=%region_2.0 | all-reduce | flops 16384 | bytes 65536 | tf_op jit(solution)/shard_map/psum | solution.py:67
  354.3 0.7 convolution_convert_fusion.3
  355.1 0.8 copy-done.3
  355.9 6.3 convolution_convert_fusion
  362.2 0.2 all-reduce.3.cloned.1.call-start
  362.4 6.8 convolution_convert_fusion.2
  369.3 34.6 %reduce-scatter.5.cloned.1.call-done = bf16[1024,320]{0,1:T(8,128)(2,1)} async-done(((bf16[1024,2560]{0,1:T(8,128)(2,1)}), bf16[1024,320]{0,1:T(8,128)(2,1)}) %reduce-scatter.5.cloned.1.call-update) | async-done | bytes 655376 | tf_op jit(solution)/shard_map/reduce_scatter | solution.py:81
  403.9 1.6 fusion.20
  405.5 15.1 %psum.65 = f32[1024]{0:T(1024)S(1)} all-reduce(f32[1024]{0:T(1024)S(1)} %get-tuple-element.41), channel_id=1, replica_groups=mesh['seq'=32,'chan'=8] {'chan'}, use_global_device_ids=true, to_apply=%region_6.0 | all-reduce | flops 1024 | bytes 8192 | tf_op jit(solution)/shard_map/psum | solution.py:84
  420.5 4.0 multiply_reduce_fusion
  424.5 1.3 collective-permute-start.1
  425.8 0.5 fusion.16
  426.4 6.8 collective-permute-done.1
  433.2 1.5 fusion.7
  434.8 7.0 fusion
  441.7 3.4 copy.25
  445.2 1.1 copy-done.2
  446.3 0.6 fusion.28
  446.9 113.1 %all-reduce.3.cloned.1.call-done = bf16[2560,320]{1,0:T(8,128)(2,1)} async-done(((bf16[2560,320]{1,0:T(8,128)(2,1)}), bf16[2560,320]{1,0:T(8,128)(2,1)}) %all-reduce.3.cloned.1.call-update) | async-done | bytes 1638416 | tf_op jit(solution)/shard_map/psum | solution.py:75
  560.0 1.5 dynamic-slice_convert_fusion
  561.5 0.1 reshape.28
  561.6 0.1 reduce_sum.108
  561.7 112.7 %all-reduce = (f32[320,16]{0,1:T(8,128)}, f32[4,320]{1,0:T(4,128)}, f32[320]{0:T(512)}, f32[5]{0:T(128)}, f32[320]{0:T(512)}) all-reduce(f32[320,16]{0,1:T(8,128)S(1)} %fusion.28, f32[4,320]{1,0:T(4,128)S(1)} %pad_maximum_fusion.1, f32[320]{0:T(512)S(1)} %get-tuple-element.58, ...), channel_id=1, replica_groups=mesh['seq'=32,'chan'=8] {'seq'}, use_global_device_ids=true, to_apply=%region_9.0 | all-reduce | flops 7045 | bytes 56360 | tf_op jit(solution)/shard_map/psum | solution.py:112
  674.4 89.2 %reduce-scatter.7.cloned.1.call-done = bf16[80,640]{1,0:T(8,128)(2,1)} async-done(((bf16[2560,640]{1,0:T(8,128)(2,1)}), bf16[80,640]{1,0:T(8,128)(2,1)}) %reduce-scatter.7.cloned.1.call-update) | async-done | bytes 102416
  763.6 1.1 copy.26
  764.6 0.8 copy.24
  765.4 0.8 copy.23
  (38 shorter events, 0.6 us)
Async XLA Ops:
  7.2 326.0 %copy-start = (bf16[320,16]{0,1:T(8,128)(2,1)S(1)}, bf16[320,16]{0,1:T(8,128)(2,1)}, u32[]{:S(2)}) copy-start(bf16[320,16]{0,1:T(8,128)(2,1)} %param.19) | copy-start | bytes 30724
  7.2 81.1 %all-gather.8.cloned.1.call-start = ((), (), s32[]{:S(2)}) async-start(), calls=%async_computation.3 | async-start | bytes 2027520 | tf_op jit(solution)/shard_map/all_gather | solution.py:42
  7.9 122.9 %all-gather.6.cloned.1.call-start = ((), (), s32[]{:S(2)}) async-start(), calls=%async_computation.2 | async-start | bytes 5898240 | tf_op jit(solution)/shard_map/all_gather | solution.py:37
  8.7 198.3 %all-gather.10.cloned.1.call-start = ((), (), s32[]{:S(2)}) async-start(), calls=%async_computation.4 | async-start | bytes 2027520 | tf_op jit(solution)/shard_map/all_gather | solution.py:39
  9.4 275.0 %all-gather.14.cloned.1.call-start = ((), (), s32[]{:S(2)}) async-start(), calls=%async_computation.6 | async-start | bytes 2027520 | tf_op jit(solution)/shard_map/all_gather | solution.py:62
  10.0 129.1 %copy-start.6 = (f32[4,320]{1,0:T(4,128)S(1)}, f32[4,320]{1,0:T(4,128)}, u32[]{:S(2)}) copy-start(f32[4,320]{1,0:T(4,128)} %param.14) | copy-start | bytes 15364
  10.0 129.1 %copy-start.7 = (f32[5]{0:T(128)S(1)}, f32[5]{0:T(128)}, u32[]{:S(2)}) copy-start(f32[5]{0:T(128)} %param.16) | copy-start | bytes 64
  10.0 317.3 %all-gather.12.cloned.1.call-start = ((), (), s32[]{:S(2)}) async-start(), calls=%async_computation.5 | async-start | bytes 5898240 | tf_op jit(solution)/shard_map/all_gather | solution.py:61
  135.8 71.1 %copy-start.8 = (f32[320]{0:T(512)S(1)}, f32[320]{0:T(512)}, u32[]{:S(2)}) copy-start(f32[320]{0:T(512)} %param.15) | copy-start | bytes 3844
  135.9 4.7 collective-permute-start
  206.9 22.8 %copy-start.4 = (f32[320]{0:T(512)S(1)}, f32[320]{0:T(512)}, u32[]{:S(2)}) copy-start(f32[320]{0:T(512)} %param.17) | copy-start | bytes 3844
  230.8 123.5 %copy-start.5 = (s32[1024]{0:T(1024)S(1)}, s32[1024]{0:T(1024)}, u32[]{:S(2)}) copy-start(s32[1024]{0:T(1024)} %param.10) | copy-start | bytes 12292
  230.8 173.1 %reduce-scatter.5.cloned.1.call-start = ((), (), s32[]{:S(2)}) async-start(), calls=%async_computation.7 | async-start | bytes 5898240 | tf_op jit(solution)/shard_map/reduce_scatter | solution.py:81
  332.4 0.8 copy-start.1
  355.0 0.8 copy-start.3
  362.2 197.8 %all-reduce.3.cloned.1.call-start = ((), (), s32[]{:S(2)}) async-start(), calls=%async_computation.8 | async-start | bytes 3932160 | tf_op jit(solution)/shard_map/psum | solution.py:75
  369.3 394.3 %reduce-scatter.7.cloned.1.call-start = ((), (), s32[]{:S(2)}) async-start(), calls=%async_computation.9 | async-start | bytes 3379200
  424.5 8.7 %collective-permute-start.1 = (f32[3,320]{0,1:T(8,128)S(1)}, f32[3,320]{0,1:T(8,128)S(1)}, u32[]{:S(2)}, u32[]{:S(2)}) collective-permute-start(f32[3,320]{0,1:T(8,128)S(1)} %slice.73), channel_id=1, source_target_pairs={{8,0},{16,8},{24,16},{32,24},{40,32},{48,40},{56,48},{64,56},{72,6... | collective-permute-start | bytes 11528 | tf_op jit(solution)/shard_map/ppermute | solution.py:15
  445.2 1.1 copy-start.2
Sparse Core Ops, SparseCore 0:
  10.6 77.6 all-gather.7
  90.2 40.5 all-gather.5
  133.4 73.5 all-gather.9
  209.4 74.9 all-gather.13
  286.7 40.5 all-gather.11
  362.3 41.5 reduce-scatter.4
  407.4 152.5 all-reduce.2
  563.8 199.6 reduce-scatter.6
where the time goes:
time: 777 us; the launch traced here: 773 us
  waiting for transfers between devices  531 us (68%)
  blocking collectives  165 us (21%)
  matrix products  38.3 us (5%)
  between operations  14.3 us (2%)
  other arithmetic  10.6 us (1%)
  local copies, waits for them, and re-layouts  9.19 us (1%)
    psum x1, waiting for transfers between devices, per_device(): lax.psum(inner_rows(full_normed, dresid).astype(jnp.bfloat16), 'seq')  113 us
    psum x1, blocking collectives, per_device(): lax.psum((head_local, taps_local, bias_local, skip_local, gain_local), 's...  113 us
    unnamed x9, waiting for transfers between devices  91.8 us
    all_gather x1, waiting for transfers between devices, per_device(): lax.all_gather(w_x_in, 'seq', axis=0, tiled=True)  78.3 us
    all_gather x1, waiting for transfers between devices, per_device(): lax.all_gather(w_gate_in, 'seq', axis=0, tiled=True)  66.1 us
    all_gather x1, waiting for transfers between devices, per_device(): out_cols = lax.all_gather(w_out, 'seq', axis=0, tiled=True)  53.6 us
    all_gather x1, waiting for transfers between devices, per_device(): full_normed = lax.all_gather(normed, 'chan', axis=1, tiled=True)  42.9 us
    all_gather x1, waiting for transfers between devices, per_device(): features = lax.all_gather(resid, 'chan', axis=1, tiled=True)  42.4 us
  transfers between devices with their start and end apart: 10, of which 10 were waited for; matrix products, arithmetic and copies ran while one was open for 5% of the time, Pallas kernels for 0%

commit v1 on v0

v1 whole, which is shorter than its diff:
```python
import jax
import jax.numpy as jnp
from jax import lax
from jax.sharding import PartitionSpec as P

HEADDIM = 64
KERNEL = 4
VOCAB = 16
INNER = 2560


def shifted(array, axis, by):
    length = lax.axis_size(axis)
    pairs = [(i, i + by) for i in range(length) if 0 <= i + by < length]
    return lax.ppermute(array, axis, pairs)


def slope(value, sig):
    return sig * (1.0 + value * (1.0 - sig))


def inner_rows(left, right, precision=None):
    return lax.dot_general(
        left,
        right,
        (((0,), (0,)), ((), ())),
        preferred_element_type=jnp.float32,
        precision=precision,
    )


def per_device(
    targets, resid, w_gate_in, w_x_in, conv_weight, conv_bias, skip_d, norm_gain, w_out, w_head
):
    f32 = jnp.float32
    bf16 = jnp.bfloat16
    exact = lax.Precision.HIGHEST
    tok_rows = resid.shape[0]
    seq_count = lax.axis_size("seq")
    local_inner = w_gate_in.shape[1]
    row_count = w_out.shape[0]
    halo_rows = KERNEL - 1
    mix_part = jnp.dot(w_out, w_head, preferred_element_type=f32)
    mix_rows = lax.psum(mix_part, "chan")
    mix_all = lax.all_gather(mix_rows, "seq", axis=0, tiled=True)
    mix = lax.dynamic_slice_in_dim(
        mix_all, lax.axis_index("chan") * local_inner, local_inner, 0
    )
    features = lax.all_gather(resid, "chan", axis=1, tiled=True)
    w_both = lax.all_gather(
        jnp.concatenate([w_gate_in, w_x_in], axis=1), "seq", axis=0, tiled=True
    )
    both_sum = jnp.dot(features, w_both, preferred_element_type=f32)
    gate_pre = both_sum[:, :local_inner].astype(bf16)
    x_pre = both_sum[:, local_inner:].astype(bf16)
    before = shifted(x_pre[tok_rows - halo_rows :], "seq", 1)
    padded = jnp.concatenate([before, x_pre], axis=0).astype(f32)
    conv_out = jnp.zeros((tok_rows, local_inner), f32) + conv_bias
    for offset in range(KERNEL):
        conv_out = conv_out + conv_weight[offset] * padded[offset : offset + tok_rows]
    sig_conv = jax.nn.sigmoid(conv_out)
    active = conv_out * sig_conv
    gate_f32 = gate_pre.astype(f32)
    sig_gate = jax.nn.sigmoid(gate_f32)
    silu_gate = gate_f32 * sig_gate
    head_scale = jnp.repeat(skip_d, HEADDIM)
    gated = active * head_scale * silu_gate
    gained = gated * norm_gain
    sq_part = jnp.sum(gated * gated, axis=1, keepdims=True)
    head_part = jnp.dot(resid, w_head, preferred_element_type=f32)
    gained_part = jnp.dot(gained, mix, precision=exact)
    stats = lax.psum(jnp.concatenate([head_part, gained_part, sq_part], axis=1), "chan")
    inverse = lax.rsqrt(stats[:, 2 * VOCAB :] / INNER + 1e-05)
    gained_head = stats[:, VOCAB : 2 * VOCAB]
    logits = stats[:, :VOCAB] + inverse * gained_head
    raised = jnp.exp(logits)
    probs = raised / jnp.sum(raised, axis=1, keepdims=True)
    onehot = (targets[:, None] == jnp.arange(VOCAB, dtype=jnp.int32)[None, :]).astype(f32)
    loss_weight = 4.0 / jnp.sqrt(jnp.asarray(tok_rows * seq_count, f32))
    dlogit = (probs - onehot) * loss_weight
    dnormed = jnp.dot(dlogit, mix.T, precision=exact)
    dot_gn = jnp.sum(dlogit * gained_head, axis=1, keepdims=True)
    dgated = inverse * norm_gain * dnormed - gated * (inverse**3 * dot_gn / INNER)
    gain_local = jnp.sum(dnormed * gated * inverse, axis=0)
    skip_local = jnp.sum(dgated * active * silu_gate, axis=0).reshape(-1, HEADDIM).sum(axis=1)
    dgate = (dgated * active * head_scale * slope(gate_f32, sig_gate)).astype(bf16)
    dconv = dgated * head_scale * silu_gate * slope(conv_out, sig_conv)
    bias_local = jnp.sum(dconv, axis=0)
    taps_local = jnp.stack(
        [jnp.sum(dconv * padded[offset : offset + tok_rows], axis=0) for offset in range(KERNEL)]
    )
    future = shifted(dconv[:halo_rows], "seq", -1)
    dpadded = jnp.concatenate([dconv, future], axis=0)
    dx_sum = jnp.zeros((tok_rows, local_inner), f32)
    for offset in range(KERNEL):
        dx_sum = (
            dx_sum
            + conv_weight[offset] * dpadded[halo_rows - offset : halo_rows - offset + tok_rows]
        )
    dx_pre = dx_sum.astype(bf16)
    normed = (gained * inverse).astype(bf16)
    full_normed = lax.all_gather(normed, "chan", axis=1, tiled=True)
    out_cols = lax.all_gather(w_out, "seq", axis=0, tiled=True)
    new_resid = (
        resid.astype(f32) + jnp.dot(full_normed, out_cols, preferred_element_type=f32)
    ).astype(bf16)
    head_local = inner_rows(new_resid.astype(f32), dlogit, exact)
    normed_local = inner_rows(gained * inverse, dlogit, exact)
    both_grads = jnp.concatenate([dgate, dx_pre], axis=1)
    grad_both = lax.psum_scatter(
        inner_rows(features, both_grads).astype(bf16), "seq", scatter_dimension=0, tiled=True
    ).astype(f32)
    grad_gate_in = grad_both[:, :local_inner]
    grad_x_in = grad_both[:, local_inner:]
    grad_head, grad_mix, grad_conv_weight, grad_conv_bias, grad_skip, grad_gain = lax.psum(
        (head_local, normed_local, taps_local, bias_local, skip_local, gain_local), "seq"
    )
    mix_grads = lax.all_gather(grad_mix, "chan", axis=0, tiled=True)
    mix_grad_rows = lax.dynamic_slice_in_dim(
        mix_grads, lax.axis_index("seq") * row_count, row_count, 0
    )
    grad_out = jnp.dot(mix_grad_rows, w_head.astype(f32).T, precision=exact)
    return (
        new_resid,
        grad_gate_in,
        grad_x_in,
        grad_out,
        grad_head,
        grad_conv_weight,
        grad_conv_bias,
        grad_skip,
        grad_gain,
    )


def solution(mesh):
    return jax.shard_map(
        per_device,
        mesh=mesh,
        in_specs=(
            P("seq"),
            P("seq", "chan"),
            P("seq", "chan"),
            P("seq", "chan"),
            P(None, "chan"),
            P("chan"),
            P("chan"),
            P("chan"),
            P("seq", "chan"),
            P("chan", None),
        ),
        out_specs=(
            P("seq", "chan"),
            P("seq", "chan"),
            P("seq", "chan"),
            P("seq", "chan"),
            P("chan", None),
            P(None, "chan"),
            P("chan"),
            P("chan"),
            P("chan"),
        ),
        check_vma=False,
    )
```

time: 777 us -> 780 us (level)
  blocking collectives: 165 us -> 209 us
  waiting for transfers between devices: 531 us -> 501 us
  matrix products: 38.3 us -> 24.5 us
    unnamed x9 -> x7, waiting for transfers between devices: 91.8 us -> 199 us
    all_gather x2 -> x1, waiting for transfers between devices: 144 us -> 63.3 us  [per_device(): lax.all_gather(jnp.concatenate([w_gate_in, w_x_in], axis=1), 'seq', axis=...]
    all_gather x0 -> x2, blocking collectives: none -> 77.6 us  [the longest x1 40.3 us: per_device(): mix_grads = lax.all_gather(grad_mix, 'chan', axis=0, tiled=True)]
    psum x1, waiting for transfers between devices: 113 us -> 72.8 us  [per_device(): lax.psum(jnp.concatenate([head_part, gained_part, sq_part], axis=1), 'chan')]
    reduce_scatter x1 -> x0, waiting for transfers between devices: 34.6 us -> none  [per_device(): lax.psum_scatter(norm_term.astype(jnp.bfloat16), 'chan', scatter_dimensio...]
    psum x4 -> x2, blocking collectives: 165 us -> 131 us  [the longest x1 116 us: per_device(): lax.psum((head_local, normed_local, taps_local, bias_local, skip_local, g...]
    all_gather x1, waiting for transfers between devices: 53.6 us -> 76.3 us  [per_device(): out_cols = lax.all_gather(w_out, 'seq', axis=0, tiled=True)]
  transfers between devices with their start and end apart: 10 -> 8, of which waited for: 10 -> 7; matrix products, arithmetic and copies ran while one was open for 5% -> 1% of each run, Pallas kernels for 0% -> 0%
where the time goes in v1:
time: 780 us
  waiting for transfers between devices  501 us (64%)
  blocking collectives  209 us (27%)
  matrix products  24.5 us (3%)
  other arithmetic  14.9 us (2%)
  between operations  14.4 us (2%)
  local copies, waits for them, and re-layouts  11 us (1%)
    unnamed x7, waiting for transfers between devices  199 us
    psum x1, blocking collectives, per_device(): lax.psum((head_local, normed_local, taps_local, bias_local, skip_local, g...  116 us
    all_gather x1, waiting for transfers between devices, per_device(): out_cols = lax.all_gather(w_out, 'seq', axis=0, tiled=True)  76.3 us
    psum x1, waiting for transfers between devices, per_device(): lax.psum(jnp.concatenate([head_part, gained_part, sq_part], axis=1), 'chan')  72.8 us
    all_gather x1, waiting for transfers between devices, per_device(): lax.all_gather(jnp.concatenate([w_gate_in, w_x_in], axis=1), 'seq', axis=...  63.3 us
    all_gather x1, waiting for transfers between devices, per_device(): full_normed = lax.all_gather(normed, 'chan', axis=1, tiled=True)  42.9 us
    all_gather x1, waiting for transfers between devices, per_device(): features = lax.all_gather(resid, 'chan', axis=1, tiled=True)  41.9 us
    all_gather x1, blocking collectives, per_device(): mix_grads = lax.all_gather(grad_mix, 'chan', axis=0, tiled=True)  40.3 us
  transfers between devices with their start and end apart: 8, of which 7 were waited for; matrix products, arithmetic and copies ran while one was open for 1% of the time, Pallas kernels for 0%

profile of v1, /device:TPU:1, one launch (start us, length us, event | category | flops | bytes accessed | tf_op | source)
XLA Modules:
  0.0 779.6 jit_solution(5755632246923646050)
XLA Ops:
  7.2 1.6 pad_maximum_fusion.2
  8.9 0.7 all-gather.9.cloned.1.call-update
  9.7 1.0 fusion.47
  10.6 15.2 %psum.56 = f32[80,16]{0,1:T(8,128)S(1)} all-reduce(f32[80,16]{0,1:T(8,128)S(1)} %fusion.47), channel_id=1, replica_groups=mesh['seq'=32,'chan'=8] {'chan'}, use_global_device_ids=true, to_apply=%region_0.0 | all-reduce | flops 1280 | bytes 10240 | tf_op jit(solution)/shard_map/psum | solution.py:44
  25.9 0.9 slice_reduce_fusion.3
  26.7 1.3 fusion.49
  28.0 63.3 %all-gather.7.cloned.1.call-done = bf16[2560,640]{1,0:T(8,128)(2,1)} async-done(((bf16[80,640]{1,0:T(8,128)(2,1)}), bf16[2560,640]{1,0:T(8,128)(2,1)}) %all-gather.7.cloned.1.call-update) | async-done | bytes 3276816 | tf_op jit(solution)/shard_map/all_gather | solution.py:50
  91.3 41.9 %all-gather.9.cloned.1.call-done = bf16[1024,2560]{0,1:T(8,128)(2,1)} async-done(((bf16[1024,320]{0,1:T(8,128)(2,1)}), bf16[1024,2560]{0,1:T(8,128)(2,1)}) %all-gather.9.cloned.1.call-update) | async-done | bytes 5242896 | tf_op jit(solution)/shard_map/all_gather | solution.py:49
  133.2 7.1 fusion.1
  140.3 0.1 slice.91
  140.4 3.2 collective-permute-start
  143.6 37.3 %all-gather = f32[32,80,16]{1,2,0:T(8,128)S(1)} all-gather(f32[1,80,16]{1,2,0:T(8,128)S(1)} %bitcast.33), channel_id=1, replica_groups=mesh['seq'=32,'chan'=8] {'seq'}, dimensions={0}, use_global_device_ids=true | all-gather | bytes 168960 | tf_op jit(solution)/shard_map/all_gather | solution.py:45
  181.0 0.1 copy.29
  181.1 0.2 reshape.28
  181.4 0.3 maximum_convert_fusion
  181.7 0.4 copy-done.8
  182.1 0.7 copy-done.3
  182.7 2.4 multiply_reduce_fusion.6
  185.1 0.9 fusion.26
  186.0 0.7 pad_maximum_fusion.1
  186.8 72.8 %all-reduce.3.cloned.1.call-done = f32[1024,33]{0,1:T(8,128)} async-done(((f32[1024,33]{0,1:T(8,128)}), f32[1024,33]{0,1:T(8,128)}) %all-reduce.3.cloned.1.call-update) | async-done | bytes 135184 | tf_op jit(solution)/shard_map/psum | solution.py:72
  259.6 0.9 fusion.40
  260.5 0.9 fusion.35
  261.4 0.9 multiply_reduce_fusion.7
  262.3 1.3 fusion.32
  263.7 0.8 fusion.41
  264.5 4.8 multiply_reduce_fusion
  269.3 1.5 collective-permute-start.1
  270.8 4.6 collective-permute-done.1
  275.4 1.5 fusion.8
  277.0 5.1 fusion
  282.1 5.7 copy.33
  287.8 0.5 all-gather.13.cloned.1.call-update
  288.4 0.5 all-gather.11.cloned.1.call-update
  289.0 0.1 reduce_sum.108
  289.2 1.2 fusion.23
  290.4 197.6 %reduce-scatter.4.cloned.1.call-done = bf16[80,640]{1,0:T(8,128)(2,1)} async-done(((bf16[2560,640]{1,0:T(8,128)(2,1)}), bf16[80,640]{1,0:T(8,128)(2,1)}) %reduce-scatter.4.cloned.1.call-update) | async-done | bytes 102416
  488.0 1.1 copy.34
  489.1 0.8 copy.31
  489.9 0.8 copy.32
  490.7 76.3 %all-gather.13.cloned.1.call-done = bf16[2560,320]{1,0:T(8,128)(2,1)} async-done(((bf16[80,320]{1,0:T(8,128)(2,1)}), bf16[2560,320]{1,0:T(8,128)(2,1)}) %all-gather.13.cloned.1.call-update) | async-done | bytes 1638416 | tf_op jit(solution)/shard_map/all_gather | solution.py:103
  567.0 42.9 %all-gather.11.cloned.1.call-done = bf16[1024,2560]{0,1:T(8,128)(2,1)} async-done(((bf16[1024,320]{0,1:T(8,128)(2,1)}), bf16[1024,2560]{0,1:T(8,128)(2,1)}) %all-gather.11.cloned.1.call-update) | async-done | bytes 5242896 | tf_op jit(solution)/shard_map/all_gather | solution.py:102
  609.8 5.0 fusion.2
  614.9 0.6 fusion.48
  615.5 115.9 %all-reduce = (f32[320,16]{0,1:T(8,128)S(1)}, f32[320,16]{0,1:T(8,128)}, f32[4,320]{1,0:T(4,128)}, f32[320]{0:T(512)}, f32[5]{0:T(128)}, /*index=5*/f32[320]{0:T(512)}) all-reduce(f32[320,16]{0,1:T(8,128)S(1)} %fusion.23, f32[320,16]{0,1:T(8,128)S(1)} %fusion.48, ...), channel_id=1, replica_groups=mesh['seq'=32,'chan'=8] {'seq'}, use_global_device_ids=true, to_apply=%region_6.0 | all-reduce | flops 12165 | bytes 97320 | tf_op jit(solution)/shard_map/psum | solution.py:115
  731.4 40.3 %all-gather.1 = f32[8,320,16]{1,2,0:T(8,128)S(1)} all-gather(f32[1,320,16]{1,2,0:T(8,128)S(1)} %bitcast.34), channel_id=1, replica_groups=mesh['seq'=32,'chan'=8] {'chan'}, dimensions={0}, use_global_device_ids=true | all-gather | bytes 184320 | tf_op jit(solution)/shard_map/all_gather | solution.py:118
  771.7 0.1 reshape.30
  771.8 1.0 fusion.36
  (45 shorter events, 0.8 us)
Async XLA Ops:
  7.2 2.5 copy-start
  7.2 84.1 %all-gather.7.cloned.1.call-start = ((), (), s32[]{:S(2)}) async-start(), calls=%async_computation.1 | async-start | bytes 3379200 | tf_op jit(solution)/shard_map/all_gather | solution.py:50
  8.9 124.4 %all-gather.9.cloned.1.call-start = ((), (), s32[]{:S(2)}) async-start(), calls=%async_computation.2 | async-start | bytes 5898240 | tf_op jit(solution)/shard_map/all_gather | solution.py:49
  9.6 250.0 %all-reduce.3.cloned.1.call-start = ((), (), s32[]{:S(2)}) async-start(), calls=%async_computation.3 | async-start | bytes 327680 | tf_op jit(solution)/shard_map/psum | solution.py:72
  28.0 152.9 %copy-start.9 = (f32[5]{0:T(128)S(1)}, f32[5]{0:T(128)}, u32[]{:S(2)}) copy-start(f32[5]{0:T(128)} %param.16) | copy-start | bytes 64
  140.3 41.1 %copy-start.2 = (bf16[1024,640]{0,1:T(8,128)(2,1)}, bf16[1024,640]{0,1:T(8,128)(2,1)S(1)}, u32[]{:S(2)}) copy-start(bf16[1024,640]{0,1:T(8,128)(2,1)S(1)} %fusion.1) | copy-start | bytes 3932164
  140.4 41.0 %collective-permute-start = (bf16[3,320]{0,1:T(8,128)(2,1)S(1)}, bf16[3,320]{0,1:T(8,128)(2,1)S(1)}, u32[]{:S(2)}, u32[]{:S(2)}) collective-permute-start(bf16[3,320]{0,1:T(8,128)(2,1)S(1)} %slice.91), channel_id=1, source_target_pairs={{0,8},{8,16},{16,24},{24,32},{32,40},{40,48},{48,56},{56,64},{64,7... | collective-permute-start | bytes 5768 | tf_op jit(solution)/shard_map/ppermute | solution.py:15
  181.4 0.7 copy-start.8
  181.4 1.3 copy-start.3
  182.7 2.4 copy-start.6
  185.1 76.3 %copy-start.7 = (s32[1024]{0:T(1024)S(1)}, s32[1024]{0:T(1024)}, u32[]{:S(2)}) copy-start(s32[1024]{0:T(1024)} %param.10) | copy-start | bytes 12292
  186.8 301.3 %reduce-scatter.4.cloned.1.call-start = ((), (), s32[]{:S(2)}) async-start(), calls=%async_computation.6 | async-start | bytes 3379200
  259.6 4.8 copy-start.1
  264.4 12.5 %slice-start = ((s8[5242880]{0:T(1024)(128)(4,1)}), s8[4194304]{0:T(1024)(128)(4,1)S(1)}, s32[]{:S(2)}) async-start(s8[5242880]{0:T(1024)(128)(4,1)} %bitcast.38), calls=%async_computation.7 | async-start | bytes 8388608
  264.5 12.5 %slice-start.1 = ((s8[5242880]{0:T(1024)(128)(4,1)}), s8[1048576]{0:T(1024)(128)(4,1)S(1)}, s32[]{:S(2)}) async-start(s8[5242880]{0:T(1024)(128)(4,1)} %bitcast.38), calls=%async_computation.8 | async-start | bytes 2097152
  269.3 6.1 collective-permute-start.1
  287.7 279.2 %all-gather.13.cloned.1.call-start = ((), (), s32[]{:S(2)}) async-start(), calls=%async_computation.5 | async-start | bytes 2027520 | tf_op jit(solution)/shard_map/all_gather | solution.py:103
  288.3 321.5 %all-gather.11.cloned.1.call-start = ((), (), s32[]{:S(2)}) async-start(), calls=%async_computation.4 | async-start | bytes 5898240 | tf_op jit(solution)/shard_map/all_gather | solution.py:102
  289.2 320.7 %copy-start.4 = (bf16[1024,320]{0,1:T(8,128)(2,1)S(1)}, bf16[1024,320]{0,1:T(8,128)(2,1)}, u32[]{:S(2)}) copy-start(bf16[1024,320]{0,1:T(8,128)(2,1)} %param.11) | copy-start | bytes 1966084
  614.9 157.9 %copy-start.5 = (bf16[1024,320]{0,1:T(8,128)(2,1)}, bf16[1024,320]{0,1:T(8,128)(2,1)S(1)}, u32[]{:S(2)}) copy-start(bf16[1024,320]{0,1:T(8,128)(2,1)S(1)} %fusion.2) | copy-start | bytes 1966084
Sparse Core Ops, SparseCore 0:
  11.2 80.0 all-gather.6
  93.2 40.0 all-gather.8
  186.9 72.7 all-reduce.2
  287.9 200.1 reduce-scatter.3
  490.5 76.4 all-gather.12
  569.2 40.5 all-gather.10

commit v2 on v1

v2 whole, which is shorter than its diff:
```python
import functools

import jax
import jax.numpy as jnp
from jax import lax
from jax.experimental import pallas as pl
from jax.experimental.pallas import tpu as pltpu
from jax.sharding import PartitionSpec as P

HEADDIM = 64
KERNEL = 4
VOCAB = 16
INNER = 2560
NX, NY, NZ = 4, 4, 8
NCHAN = 2 * NX
MESH = pl.DeviceIdType.MESH
VMEM_BYTES = 56 * 1024 * 1024


class Wire:
    def __init__(self, send, recv):
        self.send, self.recv, self.copies = send, recv, []

    def put(self, source, target, **where):
        place = len(self.copies)
        copy = pltpu.make_async_remote_copy(
            src_ref=source,
            dst_ref=target,
            send_sem=self.send.at[place],
            recv_sem=self.recv.at[place],
            device_id=where,
            device_id_type=MESH,
        )
        copy.start()
        self.copies.append(copy)
        return copy

    def finish(self):
        for copy in self.copies:
            copy.wait_send()


def greet(peers):
    barrier = pltpu.get_barrier_semaphore()
    for peer in peers:
        pl.semaphore_signal(barrier, inc=1, device_id=peer, device_id_type=MESH)
    pl.semaphore_wait(barrier, len(peers))


def take_turns(*streams):
    streams = list(streams)
    while streams:
        for stream in list(streams):
            try:
                next(stream)
            except StopIteration:
                streams.remove(stream)


def place():
    s, c = lax.axis_index("seq"), lax.axis_index("chan")
    return s // NZ, s % NZ, c


def gather_chan(wire, shard, full, c, rows):
    x, core = c // 2, c % 2
    mate = c + 1 - 2 * core
    right = lax.rem(x + 1, NX) * 2 + core
    left = lax.rem(x + NX - 1, NX) * 2 + core
    across = lax.rem(x + 2, NX) * 2 + core
    lo, hi = pl.ds(0, rows // 2), pl.ds(rows // 2, rows // 2)
    to_right_lo = wire.put(shard.at[lo], full.at[c, lo], chan=right)
    to_left_hi = wire.put(shard.at[hi], full.at[c, hi], chan=left)
    to_right_hi = wire.put(shard.at[hi], full.at[c, hi], chan=right)
    to_left_lo = wire.put(shard.at[lo], full.at[c, lo], chan=left)
    to_mate = [wire.put(shard, full.at[c], chan=mate)]
    yield
    to_right_lo.wait_recv()
    on_right = wire.put(full.at[left, lo], full.at[left, lo], chan=right)
    to_left_hi.wait_recv()
    on_left = wire.put(full.at[right, hi], full.at[right, hi], chan=left)
    yield
    to_right_hi.wait_recv()
    to_mate.append(wire.put(full.at[left], full.at[left], chan=mate))
    to_left_lo.wait_recv()
    to_mate.append(wire.put(full.at[right], full.at[right], chan=mate))
    yield
    on_right.wait_recv()
    to_mate.append(wire.put(full.at[across, lo], full.at[across, lo], chan=mate))
    on_left.wait_recv()
    to_mate.append(wire.put(full.at[across, hi], full.at[across, hi], chan=mate))
    yield
    for copy in to_mate:
        copy.wait_recv()


def ring_z(wire, first, block, halves, y, z):
    up, down = y * NZ + lax.rem(z + 1, NZ), y * NZ + lax.rem(z + NZ - 1, NZ)
    plus = wire.put(first, block(z), seq=up)
    minus = wire.put(first, block(z), seq=down)
    for step in range(1, NZ // 2):
        last = step == NZ // 2 - 1
        yield
        behind, ahead = lax.rem(z + NZ - step, NZ), lax.rem(z + step, NZ)
        plus.wait_recv()
        moved = halves(behind)[0] if last else block(behind)
        plus = wire.put(moved, moved, seq=up)
        minus.wait_recv()
        moved = halves(ahead)[1] if last else block(ahead)
        minus = wire.put(moved, moved, seq=down)
    yield
    plus.wait_recv()
    minus.wait_recv()


def gather_y_first(wire, shard, full, own, y, z, rows):
    puts = [
        wire.put(shard.at[rows], full.at[y, z, rows], seq=lax.rem(y + d, NY) * NZ + z)
        for d in (1, 3, 2)
    ]
    yield
    own.wait()
    for copy in puts:
        copy.wait_recv()
    yield from ring_z(
        wire,
        full.at[:, z, rows],
        lambda at: full.at[:, at, rows],
        lambda at: (full.at[pl.ds(0, 2), at, rows], full.at[pl.ds(2, 2), at, rows]),
        y,
        z,
    )


def gather_z_first(wire, shard, full, y, z, start, count):
    rows = pl.ds(start, count)
    cut = (count // 32) * 16
    yield from ring_z(
        wire,
        shard.at[rows],
        lambda at: full.at[y, at, rows],
        lambda at: (
            full.at[y, at, pl.ds(start, cut)],
            full.at[y, at, pl.ds(start + cut, count - cut)],
        ),
        y,
        z,
    )
    above, below = lax.rem(y + 1, NY), lax.rem(y + NY - 1, NY)
    up, down = above * NZ + z, below * NZ + z
    lo, hi = pl.ds(0, NZ // 2), pl.ds(NZ // 2, NZ // 2)
    up_lo = wire.put(full.at[y, lo, rows], full.at[y, lo, rows], seq=up)
    down_hi = wire.put(full.at[y, hi, rows], full.at[y, hi, rows], seq=down)
    up_hi = wire.put(full.at[y, hi, rows], full.at[y, hi, rows], seq=up)
    down_lo = wire.put(full.at[y, lo, rows], full.at[y, lo, rows], seq=down)
    yield
    up_lo.wait_recv()
    on_up = wire.put(full.at[below, lo, rows], full.at[below, lo, rows], seq=up)
    down_hi.wait_recv()
    on_down = wire.put(full.at[above, hi, rows], full.at[above, hi, rows], seq=down)
    yield
    for copy in (up_hi, down_lo, on_up, on_down):
        copy.wait_recv()


def gather_kernel(resid, weights, full_resid, full_weights, send, recv, local):
    y, z, c = place()
    x, core = c // 2, c % 2
    greet(
        [{"chan": c + 1 - 2 * core}]
        + [{"chan": lax.rem(x + d, NX) * 2 + core} for d in (1, NX - 1)]
        + [{"seq": lax.rem(y + d, NY) * NZ + z} for d in range(1, NY)]
        + [{"seq": y * NZ + lax.rem(z + d, NZ)} for d in (1, NZ - 1)]
    )
    wire = Wire(send, recv)
    own_weights = pltpu.make_async_copy(weights, full_weights.at[y, z], local.at[0])
    own_resid = pltpu.make_async_copy(resid, full_resid.at[c], local.at[1])
    own_weights.start()
    own_resid.start()
    rows = weights.shape[0]
    take_turns(
        gather_y_first(wire, weights, full_weights, own_weights, y, z, pl.ds(0, 32)),
        gather_z_first(wire, weights, full_weights, y, z, 32, rows - 32),
        gather_chan(wire, resid, full_resid, c, resid.shape[0]),
    )
    own_resid.wait()
    wire.finish()


def gather_all(resid, weights):
    anywhere = pl.BlockSpec(memory_space=pl.ANY)
    copies = 48
    return pl.pallas_call(
        gather_kernel,
        name="gather_all",
        out_shape=(
            jax.ShapeDtypeStruct((NCHAN, *resid.shape), resid.dtype),
            jax.ShapeDtypeStruct((NY, NZ, *weights.shape), weights.dtype),
        ),
        in_specs=[anywhere] * 2,
        out_specs=(anywhere,) * 2,
        scratch_shapes=[
            pltpu.SemaphoreType.DMA((copies,)),
            pltpu.SemaphoreType.DMA((copies,)),
            pltpu.SemaphoreType.DMA((2,)),
        ],
        compiler_params=pltpu.CompilerParams(collective_id=0, has_side_effects=True),
    )(resid, weights)


def stats_kernel(stats, out, parts, total, send, recv):
    c = lax.axis_index("chan")
    greet([{"chan": lax.rem(c + d, NCHAN)} for d in range(1, NCHAN)])
    wire = Wire(send, recv)
    width = total.shape[1]

    def lanes(chan):
        return pl.ds(pl.multiple_of(chan * width, width), width)

    puts = []
    for d in range(1, NCHAN):
        peer = lax.rem(c + d, NCHAN)
        puts.append(wire.put(stats.at[:, lanes(peer)], parts.at[d - 1], chan=peer))
    acc = stats[:, lanes(c)]
    for d in range(1, NCHAN):
        puts[d - 1].wait_recv()
        acc = acc + parts[d - 1]
    total[...] = acc
    out[:, lanes(c)] = acc
    puts = []
    for d in range(1, NCHAN):
        puts.append(wire.put(total, out.at[:, lanes(c)], chan=lax.rem(c + d, NCHAN)))
    for copy in puts:
        copy.wait_recv()
    wire.finish()


def sum_stats(stats):
    rows, tokens = stats.shape
    vmem = pl.BlockSpec(memory_space=pltpu.VMEM)
    copies = 2 * (NCHAN - 1)
    return pl.pallas_call(
        stats_kernel,
        name="sum_stats",
        out_shape=jax.ShapeDtypeStruct(stats.shape, stats.dtype),
        in_specs=[vmem],
        out_specs=vmem,
        scratch_shapes=[
            pltpu.VMEM((NCHAN - 1, rows, tokens // NCHAN), stats.dtype),
            pltpu.VMEM((rows, tokens // NCHAN), stats.dtype),
            pltpu.SemaphoreType.DMA((copies,)),
            pltpu.SemaphoreType.DMA((copies,)),
        ],
        compiler_params=pltpu.CompilerParams(collective_id=1, has_side_effects=True),
    )(stats)


def scatter_seq(wire, grads, bufs, out, y, z, start, count):
    f32, bf16 = jnp.float32, jnp.bfloat16
    from_below, from_above, via_up, via_down, got_below, got_above, lines, got_z = bufs
    rows = pl.ds(start, count)
    lo, hi = pl.ds(0, NZ // 2), pl.ds(NZ // 2, NZ // 2)
    above, below, across = lax.rem(y + 1, NY), lax.rem(y + 3, NY), lax.rem(y + 2, NY)
    up, down = above * NZ + z, below * NZ + z
    half_up = wire.put(grads.at[across, lo, rows], from_below.at[:, rows], seq=up)
    half_down = wire.put(grads.at[across, hi, rows], from_above.at[:, rows], seq=down)
    moves = [
        wire.put(grads.at[above, hi, rows], got_below.at[hi, rows], seq=up),
        wire.put(grads.at[below, lo, rows], got_above.at[lo, rows], seq=down),
    ]
    yield
    half_up.wait_recv()
    via_up[:, rows] = (
        grads[above, lo, rows].astype(f32) + from_below[:, rows].astype(f32)
    ).astype(bf16)
    moves.append(wire.put(via_up.at[:, rows], got_below.at[lo, rows], seq=up))
    half_down.wait_recv()
    via_down[:, rows] = (
        grads[below, hi, rows].astype(f32) + from_above[:, rows].astype(f32)
    ).astype(bf16)
    moves.append(wire.put(via_down.at[:, rows], got_above.at[hi, rows], seq=down))
    yield
    for copy in moves:
        copy.wait_recv()
    lines[:, rows] = (
        grads[y, :, rows].astype(f32)
        + got_below[:, rows].astype(f32)
        + got_above[:, rows].astype(f32)
    ).astype(bf16)
    puts = []
    for d in range(1, NZ):
        peer = lax.rem(z + d, NZ)
        puts.append(wire.put(lines.at[peer, rows], got_z.at[d - 1, rows], seq=y * NZ + peer))
    yield
    acc = (
        grads[y, z, rows].astype(f32)
        + got_below[z, rows].astype(f32)
        + got_above[z, rows].astype(f32)
    )
    for d in range(1, NZ):
        puts[d - 1].wait_recv()
        acc = acc + got_z[d - 1, rows].astype(f32)
    out[rows] = acc


def sum_small(wire, small, got_y, part, got_z, total, heads, y, z, c):
    puts = [
        wire.put(small, got_y.at[y], seq=lax.rem(y + d, NY) * NZ + z) for d in range(1, NY)
    ]
    got_y[y] = small[...]
    yield
    for copy in puts:
        copy.wait_recv()
    acc = got_y[0]
    for at in range(1, NY):
        acc = acc + got_y[at]
    part[...] = acc
    puts = [
        wire.put(part, got_z.at[z], seq=y * NZ + lax.rem(z + d, NZ)) for d in range(1, NZ)
    ]
    got_z[z] = acc
    yield
    for copy in puts:
        copy.wait_recv()
    acc = got_z[0]
    for at in range(1, NZ):
        acc = acc + got_z[at]
    total[...] = acc
    first = pl.ds(0, VOCAB)
    puts = [
        wire.put(total.at[first], heads.at[c], chan=lax.rem(c + d, NCHAN))
        for d in range(1, NCHAN)
    ]
    heads[c] = total[first]
    yield
    for copy in puts:
        copy.wait_recv()


def grads_kernel(
    grads, small, gained, out, total, heads, full_gained, *scratch
):
    *bufs, small_y, small_part, small_z, send, recv, local = scratch
    y, z, c = place()
    greet(
        [{"chan": lax.rem(c + d, NCHAN)} for d in range(1, NCHAN)]
        + [{"seq": lax.rem(y + d, NY) * NZ + z} for d in range(1, NY)]
        + [{"seq": y * NZ + lax.rem(z + d, NZ)} for d in range(1, NZ)]
    )
    wire = Wire(send, recv)
    own = pltpu.make_async_copy(gained, full_gained.at[c], local.at[0])
    own.start()
    rows = out.shape[0]
    take_turns(
        sum_small(wire, small, small_y, small_part, small_z, total, heads, y, z, c),
        scatter_seq(wire, grads, bufs, out, y, z, 0, 48),
        scatter_seq(wire, grads, bufs, out, y, z, 48, rows - 48),
        gather_chan(wire, gained, full_gained, c, gained.shape[0]),
    )
    own.wait()
    wire.finish()


def finish_grads(grads, small, gained):
    f32, bf16 = jnp.float32, jnp.bfloat16
    anywhere = pl.BlockSpec(memory_space=pl.ANY)
    vmem = pl.BlockSpec(memory_space=pltpu.VMEM)
    _, _, rows, cols = grads.shape
    copies = 64
    half = (NZ // 2, rows, cols)
    line = (NZ, rows, cols)
    return pl.pallas_call(
        grads_kernel,
        name="finish_grads",
        out_shape=(
            jax.ShapeDtypeStruct((rows, cols), f32),
            jax.ShapeDtypeStruct(small.shape, f32),
            jax.ShapeDtypeStruct((NCHAN, VOCAB, small.shape[1]), f32),
            jax.ShapeDtypeStruct((NCHAN, *gained.shape), bf16),
        ),
        in_specs=[vmem, vmem, anywhere],
        out_specs=(vmem, vmem, vmem, anywhere),
        scratch_shapes=[pltpu.VMEM(half, bf16)] * 4
        + [pltpu.VMEM(line, bf16)] * 3
        + [
            pltpu.VMEM((NZ - 1, rows, cols), bf16),
            pltpu.VMEM((NY, *small.shape), f32),
            pltpu.VMEM(small.shape, f32),
            pltpu.VMEM((NZ, *small.shape), f32),
            pltpu.SemaphoreType.DMA((copies,)),
            pltpu.SemaphoreType.DMA((copies,)),
            pltpu.SemaphoreType.DMA((1,)),
        ],
        compiler_params=pltpu.CompilerParams(
            collective_id=2, has_side_effects=True, vmem_limit_bytes=VMEM_BYTES
        ),
    )(grads, small, gained)


def stacked_kernel(first, left, right, out):
    depth, width = left.shape[2], out.shape[1]
    acc = jnp.zeros(out.shape, jnp.float32)
    for at in range(left.shape[0]):
        acc = acc + jnp.dot(
            left[at],
            right[pl.ds(at * depth, depth), pl.ds(first, width)],
            preferred_element_type=jnp.float32,
        )
    out[...] = acc.astype(out.dtype)


def stacked_dot(left, right, first, width, dtype):
    parts, tokens, depth = left.shape
    tile = 256
    return pl.pallas_call(
        functools.partial(stacked_kernel, first),
        name="stacked_dot",
        grid=(tokens // tile,),
        out_shape=jax.ShapeDtypeStruct((tokens, width), dtype),
        in_specs=[
            pl.BlockSpec((parts, tile, depth), lambda i: (0, i, 0)),
            pl.BlockSpec(right.shape, lambda i: (0, 0), pipeline_mode=pl.Buffered(1)),
        ],
        out_specs=pl.BlockSpec((tile, width), lambda i: (i, 0)),
        compiler_params=pltpu.CompilerParams(vmem_limit_bytes=VMEM_BYTES),
    )(left, right)


def outer_kernel(left, right, out):
    out[0] = lax.dot_general(
        left[0], right[...], (((0,), (0,)), ((), ())), preferred_element_type=jnp.float32
    ).astype(out.dtype)


def stacked_outer(left, right):
    parts, tokens, depth = left.shape
    width = right.shape[1]
    return pl.pallas_call(
        outer_kernel,
        name="stacked_outer",
        grid=(parts,),
        out_shape=jax.ShapeDtypeStruct((parts, depth, width), jnp.bfloat16),
        in_specs=[
            pl.BlockSpec((1, tokens, depth), lambda i: (i, 0, 0)),
            pl.BlockSpec(right.shape, lambda i: (0, 0), pipeline_mode=pl.Buffered(1)),
        ],
        out_specs=pl.BlockSpec((1, depth, width), lambda i: (i, 0, 0)),
        compiler_params=pltpu.CompilerParams(vmem_limit_bytes=VMEM_BYTES),
    )(left, right)


def shifted(array, axis, by):
    length = lax.axis_size(axis)
    pairs = [(i, i + by) for i in range(length) if 0 <= i + by < length]
    return lax.ppermute(array, axis, pairs)


def slope(value, sig):
    return sig * (1.0 + value * (1.0 - sig))


def inner_rows(left, right, precision=None):
    return lax.dot_general(
        left,
        right,
        (((0,), (0,)), ((), ())),
        preferred_element_type=jnp.float32,
        precision=precision,
    )


def per_device(
    targets, resid, w_gate_in, w_x_in, conv_weight, conv_bias, skip_d, norm_gain, w_out, w_head
):
    f32 = jnp.float32
    bf16 = jnp.bfloat16
    exact = lax.Precision.HIGHEST
    tok_rows = resid.shape[0]
    seq_count = lax.axis_size("seq")
    local_inner = w_gate_in.shape[1]
    row_count = w_out.shape[0]
    halo_rows = KERNEL - 1
    mix_part = lax.psum(jnp.dot(w_out, w_head, preferred_element_type=f32), "chan")
    mix_hi = mix_part.astype(bf16)
    mix_lo = (mix_part - mix_hi.astype(f32)).astype(bf16)
    spare = jnp.zeros((row_count, 2 * VOCAB), bf16)
    shard = jnp.concatenate([w_gate_in, w_x_in, w_out, mix_hi, mix_lo, spare], axis=1)
    features, full = gather_all(resid, shard)
    full = full.reshape(INNER, shard.shape[1])
    mix_at = 3 * local_inner
    mix_rows = lax.dynamic_slice(
        full, (lax.axis_index("chan") * local_inner, mix_at), (local_inner, 2 * VOCAB)
    ).astype(f32)
    mix = mix_rows[:, :VOCAB] + mix_rows[:, VOCAB:]
    both_pre = stacked_dot(features, full, 0, 2 * local_inner, bf16)
    gate_pre = both_pre[:, :local_inner]
    x_pre = both_pre[:, local_inner:]
    before = shifted(x_pre[tok_rows - halo_rows :], "seq", 1)
    padded = jnp.concatenate([before, x_pre], axis=0).astype(f32)
    conv_out = jnp.zeros((tok_rows, local_inner), f32) + conv_bias
    for offset in range(KERNEL):
        conv_out = conv_out + conv_weight[offset] * padded[offset : offset + tok_rows]
    sig_conv = jax.nn.sigmoid(conv_out)
    active = conv_out * sig_conv
    gate_f32 = gate_pre.astype(f32)
    sig_gate = jax.nn.sigmoid(gate_f32)
    silu_gate = gate_f32 * sig_gate
    head_scale = jnp.repeat(skip_d, HEADDIM)
    gated = active * head_scale * silu_gate
    gained = gated * norm_gain
    sq_part = jnp.sum(gated * gated, axis=1)[None, :]
    head_part = lax.dot_general(
        w_head, resid, (((0,), (1,)), ((), ())), preferred_element_type=f32
    )
    gained_part = lax.dot_general(
        mix, gained, (((0,), (1,)), ((), ())), precision=exact, preferred_element_type=f32
    )
    stats = sum_stats(
        jnp.concatenate([head_part, gained_part, sq_part, jnp.zeros((7, tok_rows), f32)], axis=0)
    )
    inverse_row = lax.rsqrt(stats[2 * VOCAB : 2 * VOCAB + 1] / INNER + 1e-05)
    gained_head = stats[VOCAB : 2 * VOCAB]
    logits = stats[:VOCAB] + inverse_row * gained_head
    raised = jnp.exp(logits)
    probs = raised / jnp.sum(raised, axis=0, keepdims=True)
    onehot = (targets[None, :] == jnp.arange(VOCAB, dtype=jnp.int32)[:, None]).astype(f32)
    loss_weight = 4.0 / jnp.sqrt(jnp.asarray(tok_rows * seq_count, f32))
    dlogit_t = (probs - onehot) * loss_weight
    dot_row = jnp.sum(dlogit_t * gained_head, axis=0, keepdims=True)
    per_token = jnp.concatenate(
        [dlogit_t, inverse_row, inverse_row**3 * dot_row / INNER], axis=0
    ).T
    dlogit = per_token[:, :VOCAB]
    inverse = per_token[:, VOCAB : VOCAB + 1]
    pull = per_token[:, VOCAB + 1 :]
    dnormed = jnp.dot(dlogit, mix.T, precision=exact)
    dgated = inverse * norm_gain * dnormed - gated * pull
    gain_local = jnp.sum(dnormed * gated * inverse, axis=0)
    skip_local = jnp.sum(dgated * active * silu_gate, axis=0)
    dgate = (dgated * active * head_scale * slope(gate_f32, sig_gate)).astype(bf16)
    dconv = dgated * head_scale * silu_gate * slope(conv_out, sig_conv)
    bias_local = jnp.sum(dconv, axis=0)
    taps_local = jnp.stack(
        [jnp.sum(dconv * padded[offset : offset + tok_rows], axis=0) for offset in range(KERNEL)]
    )
    future = shifted(dconv[:halo_rows], "seq", -1)
    dpadded = jnp.concatenate([dconv, future], axis=0)
    dx_sum = jnp.zeros((tok_rows, local_inner), f32)
    for offset in range(KERNEL):
        dx_sum = (
            dx_sum
            + conv_weight[offset] * dpadded[halo_rows - offset : halo_rows - offset + tok_rows]
        )
    dx_pre = dx_sum.astype(bf16)
    head_local = jnp.dot(dlogit_t, resid.astype(f32), precision=exact)
    normed_local = jnp.dot(dlogit_t * inverse_row, gained, precision=exact)
    small = jnp.concatenate(
        [
            normed_local,
            head_local,
            taps_local,
            bias_local[None],
            gain_local[None],
            skip_local[None],
            jnp.zeros((1, local_inner), f32),
        ],
        axis=0,
    )
    both_grads = jnp.concatenate([dgate, dx_pre], axis=1)
    grads = stacked_outer(features, both_grads).reshape(NY, NZ, row_count, 2 * local_inner)
    grad_both, total, mix_grads, full_gained = finish_grads(grads, small, gained.astype(bf16))
    grad_gate_in = grad_both[:, :local_inner]
    grad_x_in = grad_both[:, local_inner:]
    at = 2 * VOCAB
    grad_conv_weight = total[at : at + KERNEL]
    grad_conv_bias = total[at + KERNEL]
    grad_gain = total[at + KERNEL + 1]
    grad_skip = total[at + KERNEL + 2].reshape(-1, HEADDIM).sum(axis=1)
    out_sum = stacked_dot(full_gained, full, 2 * local_inner, local_inner, f32)
    new_resid = (resid.astype(f32) + inverse * out_sum).astype(bf16)
    mix_grads = mix_grads.transpose(1, 0, 2).reshape(VOCAB, INNER)
    out_cols = full[:, 2 * local_inner : 3 * local_inner]
    grad_head = total[VOCAB : 2 * VOCAB].T + inner_rows(
        out_cols.astype(f32), mix_grads.T, exact
    )
    mix_grad_rows = lax.dynamic_slice_in_dim(
        mix_grads, lax.axis_index("seq") * row_count, row_count, 1
    )
    grad_out = inner_rows(mix_grad_rows, w_head.astype(f32).T, exact)
    return (
        new_resid,
        grad_gate_in,
        grad_x_in,
        grad_out,
        grad_head,
        grad_conv_weight,
        grad_conv_bias,
        grad_skip,
        grad_gain,
    )


def solution(mesh):
    return jax.shard_map(
        per_device,
        mesh=mesh,
        in_specs=(
            P("seq"),
            P("seq", "chan"),
            P("seq", "chan"),
            P("seq", "chan"),
            P(None, "chan"),
            P("chan"),
            P("chan"),
            P("chan"),
            P("seq", "chan"),
            P("chan", None),
        ),
        out_specs=(
            P("seq", "chan"),
            P("seq", "chan"),
            P("seq", "chan"),
            P("seq", "chan"),
            P("chan", None),
            P(None, "chan"),
            P("chan"),
            P("chan"),
            P("chan"),
        ),
        check_vma=False,
    )
```

time: 780 us -> 246 us (0.32)
  waiting for transfers between devices: 501 us -> 0.27 us
  blocking collectives: 209 us -> 24 us
  Pallas kernels: 0 us -> 171 us
  matrix products: 24.5 us -> 10.2 us
  between operations: 14.4 us -> 1.04 us
    all_gather x4 -> x0, waiting for transfers between devices: 224 us -> none  [the longest x1 76.3 us: per_device(): out_cols = lax.all_gather(w_out, 'seq', axis=0, tiled=True)]
    unnamed x7 -> x0, waiting for transfers between devices: 199 us -> none
    pallas_call x0 -> x6, Pallas kernels: none -> 171 us  [the longest x1 61.9 us: gather_all(): pl.pallas_call(gather_kernel, name='gather_all', out_shape=(jax.ShapeDtyp...]
    psum x2 -> x1, blocking collectives: 131 us -> 24 us  [per_device(): lax.psum(jnp.dot(w_out, w_head, preferred_element_type=f32), 'chan')]
    all_gather x2 -> x0, blocking collectives: 77.6 us -> none  [the longest x1 40.3 us: per_device(): mix_grads = lax.all_gather(grad_mix, 'chan', axis=0, tiled=True)]
    psum x1 -> x0, waiting for transfers between devices: 72.8 us -> none  [per_device(): lax.psum(jnp.concatenate([head_part, gained_part, sq_part], axis=1), 'chan')]
    dot_general x6 -> x5, matrix products: 16.3 us -> 4.22 us  [the longest x1 1.49 us: per_device(): lax.dot_general(mix, gained, (((0,), (1,)), ((), ())), precision=exact, p...]
  transfers between devices with their start and end apart: 8 -> 2, of which waited for: 7 -> 1; matrix products, arithmetic and copies ran while one was open for 1% -> 2% of each run, Pallas kernels for 0% -> 0%
where the time goes in v2:
time: 246 us; the launch traced here: 245 us
  Pallas kernels  171 us (70%)
  blocking collectives  24 us (10%)
  other arithmetic  21.6 us (9%)
  local copies, waits for them, and re-layouts  13.9 us (6%)
  matrix products  10.2 us (4%)
  starting transfers between devices  2.96 us (1%)
    pallas_call x1, Pallas kernels, gather_all(): pl.pallas_call(gather_kernel, name='gather_all', out_shape=(jax.ShapeDtyp...  61.9 us
    pallas_call x1, Pallas kernels, finish_grads(): pl.pallas_call(grads_kernel, name='finish_grads', out_shape=(jax.ShapeDty...  61.6 us
    psum x1, blocking collectives, per_device(): lax.psum(jnp.dot(w_out, w_head, preferred_element_type=f32), 'chan')  24 us
    pallas_call x2, Pallas kernels, stacked_dot(): pl.pallas_call(functools.partial(stacked_kernel, first), name='stacked_do...  19.3 us
    pallas_call x1, Pallas kernels, sum_stats(): pl.pallas_call(stats_kernel, name='sum_stats', out_shape=jax.ShapeDtypeSt...  18.1 us
    pallas_call x1, Pallas kernels, stacked_outer(): pl.pallas_call(outer_kernel, name='stacked_outer', grid=(parts,), out_sha...  10 us
  transfers between devices with their start and end apart: 2, of which 1 were waited for; matrix products, arithmetic and copies ran while one was open for 2% of the time, Pallas kernels for 0%

profile of v2, /device:TPU:1, one launch (start us, length us, event | category | flops | bytes accessed | tf_op | source)
XLA Modules:
  0.0 244.8 jit_solution(16044432947712418819)
XLA Ops:
  0.7 0.7 copy-done
  1.4 1.0 fusion.43
  2.3 24.0 %psum.7 = f32[80,16]{1,0:T(8,128)S(1)} all-reduce(f32[80,16]{1,0:T(8,128)S(1)} %fusion.43), channel_id=1, replica_groups=mesh['seq'=32,'chan'=8] {'chan'}, use_global_device_ids=true, to_apply=%region_0.0 | all-reduce | flops 1280 | bytes 10240 | tf_op jit(solution)/shard_map/psum | solution.py:483
  26.3 2.3 copy.32.resid
  28.6 0.8 concatenate.21.weights
  29.4 61.9 %gather_all.1 = (bf16[8,1024,320]{2,1,0:T(8,128)(2,1)}, bf16[4,8,80,1024]{3,2,1,0:T(8,128)(2,1)}) custom-call(bf16[1024,320]{1,0:T(8,128)(2,1)} %copy.32.resid, bf16[80,1024]{1,0:T(8,128)(2,1)} %concatenate.21.weights), custom_call_target="tpu_custom_call" | custom-call | tf_op jit(solution)/shard_map/gather_all/pallas_call | solution.py:193
  91.4 10.5 %stacked_dot.2 = bf16[1024,640]{1,0:T(8,128)(2,1)} custom-call(bf16[8,1024,320]{2,1,0:T(8,128)(2,1)} %get-tuple-element.16.left, bf16[2560,1024]{1,0:T(8,128)(2,1)} %bitcast.20), custom_call_target="tpu_custom_call" | custom-call | tf_op jit(solution)/shard_map/stacked_dot/pallas_call | solution.py:415
  101.9 0.8 slice.135
  102.7 1.5 collective-permute-start
  104.2 0.2 fusion.42
  104.4 1.0 dynamic-slice_convert_fusion
  105.4 1.5 slice.136
  107.0 0.1 mul.241
  107.1 0.1 pad.10.clone
  107.2 0.2 maximum_convert_fusion
  107.4 0.2 copy-done.12
  107.6 4.1 %multiply_convert_fusion = (bf16[1024,320]{1,0:T(8,128)(2,1)}, f32[1024,320]{1,0:T(8,128)S(1)}, f32[1024,320]{1,0:T(8,128)}) fusion(f32[320]{0:T(512)S(1)} %copy-done.12, bf16[1024,640]{1,0:T(8,128)(2,1)} %stacked_dot.2, f32[320]{0:T(512)S(1)} %mul.241, f32[1027,320]{1,0:T(8,128)S(1)} %maximum_convert_fusion, f32[320]{0:T(512)S(1)} %get-tuple-element.58, ...), kind=kLoop, calls=%fused_computation.38 | loop fusion | flops 6881280 | bytes 9184000 | tf_op jit(solution)/shard_map/convert_element_type | solution.py:571
  111.7 0.2 multiply_reduce_fusion.6
  112.0 1.5 fusion.21
  113.5 0.8 maximum_maximum_fusion.stats
  114.2 18.1 %sum_stats.1 = f32[40,1024]{1,0:T(8,128)} custom-call(f32[40,1024]{1,0:T(8,128)} %maximum_maximum_fusion.stats), custom_call_target="tpu_custom_call" | custom-call | tf_op jit(solution)/shard_map/sum_stats/pallas_call | solution.py:242
  132.3 0.8 add_rsqrt_fusion
  133.1 0.9 fusion.39
  134.0 0.9 multiply_reduce_fusion.7
  134.9 0.8 fusion.36
  135.7 1.9 fusion.29
  137.7 0.9 fusion.19
  138.6 3.3 %multiply_reduce_fusion = (f32[320]{0:T(512)S(1)}, f32[1024,320]{1,0:T(8,128)S(1)}, f32[320]{0:T(512)S(1)}, f32[320]{0:T(512)S(1)}, f32[320]{0:T(512)S(1)}, /*in...) fusion(bf16[1024,640]{1,0:T(8,128)(2,1)S(1)} %copy-done.1, ...), kind=kLoop, calls=%fused_computation.25 | loop fusion | flops 11466560 | bytes 12471552 | tf_op jit(solution)/shard_map/reduce_sum | solution.py:539
  141.9 0.6 fusion.16
  142.6 0.5 copy-done.3
  143.1 1.5 collective-permute-start.1
  144.6 0.6 fusion.44
  145.4 1.8 concatenate.27.small
  147.2 0.3 collective-permute-done.1
  147.5 4.2 %fusion.7 = bf16[1024,320]{1,0:T(8,128)(2,1)S(1)} fusion(f32[3,320]{1,0:T(4,128)S(1)} %collective-permute-done.1, f32[1024,320]{1,0:T(8,128)} %copy-done.3, f32[320]{0:T(512)S(1)} %get-tuple-element.58, f32[320]{0:T(512)S(1)} %get-tuple-element.59, f32[320]{0:T(512)S(1)} %get-tuple-element.57, f32[320]{0:T(512)S(1)} %get-tuple-element.56), kind=kLoop, calls=%fused_computation.12 | loop fusion | flops 3604480 | bytes 1975040 | tf_op jit(solution)/shard_map/convert_element_type | solution.py:554
  151.6 1.5 pad_maximum_fusion.1.right
  153.2 10.0 %stacked_outer.1 = bf16[8,320,640]{2,1,0:T(8,128)(2,1)} custom-call(bf16[8,1024,320]{2,1,0:T(8,128)(2,1)} %get-tuple-element.16.left, bf16[1024,640]{1,0:T(8,128)(2,1)} %pad_maximum_fusion.1.right), custom_call_target="tpu_custom_call" | custom-call | tf_op jit(solution)/shard_map/stacked_outer/pallas_call | solution.py:438
  163.2 61.6 %finish_grads.1 = (f32[80,640]{1,0:T(8,128)}, f32[40,320]{1,0:T(8,128)}, f32[8,16,320]{2,1,0:T(8,128)}, bf16[8,1024,320]{2,1,0:T(8,128)(2,1)}) custom-call(bf16[4,8,80,640]{3,2,1,0:T(8,128)(2,1)} %bitcast.24, f32[40,320]{1,0:T(8,128)} %concatenate.27.small, bf16[1024,320]{1,0:T(8,128)(2,1)} %get-tuple-element.60.gained), custom_call_target="tpu_custom_call" | custom-call | tf_op jit(solution)/shard_map/finish_grads/pallas_call | solution.py:372
  224.8 1.3 slice.129
  226.1 1.4 slice_reduce_fusion
  227.5 8.8 %stacked_dot.3 = f32[1024,320]{1,0:T(8,128)} custom-call(bf16[8,1024,320]{2,1,0:T(8,128)(2,1)} %get-tuple-element.17.left, bf16[2560,1024]{1,0:T(8,128)(2,1)} %bitcast.22), custom_call_target="tpu_custom_call" | custom-call | tf_op jit(solution)/shard_map/stacked_dot/pallas_call | solution.py:415
  236.3 1.7 add_convert_fusion
  238.0 1.1 copy.38
  239.2 0.6 reduce_sum.109
  239.9 0.1 reshape.34
  240.0 3.0 %fusion.23 = f32[320,16]{0,1:T(8,128)} fusion(f32[16,2560]{1,0:T(8,128)S(1)} %reshape.34, bf16[2560,1024]{1,0:T(8,128)(2,1)} %bitcast.23, f32[40,320]{1,0:T(8,128)} %get-tuple-element.20), kind=kOutput, calls=%fused_computation.44 | convolution fusion | flops 157291520 | bytes 2174976 | tf_op jit(solution)/shard_map/dot_general | solution.py:463
  243.1 1.0 fusion.33
  244.0 0.8 fusion.40
  (51 shorter events, 0.4 us)
Async XLA Ops:
  0.6 0.7 copy-start
  0.7 27.9 %copy-start.8 = (bf16[80,320]{1,0:T(8,128)(2,1)S(1)}, bf16[80,320]{1,0:T(8,128)(2,1)}, u32[]{:S(2)}) copy-start(bf16[80,320]{1,0:T(8,128)(2,1)} %param.18) | copy-start | bytes 153604
  0.7 27.9 %copy-start.11 = (bf16[80,320]{1,0:T(8,128)(2,1)S(1)}, bf16[80,320]{1,0:T(8,128)(2,1)}, u32[]{:S(2)}) copy-start(bf16[80,320]{1,0:T(8,128)(2,1)} %param.13) | copy-start | bytes 153604
  0.7 27.9 %copy-start.10 = (bf16[80,320]{1,0:T(8,128)(2,1)S(1)}, bf16[80,320]{1,0:T(8,128)(2,1)}, u32[]{:S(2)}) copy-start(bf16[80,320]{1,0:T(8,128)(2,1)} %param.12) | copy-start | bytes 153604
  91.4 12.8 %copy-start.5 = (bf16[1024,320]{0,1:T(8,128)(2,1)S(1)}, bf16[1024,320]{0,1:T(8,128)(2,1)}, u32[]{:S(2)}) copy-start(bf16[1024,320]{0,1:T(8,128)(2,1)} %param.11) | copy-start | bytes 1966084
  91.4 14.0 %copy-start.14 = (f32[4,320]{1,0:T(4,128)S(1)}, f32[4,320]{1,0:T(4,128)}, u32[]{:S(2)}) copy-start(f32[4,320]{1,0:T(4,128)} %param.14) | copy-start | bytes 15364
  101.9 5.0 %copy-start.16 = (f32[5]{0:T(128)S(1)}, f32[5]{0:T(128)}, u32[]{:S(2)}) copy-start(f32[5]{0:T(128)} %param.16) | copy-start | bytes 64
  102.7 4.5 %collective-permute-start = (bf16[3,320]{1,0:T(4,128)(2,1)S(1)}, bf16[3,320]{1,0:T(4,128)(2,1)S(1)}, u32[]{:S(2)}, u32[]{:S(2)}) collective-permute-start(bf16[3,320]{1,0:T(4,128)(2,1)S(1)} %slice.135), channel_id=1, source_target_pairs={{0,8},{8,16},{16,24},{24,32},{32,40},{40,48},{48,56},{56,64},{64,7... | collective-permute-start | bytes 5768 | tf_op jit(solution)/shard_map/ppermute | solution.py:455
  106.9 0.7 copy-start.12
  106.9 0.7 copy-start.15
  112.0 22.0 %copy-start.13 = (s32[1024]{0:T(1024)S(1)}, s32[1024]{0:T(1024)}, u32[]{:S(2)}) copy-start(s32[1024]{0:T(1024)} %param.10) | copy-start | bytes 12292
  135.7 2.9 %copy-start.1 = (bf16[1024,640]{1,0:T(8,128)(2,1)S(1)}, bf16[1024,640]{1,0:T(8,128)(2,1)}, u32[]{:S(2)}) copy-start(bf16[1024,640]{1,0:T(8,128)(2,1)} %stacked_dot.2) | copy-start | bytes 3932164
  135.7 2.9 %copy-start.4 = (f32[1024,320]{1,0:T(8,128)S(1)}, f32[1024,320]{1,0:T(8,128)}, u32[]{:S(2)}) copy-start(f32[1024,320]{1,0:T(8,128)} %get-tuple-element.62) | copy-start | bytes 3932164
  141.9 1.2 copy-start.3
  141.9 2.7 %copy-start.6 = (bf16[1024,320]{0,1:T(8,128)(2,1)S(1)}, bf16[1024,320]{0,1:T(8,128)(2,1)}, u32[]{:S(2)}) copy-start(bf16[1024,320]{0,1:T(8,128)(2,1)} %param.11) | copy-start | bytes 1966084
  143.1 4.4 %collective-permute-start.1 = (f32[3,320]{1,0:T(4,128)S(1)}, f32[3,320]{1,0:T(4,128)S(1)}, u32[]{:S(2)}, u32[]{:S(2)}) collective-permute-start(f32[3,320]{1,0:T(4,128)S(1)} %slice.145), channel_id=1, source_target_pairs={{8,0},{16,8},{24,16},{32,24},{40,32},{48,40},{56,48},{64,56},{72,6... | collective-permute-start | bytes 11528 | tf_op jit(solution)/shard_map/ppermute | solution.py:455
  227.5 8.8 %copy-start.2 = (bf16[1024,320]{1,0:T(8,128)(2,1)S(1)}, bf16[1024,320]{1,0:T(8,128)(2,1)}, u32[]{:S(2)}) copy-start(bf16[1024,320]{1,0:T(8,128)(2,1)} %copy.32.resid) | copy-start | bytes 1966084
  236.3 3.6 %copy-start.9 = (f32[8,16,320]{2,1,0:T(8,128)S(1)}, f32[8,16,320]{2,1,0:T(8,128)}, u32[]{:S(2)}) copy-start(f32[8,16,320]{2,1,0:T(8,128)} %get-tuple-element.19) | copy-start | bytes 491524
  239.1 4.9 %copy-start.7 = (f32[80,640]{1,0:T(8,128)S(1)}, f32[80,640]{1,0:T(8,128)}, u32[]{:S(2)}) copy-start(f32[80,640]{1,0:T(8,128)} %get-tuple-element.18) | copy-start | bytes 614404

commit v3 on v2

v3 whole, which is shorter than its diff:
```python
import functools

import jax
import jax.numpy as jnp
from jax import lax
from jax.experimental import pallas as pl
from jax.experimental.pallas import tpu as pltpu
from jax.sharding import PartitionSpec as P

HEADDIM = 64
KERNEL = 4
VOCAB = 16
INNER = 2560
NX, NY, NZ = 4, 4, 8
NCHAN = 2 * NX
MESH = pl.DeviceIdType.MESH
VMEM_BYTES = 56 * 1024 * 1024


class Wire:
    def __init__(self, send, recv):
        self.send, self.recv, self.copies = send, recv, []

    def put(self, source, target, **where):
        place = len(self.copies)
        copy = pltpu.make_async_remote_copy(
            src_ref=source,
            dst_ref=target,
            send_sem=self.send.at[place],
            recv_sem=self.recv.at[place],
            device_id=where,
            device_id_type=MESH,
        )
        copy.start()
        self.copies.append(copy)
        return copy

    def finish(self):
        for copy in self.copies:
            copy.wait_send()


def greet(peers):
    barrier = pltpu.get_barrier_semaphore()
    for peer in peers:
        pl.semaphore_signal(barrier, inc=1, device_id=peer, device_id_type=MESH)
    pl.semaphore_wait(barrier, len(peers))


def in_order(*streams):
    for stream in streams:
        next(stream, None)


def place():
    s, c = lax.axis_index("seq"), lax.axis_index("chan")
    return s // NZ, s % NZ, c


def gather_chan(wire, shard, full, c, rows):
    x, core = c // 2, c % 2
    mate = c + 1 - 2 * core
    right = lax.rem(x + 1, NX) * 2 + core
    left = lax.rem(x + NX - 1, NX) * 2 + core
    across = lax.rem(x + 2, NX) * 2 + core
    lo, hi = pl.ds(0, rows // 2), pl.ds(rows // 2, rows // 2)
    to_right_lo = wire.put(shard.at[lo], full.at[c, lo], chan=right)
    to_left_hi = wire.put(shard.at[hi], full.at[c, hi], chan=left)
    to_right_hi = wire.put(shard.at[hi], full.at[c, hi], chan=right)
    to_left_lo = wire.put(shard.at[lo], full.at[c, lo], chan=left)
    to_mate = [wire.put(shard, full.at[c], chan=mate)]
    yield
    to_right_lo.wait_recv()
    on_right = wire.put(full.at[left, lo], full.at[left, lo], chan=right)
    to_left_hi.wait_recv()
    on_left = wire.put(full.at[right, hi], full.at[right, hi], chan=left)
    yield
    to_right_hi.wait_recv()
    to_mate.append(wire.put(full.at[left], full.at[left], chan=mate))
    to_left_lo.wait_recv()
    to_mate.append(wire.put(full.at[right], full.at[right], chan=mate))
    yield
    on_right.wait_recv()
    to_mate.append(wire.put(full.at[across, lo], full.at[across, lo], chan=mate))
    on_left.wait_recv()
    to_mate.append(wire.put(full.at[across, hi], full.at[across, hi], chan=mate))
    yield
    for copy in to_mate:
        copy.wait_recv()


def ring_z(wire, first, block, halves, y, z):
    up, down = y * NZ + lax.rem(z + 1, NZ), y * NZ + lax.rem(z + NZ - 1, NZ)
    plus = wire.put(first, block(z), seq=up)
    minus = wire.put(first, block(z), seq=down)
    for step in range(1, NZ // 2):
        last = step == NZ // 2 - 1
        yield
        behind, ahead = lax.rem(z + NZ - step, NZ), lax.rem(z + step, NZ)
        plus.wait_recv()
        moved = halves(behind)[0] if last else block(behind)
        plus = wire.put(moved, moved, seq=up)
        minus.wait_recv()
        moved = halves(ahead)[1] if last else block(ahead)
        minus = wire.put(moved, moved, seq=down)
    yield
    plus.wait_recv()
    minus.wait_recv()


def exchange_y(wire, shard, full, y, z, rows):
    puts = [
        wire.put(shard.at[rows], full.at[y, z, rows], seq=lax.rem(y + d, NY) * NZ + z)
        for d in (1, 3, 2)
    ]
    yield
    for copy in puts:
        copy.wait_recv()


def ring_z_columns(wire, full, y, z, rows):
    yield from ring_z(
        wire,
        full.at[:, z, rows],
        lambda at: full.at[:, at, rows],
        lambda at: (full.at[pl.ds(0, 2), at, rows], full.at[pl.ds(2, 2), at, rows]),
        y,
        z,
    )


def ring_z_own(wire, shard, full, y, z, start, count):
    cut = (count // 32) * 16
    yield from ring_z(
        wire,
        shard.at[pl.ds(start, count)],
        lambda at: full.at[y, at, pl.ds(start, count)],
        lambda at: (
            full.at[y, at, pl.ds(start, cut)],
            full.at[y, at, pl.ds(start + cut, count - cut)],
        ),
        y,
        z,
    )


def exchange_y_lines(wire, full, y, z, rows):
    above, below = lax.rem(y + 1, NY), lax.rem(y + NY - 1, NY)
    up, down = above * NZ + z, below * NZ + z
    lo, hi = pl.ds(0, NZ // 2), pl.ds(NZ // 2, NZ // 2)
    up_lo = wire.put(full.at[y, lo, rows], full.at[y, lo, rows], seq=up)
    down_hi = wire.put(full.at[y, hi, rows], full.at[y, hi, rows], seq=down)
    up_hi = wire.put(full.at[y, hi, rows], full.at[y, hi, rows], seq=up)
    down_lo = wire.put(full.at[y, lo, rows], full.at[y, lo, rows], seq=down)
    yield
    up_lo.wait_recv()
    on_up = wire.put(full.at[below, lo, rows], full.at[below, lo, rows], seq=up)
    down_hi.wait_recv()
    on_down = wire.put(full.at[above, hi, rows], full.at[above, hi, rows], seq=down)
    yield
    for copy in (up_hi, down_lo, on_up, on_down):
        copy.wait_recv()


def gather_mix(wire, w_out, w_head, out, bufs, y, z, c):
    part, got_c, mine, line, picked = bufs
    rows = w_out.shape[0]
    part[...] = jnp.zeros_like(part)
    part[:, pl.ds(0, rows)] = lax.dot_general(
        w_head[...],
        w_out[...],
        (((1,), (1,)), ((), ())),
        preferred_element_type=jnp.float32,
    )
    puts = [
        wire.put(part, got_c.at[d - 1], chan=lax.rem(c + d, NCHAN)) for d in range(1, NCHAN)
    ]
    yield
    acc = part[...]
    for d in range(1, NCHAN):
        puts[d - 1].wait_recv()
        acc = acc + got_c[d - 1]
    mine[...] = acc
    line[z] = acc
    puts = [
        wire.put(mine, line.at[z], seq=y * NZ + lax.rem(z + d, NZ)) for d in range(1, NZ)
    ]
    yield
    for copy in puts:
        copy.wait_recv()
    kept = pl.ds((c % 2) * (NZ // 2), NZ // 2)
    puts = [
        wire.put(line.at[kept], picked.at[y], seq=lax.rem(y + d, NY) * NZ + z)
        for d in range(1, NY)
    ]
    picked[y] = line[kept]
    yield
    for copy in puts:
        copy.wait_recv()
    for at in range(NZ // 2):
        out[:, pl.ds(at * rows, rows)] = picked[c // 2, at][:, :rows]


def gather_kernel(
    resid, weights, w_out, w_head, full_resid, full_weights, mix, *scratch
):
    *mix_bufs, send, recv, local = scratch
    y, z, c = place()
    greet(
        [{"chan": lax.rem(c + d, NCHAN)} for d in range(1, NCHAN)]
        + [{"seq": lax.rem(y + d, NY) * NZ + z} for d in range(1, NY)]
        + [{"seq": y * NZ + lax.rem(z + d, NZ)} for d in range(1, NZ)]
    )
    wire = Wire(send, recv)
    own_weights = pltpu.make_async_copy(weights, full_weights.at[y, z], local.at[0])
    own_resid = pltpu.make_async_copy(resid, full_resid.at[c], local.at[1])
    own_weights.start()
    own_resid.start()
    rows, first = weights.shape[0], 32
    one, rest = pl.ds(0, first), pl.ds(first, rows - first)
    b_ring = ring_z_own(wire, weights, full_weights, y, z, first, rows - first)
    b_lines = exchange_y_lines(wire, full_weights, y, z, rest)
    a_own = exchange_y(wire, weights, full_weights, y, z, one)
    a_ring = ring_z_columns(wire, full_weights, y, z, one)
    chans = gather_chan(wire, resid, full_resid, c, resid.shape[0])
    mixes = gather_mix(wire, w_out, w_head, mix, mix_bufs, y, z, c)
    in_order(b_ring, a_own, chans, mixes, b_ring, a_own, mixes, b_ring, mixes, b_ring)
    own_weights.wait()
    in_order(b_ring, b_lines, a_ring, mixes, chans, a_ring, chans, a_ring, b_lines)
    in_order(a_ring, chans, a_ring, b_lines, chans)
    own_resid.wait()
    wire.finish()


def gather_all(resid, weights, w_out, w_head):
    anywhere = pl.BlockSpec(memory_space=pl.ANY)
    vmem = pl.BlockSpec(memory_space=pltpu.VMEM)
    f32 = jnp.float32
    copies = 64
    block = (VOCAB, 128)
    return pl.pallas_call(
        gather_kernel,
        name="gather_all",
        out_shape=(
            jax.ShapeDtypeStruct((NCHAN, *resid.shape), resid.dtype),
            jax.ShapeDtypeStruct((NY, NZ, *weights.shape), weights.dtype),
            jax.ShapeDtypeStruct((VOCAB, resid.shape[1]), f32),
        ),
        in_specs=[anywhere] * 2 + [vmem] * 2,
        out_specs=(anywhere, anywhere, vmem),
        scratch_shapes=[
            pltpu.VMEM(block, f32),
            pltpu.VMEM((NCHAN - 1, *block), f32),
            pltpu.VMEM(block, f32),
            pltpu.VMEM((NZ, *block), f32),
            pltpu.VMEM((NY, NZ // 2, *block), f32),
            pltpu.SemaphoreType.DMA((copies,)),
            pltpu.SemaphoreType.DMA((copies,)),
            pltpu.SemaphoreType.DMA((2,)),
        ],
        compiler_params=pltpu.CompilerParams(collective_id=0, has_side_effects=True),
        cost_estimate=pl.CostEstimate(flops=10**10, bytes_accessed=10**8, transcendentals=0),
    )(resid, weights, w_out, w_head)


EXACT = lax.Precision.HIGHEST
LANES = 128
EDGE = 16
SUMS = 40
FACTS = 24


def middle_kernel(
    gate,
    xs,
    resid,
    head_t,
    mix_t,
    params,
    targets,
    dgate,
    dx,
    small,
    gained,
    facts,
    padded,
    prods,
    to_gate,
    to_conv,
    sums,
    parts,
    mine,
    before,
    after,
    acc_rows,
    acc_heads,
    send,
    recv,
):
    f32, bf16 = jnp.float32, jnp.bfloat16
    tokens = gate.shape[0]
    y, z, c = place()
    s = y * NZ + z
    last_seq = NY * NZ - 1
    later, sooner = lax.rem(s + 1, NY * NZ), lax.rem(s + last_seq, NY * NZ)
    greet(
        [{"chan": lax.rem(c + d, NCHAN)} for d in range(1, NCHAN)]
        + [{"seq": later}, {"seq": sooner}]
    )

    def copy_of(source, target, at, where):
        return pltpu.make_async_remote_copy(
            src_ref=source,
            dst_ref=target,
            send_sem=send.at[at],
            recv_sem=recv.at[at],
            device_id=where,
            device_id_type=MESH,
        )

    edge = copy_of(xs.at[pl.ds(tokens - EDGE, EDGE)], before, 2 * NCHAN, {"seq": later})
    edge.start()
    taps = [params[k : k + 1, :] for k in range(KERNEL)]
    bias, skip, gain = params[4:5, :], params[5:6, :], params[6:7, :]
    mix = mix_t[...]
    padded[pl.ds(EDGE, tokens), :] = xs[...].astype(f32)

    def window(tile):
        start = pl.multiple_of(tile * LANES, LANES)
        return pl.ds(start, LANES), padded[pl.ds(start, LANES + EDGE), :]

    def shifted(win, k):
        first = EDGE - (KERNEL - 1) + k
        return win[first : first + LANES]

    def share(step):
        peer = lax.rem(c + 1 + step, NCHAN)
        return copy_of(sums.at[peer], parts.at[step], step, {"chan": peer})

    def forward(tile):
        rows, win = window(tile)
        conv = bias + taps[0] * shifted(win, 0)
        for k in range(1, KERNEL):
            conv = conv + taps[k] * shifted(win, k)
        sig_conv = jax.nn.sigmoid(conv)
        active = conv * sig_conv
        gate_pre = gate[rows, :].astype(f32)
        sig_gate = jax.nn.sigmoid(gate_pre)
        silu_gate = gate_pre * sig_gate
        prod = active * silu_gate
        prods[rows, :] = prod
        to_gate[rows, :] = skip * active * slope(gate_pre, sig_gate)
        to_conv[rows, :] = skip * silu_gate * slope(conv, sig_conv)
        gated = prod * skip
        with_gain = gated * gain
        gained[rows, :] = with_gain.astype(bf16)
        by_lanes = (((1,), (1,)), ((), ()))
        sums[tile, pl.ds(0, VOCAB)] = lax.dot_general(
            head_t[...], resid[rows, :], by_lanes, preferred_element_type=f32
        )
        sums[tile, pl.ds(VOCAB, VOCAB)] = lax.dot_general(
            mix, with_gain, by_lanes, precision=EXACT, preferred_element_type=f32
        )
        sums[tile, pl.ds(2 * VOCAB, 8)] = lax.dot_general(
            jnp.ones((8, gated.shape[1]), f32),
            gated * gated,
            by_lanes,
            precision=EXACT,
            preferred_element_type=f32,
        )

    edge.wait_recv()
    padded[pl.ds(0, EDGE), :] = before[...].astype(f32) * (s > 0).astype(f32)

    def forward_step(step, carry):
        forward(lax.rem(c + 1 + step, NCHAN))
        share(step).start()
        return carry

    lax.fori_loop(0, NCHAN - 1, forward_step, 0)
    forward(c)
    total = sums[c]
    for step in range(NCHAN - 1):
        share(step).wait_recv()
        total = total + parts[step]
    inverse = lax.rsqrt(total[2 * VOCAB : 2 * VOCAB + 1] / INNER + 1e-05)
    gained_head = total[VOCAB : 2 * VOCAB]
    raised = jnp.exp(total[:VOCAB] + inverse * gained_head)
    probs = raised / jnp.sum(raised, axis=0, keepdims=True)
    words = lax.broadcasted_iota(jnp.int32, (VOCAB, LANES), 0)
    onehot = (words == targets[c]).astype(f32)
    weight = 4.0 / float(tokens * NY * NZ) ** 0.5
    dlogit = (probs - onehot) * weight
    dot_gn = jnp.sum(dlogit * gained_head, axis=0, keepdims=True)
    mine[pl.ds(0, VOCAB), :] = dlogit
    mine[pl.ds(VOCAB, 8), :] = jnp.concatenate(
        [inverse, inverse * inverse * inverse * dot_gn / INNER, jnp.zeros((6, LANES), f32)],
        axis=0,
    )
    facts[c] = mine[...]

    def tell(d):
        return copy_of(
            mine, facts.at[c], NCHAN - 1 + d, {"chan": lax.rem(c + d, NCHAN)}
        )

    for d in range(1, NCHAN):
        tell(d).start()
    acc_rows[...] = jnp.zeros_like(acc_rows)
    acc_heads[...] = jnp.zeros_like(acc_heads)
    for d in range(1, NCHAN):
        tell(d).wait_recv()
    second = (
        lax.broadcasted_iota(jnp.int32, (8, mix.shape[1]), 0) == 1
    ).astype(f32)

    def fold(value):
        return jnp.sum(value.reshape(LANES // 8, 8, value.shape[1]), axis=0)

    def backward(tile):
        rows, win = window(tile)
        fact = facts[tile]
        dlogit = fact[:VOCAB]
        scaled = dlogit * fact[VOCAB : VOCAB + 1]
        by_rows = (((0,), (0,)), ((), ()))
        dnormed = lax.dot_general(
            scaled, mix, by_rows, precision=EXACT, preferred_element_type=f32
        )
        pull = lax.dot_general(
            fact[VOCAB : VOCAB + 8], second, by_rows, precision=EXACT, preferred_element_type=f32
        )
        prod = prods[rows, :]
        dgated = gain * dnormed - skip * prod * pull
        dgate[rows, :] = (dgated * to_gate[rows, :]).astype(bf16)
        dconv = dgated * to_conv[rows, :]
        to_conv[rows, :] = dconv
        for k in range(KERNEL):
            acc_rows[k] += fold(dconv * shifted(win, k))
        acc_rows[KERNEL] += fold(dconv)
        acc_rows[KERNEL + 1] += fold(dgated * prod)
        acc_heads[0] += jnp.dot(scaled, prod, precision=EXACT, preferred_element_type=f32)
        acc_heads[1] += jnp.dot(
            dlogit, resid[rows, :].astype(f32), precision=EXACT, preferred_element_type=f32
        )

    backward(0)
    first_rows = copy_of(to_conv.at[pl.ds(0, 8)], after, 2 * NCHAN + 1, {"seq": sooner})
    first_rows.start()

    def backward_step(tile, carry):
        backward(tile)
        return carry

    lax.fori_loop(1, tokens // LANES, backward_step, 0)
    by_channel = acc_heads[0]
    small[pl.ds(0, VOCAB), :] = by_channel * skip * gain
    small[pl.ds(VOCAB, VOCAB), :] = acc_heads[1]
    lines = [jnp.sum(acc_rows[k], axis=0, keepdims=True) for k in range(KERNEL + 2)]
    lines.insert(KERNEL + 1, skip * jnp.sum(mix * by_channel, axis=0, keepdims=True))
    lines.append(jnp.zeros_like(skip))
    small[pl.ds(2 * VOCAB, 8), :] = jnp.concatenate(lines, axis=0)
    first_rows.wait_recv()
    to_conv[pl.ds(tokens, 8), :] = after[...] * (s < last_seq).astype(f32)

    def spread_step(tile, carry):
        start = pl.multiple_of(tile * LANES, LANES)
        win = to_conv[pl.ds(start, LANES + 8), :]
        acc = taps[KERNEL - 1] * win[0:LANES]
        for k in range(KERNEL - 1):
            acc = acc + taps[k] * win[KERNEL - 1 - k : KERNEL - 1 - k + LANES]
        dx[pl.ds(start, LANES), :] = acc.astype(bf16)
        return carry

    lax.fori_loop(0, tokens // LANES, spread_step, 0)
    edge.wait_send()
    first_rows.wait_send()
    for d in range(1, NCHAN):
        share(d - 1).wait_send()
        tell(d).wait_send()


def middle(gate, xs, resid, head_t, mix_t, params, targets):
    f32, bf16 = jnp.float32, jnp.bfloat16
    vmem = pl.BlockSpec(memory_space=pltpu.VMEM)
    tokens, width = gate.shape
    copies = 2 * NCHAN + 2
    return pl.pallas_call(
        middle_kernel,
        name="middle",
        out_shape=(
            jax.ShapeDtypeStruct((tokens, width), bf16),
            jax.ShapeDtypeStruct((tokens, width), bf16),
            jax.ShapeDtypeStruct((SUMS, width), f32),
            jax.ShapeDtypeStruct((tokens, width), bf16),
            jax.ShapeDtypeStruct((NCHAN, FACTS, LANES), f32),
        ),
        in_specs=[vmem] * 7,
        out_specs=(vmem,) * 5,
        scratch_shapes=[
            pltpu.VMEM((tokens + EDGE, width), f32),
            pltpu.VMEM((tokens, width), f32),
            pltpu.VMEM((tokens, width), f32),
            pltpu.VMEM((tokens + 8, width), f32),
            pltpu.VMEM((NCHAN, SUMS, LANES), f32),
            pltpu.VMEM((NCHAN - 1, SUMS, LANES), f32),
            pltpu.VMEM((FACTS, LANES), f32),
            pltpu.VMEM((EDGE, width), bf16),
            pltpu.VMEM((8, width), f32),
            pltpu.VMEM((KERNEL + 2, 8, width), f32),
            pltpu.VMEM((2, VOCAB, width), f32),
            pltpu.SemaphoreType.DMA((copies,)),
            pltpu.SemaphoreType.DMA((copies,)),
        ],
        compiler_params=pltpu.CompilerParams(
            collective_id=1, has_side_effects=True, vmem_limit_bytes=VMEM_BYTES
        ),
        cost_estimate=pl.CostEstimate(flops=10**10, bytes_accessed=10**7, transcendentals=0),
    )(gate, xs, resid, head_t, mix_t, params, targets)


def scatter_seq(wire, grads, bufs, out, y, z, start, count):
    f32, bf16 = jnp.float32, jnp.bfloat16
    from_below, from_above, via_up, via_down, got_below, got_above, lines, got_z = bufs
    rows = pl.ds(start, count)
    lo, hi = pl.ds(0, NZ // 2), pl.ds(NZ // 2, NZ // 2)
    above, below, across = lax.rem(y + 1, NY), lax.rem(y + 3, NY), lax.rem(y + 2, NY)
    up, down = above * NZ + z, below * NZ + z
    half_up = wire.put(grads.at[across, lo, rows], from_below.at[:, rows], seq=up)
    half_down = wire.put(grads.at[across, hi, rows], from_above.at[:, rows], seq=down)
    moves = [
        wire.put(grads.at[above, hi, rows], got_below.at[hi, rows], seq=up),
        wire.put(grads.at[below, lo, rows], got_above.at[lo, rows], seq=down),
    ]
    yield
    half_up.wait_recv()
    via_up[:, rows] = (
        grads[above, lo, rows].astype(f32) + from_below[:, rows].astype(f32)
    ).astype(bf16)
    moves.append(wire.put(via_up.at[:, rows], got_below.at[lo, rows], seq=up))
    half_down.wait_recv()
    via_down[:, rows] = (
        grads[below, hi, rows].astype(f32) + from_above[:, rows].astype(f32)
    ).astype(bf16)
    moves.append(wire.put(via_down.at[:, rows], got_above.at[hi, rows], seq=down))
    yield
    for copy in moves[:2]:
        copy.wait_recv()
    yield
    for copy in moves[2:]:
        copy.wait_recv()
    lines[:, rows] = (
        grads[y, :, rows].astype(f32)
        + got_below[:, rows].astype(f32)
        + got_above[:, rows].astype(f32)
    ).astype(bf16)
    puts = []
    for d in range(1, NZ):
        peer = lax.rem(z + d, NZ)
        puts.append(wire.put(lines.at[peer, rows], got_z.at[d - 1, rows], seq=y * NZ + peer))
    yield
    acc = (
        grads[y, z, rows].astype(f32)
        + got_below[z, rows].astype(f32)
        + got_above[z, rows].astype(f32)
    )
    for d in range(1, NZ):
        puts[d - 1].wait_recv()
        acc = acc + got_z[d - 1, rows].astype(f32)
    out[rows] = acc


def sum_small(wire, small, got_y, part, got_z, total, heads, y, z, c):
    puts = [
        wire.put(small, got_y.at[y], seq=lax.rem(y + d, NY) * NZ + z) for d in range(1, NY)
    ]
    got_y[y] = small[...]
    yield
    for copy in puts:
        copy.wait_recv()
    acc = got_y[0]
    for at in range(1, NY):
        acc = acc + got_y[at]
    part[...] = acc
    puts = [
        wire.put(part, got_z.at[z], seq=y * NZ + lax.rem(z + d, NZ)) for d in range(1, NZ)
    ]
    got_z[z] = acc
    yield
    for copy in puts:
        copy.wait_recv()
    acc = got_z[0]
    for at in range(1, NZ):
        acc = acc + got_z[at]
    total[...] = acc
    first = pl.ds(0, VOCAB)
    puts = [
        wire.put(total.at[first], heads.at[c], chan=lax.rem(c + d, NCHAN))
        for d in range(1, NCHAN)
    ]
    heads[c] = total[first]
    yield
    for copy in puts:
        copy.wait_recv()


def grads_kernel(
    grads, small, gained, out, total, heads, full_gained, *scratch
):
    *bufs, small_y, small_part, small_z, send, recv, local = scratch
    y, z, c = place()
    greet(
        [{"chan": lax.rem(c + d, NCHAN)} for d in range(1, NCHAN)]
        + [{"seq": lax.rem(y + d, NY) * NZ + z} for d in range(1, NY)]
        + [{"seq": y * NZ + lax.rem(z + d, NZ)} for d in range(1, NZ)]
    )
    wire = Wire(send, recv)
    own = pltpu.make_async_copy(gained, full_gained.at[c], local.at[0])
    own.start()
    rows = out.shape[0]
    smalls = sum_small(wire, small, small_y, small_part, small_z, total, heads, y, z, c)
    one = scatter_seq(wire, grads, bufs, out, y, z, 0, 48)
    two = scatter_seq(wire, grads, bufs, out, y, z, 48, rows - 48)
    chans = gather_chan(wire, gained, full_gained, c, gained.shape[0])
    in_order(smalls, one, chans, smalls, one, chans, one, two, one)
    in_order(smalls, chans, two, two, two, chans, smalls, one, two, chans)
    own.wait()
    wire.finish()


def finish_grads(grads, small, gained):
    f32, bf16 = jnp.float32, jnp.bfloat16
    anywhere = pl.BlockSpec(memory_space=pl.ANY)
    vmem = pl.BlockSpec(memory_space=pltpu.VMEM)
    _, _, rows, cols = grads.shape
    copies = 64
    half = (NZ // 2, rows, cols)
    line = (NZ, rows, cols)
    return pl.pallas_call(
        grads_kernel,
        name="finish_grads",
        out_shape=(
            jax.ShapeDtypeStruct((rows, cols), f32),
            jax.ShapeDtypeStruct(small.shape, f32),
            jax.ShapeDtypeStruct((NCHAN, VOCAB, small.shape[1]), f32),
            jax.ShapeDtypeStruct((NCHAN, *gained.shape), bf16),
        ),
        in_specs=[vmem, vmem, anywhere],
        out_specs=(vmem, vmem, vmem, anywhere),
        scratch_shapes=[pltpu.VMEM(half, bf16)] * 4
        + [pltpu.VMEM(line, bf16)] * 3
        + [
            pltpu.VMEM((NZ - 1, rows, cols), bf16),
            pltpu.VMEM((NY, *small.shape), f32),
            pltpu.VMEM(small.shape, f32),
            pltpu.VMEM((NZ, *small.shape), f32),
            pltpu.SemaphoreType.DMA((copies,)),
            pltpu.SemaphoreType.DMA((copies,)),
            pltpu.SemaphoreType.DMA((1,)),
        ],
        compiler_params=pltpu.CompilerParams(
            collective_id=2, has_side_effects=True, vmem_limit_bytes=VMEM_BYTES
        ),
        cost_estimate=pl.CostEstimate(flops=10**10, bytes_accessed=10**8, transcendentals=0),
    )(grads, small, gained)


def sum_of_dots(left, right):
    depth = left.shape[2]
    acc = jnp.dot(left[0], right[pl.ds(0, depth), :], preferred_element_type=jnp.float32)
    for at in range(1, left.shape[0]):
        acc = acc + jnp.dot(
            left[at], right[pl.ds(at * depth, depth), :], preferred_element_type=jnp.float32
        )
    return acc


def project_kernel(left, right, gate, xs):
    acc = sum_of_dots(left, right)
    width = gate.shape[1]
    gate[...] = acc[:, :width].astype(gate.dtype)
    xs[...] = acc[:, width:].astype(xs.dtype)


def project(left, right):
    parts, tokens, depth = left.shape
    tile, width = 256, right.shape[1] // 2
    half = pl.BlockSpec((tile, width), lambda i: (i, 0))
    return pl.pallas_call(
        project_kernel,
        name="project",
        grid=(tokens // tile,),
        out_shape=(jax.ShapeDtypeStruct((tokens, width), jnp.bfloat16),) * 2,
        in_specs=[
            pl.BlockSpec((parts, tile, depth), lambda i: (0, i, 0)),
            pl.BlockSpec(right.shape, lambda i: (0, 0), pipeline_mode=pl.Buffered(1)),
        ],
        out_specs=(half, half),
        compiler_params=pltpu.CompilerParams(vmem_limit_bytes=VMEM_BYTES),
    )(left, right)


def residual_kernel(left, right, resid, facts, out):
    acc = sum_of_dots(left, right)
    inverse = (
        lax.broadcasted_iota(jnp.int32, (8, out.shape[1]), 0) == 0
    ).astype(jnp.float32)
    for at in range(facts.shape[0]):
        rows = pl.ds(at * LANES, LANES)
        scale = lax.dot_general(
            facts[at, pl.ds(VOCAB, 8)],
            inverse,
            (((0,), (0,)), ((), ())),
            precision=EXACT,
            preferred_element_type=jnp.float32,
        )
        summed = resid[rows, :].astype(jnp.float32) + scale * acc[at * LANES : at * LANES + LANES]
        out[rows, :] = summed.astype(out.dtype)


def add_projected(left, right, resid, facts):
    parts, tokens, depth = left.shape
    tile, width = 256, right.shape[1]
    rows = pl.BlockSpec((tile, width), lambda i: (i, 0))
    return pl.pallas_call(
        residual_kernel,
        name="add_projected",
        grid=(tokens // tile,),
        out_shape=jax.ShapeDtypeStruct((tokens, width), jnp.bfloat16),
        in_specs=[
            pl.BlockSpec((parts, tile, depth), lambda i: (0, i, 0)),
            pl.BlockSpec(right.shape, lambda i: (0, 0), pipeline_mode=pl.Buffered(1)),
            rows,
            pl.BlockSpec((tile // LANES, FACTS, LANES), lambda i: (i, 0, 0)),
        ],
        out_specs=rows,
        compiler_params=pltpu.CompilerParams(vmem_limit_bytes=VMEM_BYTES),
    )(left, right, resid, facts)


def outer_kernel(left, dgate, dx, out, both):
    width = dgate.shape[1]

    @pl.when(pl.program_id(0) == 0)
    def _():
        both[:, pl.ds(0, width)] = dgate[...]
        both[:, pl.ds(width, width)] = dx[...]

    out[0] = lax.dot_general(
        left[0], both[...], (((0,), (0,)), ((), ())), preferred_element_type=jnp.float32
    ).astype(out.dtype)


def stacked_outer(left, dgate, dx):
    parts, tokens, depth = left.shape
    width = 2 * dgate.shape[1]
    whole = pl.BlockSpec(dgate.shape, lambda i: (0, 0), pipeline_mode=pl.Buffered(1))
    return pl.pallas_call(
        outer_kernel,
        name="stacked_outer",
        grid=(parts,),
        out_shape=jax.ShapeDtypeStruct((parts, depth, width), jnp.bfloat16),
        in_specs=[pl.BlockSpec((1, tokens, depth), lambda i: (i, 0, 0)), whole, whole],
        out_specs=pl.BlockSpec((1, depth, width), lambda i: (i, 0, 0)),
        scratch_shapes=[pltpu.VMEM((tokens, width), jnp.bfloat16)],
        compiler_params=pltpu.CompilerParams(vmem_limit_bytes=VMEM_BYTES),
    )(left, dgate, dx)


def slope(value, sig):
    return sig * (1.0 + value * (1.0 - sig))


def inner_rows(left, right, precision=None):
    return lax.dot_general(
        left,
        right,
        (((0,), (0,)), ((), ())),
        preferred_element_type=jnp.float32,
        precision=precision,
    )


def per_device(
    targets, resid, w_gate_in, w_x_in, conv_weight, conv_bias, skip_d, norm_gain, w_out, w_head
):
    f32 = jnp.float32
    local_inner = w_gate_in.shape[1]
    row_count = w_out.shape[0]
    out_cols = lax.all_gather(w_out, "seq", axis=0, tiled=True)
    head_t = w_head.T
    features, full, mix_t = gather_all(
        resid, jnp.concatenate([w_gate_in, w_x_in], axis=1), w_out, head_t
    )
    gate_pre, x_pre = project(features, full.reshape(INNER, 2 * local_inner))
    params = jnp.concatenate(
        [
            conv_weight,
            conv_bias[None],
            jnp.repeat(skip_d, HEADDIM)[None],
            norm_gain[None],
            jnp.zeros((1, local_inner), f32),
        ],
        axis=0,
    )
    dgate, dx_pre, small, gained, facts = middle(
        gate_pre, x_pre, resid, head_t, mix_t, params, targets.reshape(NCHAN, 1, LANES)
    )
    grads = stacked_outer(features, dgate, dx_pre).reshape(NY, NZ, row_count, 2 * local_inner)
    grad_both, total, mix_grads, full_gained = finish_grads(grads, small, gained)
    grad_gate_in = grad_both[:, :local_inner]
    grad_x_in = grad_both[:, local_inner:]
    at = 2 * VOCAB
    grad_conv_weight = total[at : at + KERNEL]
    grad_conv_bias = total[at + KERNEL]
    grad_gain = total[at + KERNEL + 1]
    grad_skip = total[at + KERNEL + 2].reshape(-1, HEADDIM).sum(axis=1)
    new_resid = add_projected(full_gained, out_cols, resid, facts)
    mix_grads = mix_grads.transpose(1, 0, 2).reshape(VOCAB, INNER)
    grad_head = total[VOCAB : 2 * VOCAB].T + inner_rows(
        out_cols.astype(f32), mix_grads.T, EXACT
    )
    mix_grad_rows = lax.dynamic_slice_in_dim(
        mix_grads, lax.axis_index("seq") * row_count, row_count, 1
    )
    grad_out = inner_rows(mix_grad_rows, w_head.astype(f32).T, EXACT)
    return (
        new_resid,
        grad_gate_in,
        grad_x_in,
        grad_out,
        grad_head,
        grad_conv_weight,
        grad_conv_bias,
        grad_skip,
        grad_gain,
    )


def solution(mesh):
    return jax.shard_map(
        per_device,
        mesh=mesh,
        in_specs=(
            P("seq"),
            P("seq", "chan"),
            P("seq", "chan"),
            P("seq", "chan"),
            P(None, "chan"),
            P("chan"),
            P("chan"),
            P("chan"),
            P("seq", "chan"),
            P("chan", None),
        ),
        out_specs=(
            P("seq", "chan"),
            P("seq", "chan"),
            P("seq", "chan"),
            P("seq", "chan"),
            P("chan", None),
            P(None, "chan"),
            P("chan"),
            P("chan"),
            P("chan"),
        ),
        check_vma=False,
    )
```

time: 246 us -> 208 us (0.85)
  blocking collectives: 24 us -> 0 us
  other arithmetic: 21.6 us -> 2.22 us
  between operations: 1.04 us -> 14.1 us
  matrix products: 10.2 us -> 3.21 us
  Pallas kernels: 171 us -> 174 us
  starting transfers between devices: 2.96 us -> 0.04 us
    psum x1 -> x0, blocking collectives: 24 us -> none  [per_device(): lax.psum(jnp.dot(w_out, w_head, preferred_element_type=f32), 'chan')]
    pallas_call x3, Pallas kernels: 37.4 us -> 52.1 us  [the longest x1 33.1 us: middle(): pl.pallas_call(middle_kernel, name='middle', out_shape=(jax.ShapeDtypeStr...]
    pallas_call x1, Pallas kernels: 61.6 us -> 48.8 us  [finish_grads(): pl.pallas_call(grads_kernel, name='finish_grads', out_shape=(jax.ShapeDty...]
    convert_element_type x7 -> x0, other arithmetic: 11.8 us -> none  [the longest x1 4.16 us: per_device(): dx_pre = dx_sum.astype(bf16)]
    dot_general x6 -> x0, matrix products: 6.15 us -> none  [the longest x1 1.94 us: per_device(): dnormed = jnp.dot(dlogit, mix.T, precision=exact)]
    reduce_sum x4 -> x0, other arithmetic: 5.28 us -> none  [the longest x1 3.3 us: per_device(): skip_local = jnp.sum(dgated * active * silu_gate, axis=0)]
    ppermute x2 -> x0, starting transfers between devices: 2.96 us -> none  [shifted(): return lax.ppermute(array, axis, pairs)]
  transfers between devices with their start and end apart: 2 -> 1, of which waited for: 1 -> 0; matrix products, arithmetic and copies ran while one was open for 2% -> 7% of each run, Pallas kernels for 0% -> 80%
where the time goes in v3:
time: 208 us
  Pallas kernels  174 us (84%)
  between operations  14.1 us (7%)
  local copies, waits for them, and re-layouts  12.9 us (6%)
  matrix products  3.21 us (2%)
  other arithmetic  2.22 us (1%)
    pallas_call x1, Pallas kernels, gather_all(): pl.pallas_call(gather_kernel, name='gather_all', out_shape=(jax.ShapeDtyp...  63.1 us
    pallas_call x1, Pallas kernels, finish_grads(): pl.pallas_call(grads_kernel, name='finish_grads', out_shape=(jax.ShapeDty...  48.8 us
    pallas_call x1, Pallas kernels, middle(): pl.pallas_call(middle_kernel, name='middle', out_shape=(jax.ShapeDtypeStr...  33.1 us
    pallas_call x1, Pallas kernels, stacked_outer(): pl.pallas_call(outer_kernel, name='stacked_outer', grid=(parts,), out_sha...  10.5 us
    pallas_call x1, Pallas kernels, project(): pl.pallas_call(project_kernel, name='project', grid=(tokens // tile,), ou...  10.3 us
    pallas_call x1, Pallas kernels, add_projected(): pl.pallas_call(residual_kernel, name='add_projected', grid=(tokens // til...  8.71 us
    unnamed x8, local copies, waits for them, and re-layouts  4.49 us
  transfers between devices with their start and end apart: 1, of which 0 were waited for; matrix products, arithmetic and copies ran while one was open for 7% of the time, Pallas kernels for 80%

profile of v3, /device:TPU:1, one launch (start us, length us, event | category | flops | bytes accessed | tf_op | source)
XLA Modules:
  0.0 207.6 jit_solution(3756394883778191446)
XLA Ops:
  7.2 0.0 all-gather.2.cloned.1.call-start
  7.2 0.7 all-gather.2.cloned.1.call-update
  7.9 2.3 %copy.23.resid = bf16[1024,320]{1,0:T(8,128)(2,1)} copy(bf16[1024,320]{0,1:T(8,128)(2,1)} %param.11) | data formatting | bytes 1310720 | tf_op args[1]
  10.2 0.7 broadcast_in_dim.13
  10.9 0.1 broadcast_in_dim_reshape.3
  11.0 0.7 broadcast_in_dim.12
  11.7 0.7 broadcast_in_dim.14
  12.3 1.6 pad_maximum_fusion.weights
  13.9 63.1 %gather_all.1 = (bf16[8,1024,320]{2,1,0:T(8,128)(2,1)}, bf16[4,8,80,640]{3,2,1,0:T(8,128)(2,1)}, f32[16,320]{1,0:T(8,128)}) custom-call(bf16[1024,320]{1,0:T(8,128)(2,1)} %copy.23.resid, bf16[80,640]{1,0:T(8,128)(2,1)} %pad_maximum_fusion.weights, bf16[80,320]{1,0:T(8,128)(2,1)} %w_out.1, bf16[16,320]{1,0:T(8,128)(2,1)} %bitcast.13), custom_call_target="tpu_custom_call" | custom-call | flops 10000000000 | bytes 100000000 | tf_op jit(solution)/shard_map/gather_all/pallas_call | solution.py:241
  77.0 0.0 copy-start.2
  77.0 10.3 %project.1 = (bf16[1024,320]{1,0:T(8,128)(2,1)}, bf16[1024,320]{1,0:T(8,128)(2,1)}) custom-call(bf16[8,1024,320]{2,1,0:T(8,128)(2,1)} %get-tuple-element.23.left, bf16[2560,640]{1,0:T(8,128)(2,1)} %bitcast.11), custom_call_target="tpu_custom_call" | custom-call | tf_op jit(solution)/shard_map/project/pallas_call | solution.py:688
  87.3 0.0 copy-done.2
  87.3 0.6 concatenate.7.params
  87.9 33.1 %middle.1 = (bf16[1024,320]{1,0:T(8,128)(2,1)}, bf16[1024,320]{1,0:T(8,128)(2,1)}, f32[40,320]{1,0:T(8,128)}, bf16[1024,320]{1,0:T(8,128)(2,1)}, f32[8,24,128]{2,1,0:T(8,128)}) custom-call(bf16[1024,320]{1,0:T(8,128)(2,1)} %get-tuple-element.25.gate, bf16[1024,320]{1,0:T(8,128)(2,1)} %get-tuple-element.26.xs, bf16[1024,320]{1,0:T(8,128)(2,1)} %copy.23.resid, ...), custom_call_target="tpu_custom_call" | custom-call | flops 10000000000 | bytes 10000000 | tf_op jit(solution)/shard_map/middle/pallas_call | solution.py:487
  121.1 10.5 %stacked_outer.1 = bf16[8,320,640]{2,1,0:T(8,128)(2,1)} custom-call(bf16[8,1024,320]{2,1,0:T(8,128)(2,1)} %get-tuple-element.23.left, bf16[1024,320]{1,0:T(8,128)(2,1)} %get-tuple-element.28.dgate, bf16[1024,320]{1,0:T(8,128)(2,1)} %get-tuple-element.29.dx), custom_call_target="tpu_custom_call" | custom-call | tf_op jit(solution)/shard_map/stacked_outer/pallas_call | solution.py:757
  131.6 0.0 copy-start.1
  131.6 48.8 %finish_grads.1 = (f32[80,640]{1,0:T(8,128)}, f32[40,320]{1,0:T(8,128)}, f32[8,16,320]{2,1,0:T(8,128)}, bf16[8,1024,320]{2,1,0:T(8,128)(2,1)}) custom-call(bf16[4,8,80,640]{3,2,1,0:T(8,128)(2,1)} %bitcast.10, f32[40,320]{1,0:T(8,128)} %get-tuple-element.30.small, bf16[1024,320]{1,0:T(8,128)(2,1)} %get-tuple-element.31.gained), custom_call_target="tpu_custom_call" | custom-call | flops 10000000000 | bytes 100000000 | tf_op jit(solution)/shard_map/finish_grads/pallas_call | solution.py:638
  180.4 1.0 copy.26
  181.4 0.1 reshape.33
  181.5 1.3 slice.24
  182.8 1.4 slice_reduce_fusion
  184.2 0.1 reshape_squeeze.3
  184.3 0.6 reduce_sum.9
  184.9 0.0 copy-done.1
  184.9 1.0 fusion.1
  185.9 1.7 fusion.4
  187.6 0.0 all-gather.2.cloned.1.call-done.right
  187.6 0.0 copy-start
  187.6 8.7 %add_projected.1 = bf16[1024,320]{1,0:T(8,128)(2,1)} custom-call(bf16[8,1024,320]{2,1,0:T(8,128)(2,1)} %get-tuple-element.32.left, bf16[2560,320]{1,0:T(8,128)(2,1)} %all-gather.2.cloned.1.call-done.right, bf16[1024,320]{1,0:T(8,128)(2,1)} %copy.23.resid, f32[8,24,128]{2,1,0:T(8,128)} %get-tuple-element.33.facts), custom_call_target="tpu_custom_call" | custom-call | tf_op jit(solution)/shard_map/add_projected/pallas_call | solution.py:724
  196.3 2.2 %copy.27 = bf16[1024,320]{0,1:T(8,128)(2,1)} copy(bf16[1024,320]{1,0:T(8,128)(2,1)} %add_projected.1) | data formatting | bytes 1310720
  198.5 0.0 copy-done
  198.5 2.2 %fusion = f32[320,16]{0,1:T(8,128)} fusion(f32[16,2560]{1,0:T(8,128)S(1)} %reshape.33, bf16[2560,320]{1,0:T(8,128)(2,1)S(1)} %copy-done, f32[40,320]{1,0:T(8,128)} %get-tuple-element.36), kind=kOutput, calls=%fused_computation.1 | convolution fusion | flops 157291520 | bytes 1843200 | tf_op jit(solution)/shard_map/dot_general | solution.py:774
  (1 shorter events, 0.0 us)
Async XLA Ops:
  7.2 180.4 %all-gather.2.cloned.1.call-start = ((), (), s32[]{:S(2)}) async-start(), calls=%async_computation | async-start | bytes 2027520 | tf_op jit(solution)/shard_map/all_gather | solution.py:789
  77.0 10.3 %copy-start.2 = (f32[4,320]{1,0:T(4,128)S(1)}, f32[4,320]{1,0:T(4,128)}, u32[]{:S(2)}) copy-start(f32[4,320]{1,0:T(4,128)} %param.14) | copy-start | bytes 15364
  131.6 53.3 %copy-start.1 = (bf16[320,16]{0,1:T(8,128)(2,1)S(1)}, bf16[320,16]{0,1:T(8,128)(2,1)}, u32[]{:S(2)}) copy-start(bf16[320,16]{0,1:T(8,128)(2,1)} %param.19) | copy-start | bytes 30724
  187.6 10.9 %copy-start = (bf16[2560,320]{1,0:T(8,128)(2,1)S(1)}, bf16[2560,320]{1,0:T(8,128)(2,1)}, u32[]{:S(2)}) copy-start(bf16[2560,320]{1,0:T(8,128)(2,1)} %all-gather.2.cloned.1.call-done.right) | copy-start | bytes 4915204
Sparse Core Ops, SparseCore 0:
  10.6 79.1 all-gather.1

commit v4 on v3

--- a/solution.py
+++ b/solution.py
@@ -66,6 +66,7 @@
     lo, hi = pl.ds(0, rows // 2), pl.ds(rows // 2, rows // 2)
     to_right_lo = wire.put(shard.at[lo], full.at[c, lo], chan=right)
     to_left_hi = wire.put(shard.at[hi], full.at[c, hi], chan=left)
+    yield
     to_right_hi = wire.put(shard.at[hi], full.at[c, hi], chan=right)
     to_left_lo = wire.put(shard.at[lo], full.at[c, lo], chan=left)
     to_mate = [wire.put(shard, full.at[c], chan=mate)]
@@ -129,36 +130,53 @@
     )
 
 
-def ring_z_own(wire, shard, full, y, z, start, count):
-    cut = (count // 32) * 16
-    yield from ring_z(
-        wire,
-        shard.at[pl.ds(start, count)],
-        lambda at: full.at[y, at, pl.ds(start, count)],
-        lambda at: (
-            full.at[y, at, pl.ds(start, cut)],
-            full.at[y, at, pl.ds(start + cut, count - cut)],
-        ),
-        y,
-        z,
-    )
-
-
-def exchange_y_lines(wire, full, y, z, rows):
+def gather_z_then_y(wire, shard, full, y, z, rows):
     above, below = lax.rem(y + 1, NY), lax.rem(y + NY - 1, NY)
-    up, down = above * NZ + z, below * NZ + z
-    lo, hi = pl.ds(0, NZ // 2), pl.ds(NZ // 2, NZ // 2)
-    up_lo = wire.put(full.at[y, lo, rows], full.at[y, lo, rows], seq=up)
-    down_hi = wire.put(full.at[y, hi, rows], full.at[y, hi, rows], seq=down)
-    up_hi = wire.put(full.at[y, hi, rows], full.at[y, hi, rows], seq=up)
-    down_lo = wire.put(full.at[y, lo, rows], full.at[y, lo, rows], seq=down)
-    yield
-    up_lo.wait_recv()
-    on_up = wire.put(full.at[below, lo, rows], full.at[below, lo, rows], seq=up)
-    down_hi.wait_recv()
-    on_down = wire.put(full.at[above, hi, rows], full.at[above, hi, rows], seq=down)
-    yield
-    for copy in (up_hi, down_lo, on_up, on_down):
+    y_up, y_down = above * NZ + z, below * NZ + z
+    z_up, z_down = y * NZ + lax.rem(z + 1, NZ), y * NZ + lax.rem(z + NZ - 1, NZ)
+    waiting, rest = [], []
+
+    def spread(source, at, upward):
+        block = full.at[y, at, rows]
+        up, down = wire.put(source, block, seq=y_up), wire.put(source, block, seq=y_down)
+        waiting.append((up, down, at, upward))
+
+    def pass_on(count):
+        for up, down, at, upward in waiting[:count]:
+            if upward:
+                up.wait_recv()
+                block = full.at[below, at, rows]
+                rest.extend([down, wire.put(block, block, seq=y_up)])
+            else:
+                down.wait_recv()
+                block = full.at[above, at, rows]
+                rest.extend([up, wire.put(block, block, seq=y_down)])
+        del waiting[:count]
+
+    own = full.at[y, z, rows]
+    plus, minus = wire.put(shard.at[rows], own, seq=z_up), wire.put(shard.at[rows], own, seq=z_down)
+    spread(shard.at[rows], z, True)
+    for step in range(1, NZ // 2 + 1):
+        yield
+        before = len(waiting)
+        behind = lax.rem(z + NZ - step, NZ)
+        plus.wait_recv()
+        block = full.at[y, behind, rows]
+        if step < NZ // 2:
+            plus = wire.put(block, block, seq=z_up)
+        spread(block, behind, step < NZ // 2)
+        if step < NZ // 2:
+            ahead = lax.rem(z + step, NZ)
+            minus.wait_recv()
+            block = full.at[y, ahead, rows]
+            if step < NZ // 2 - 1:
+                minus = wire.put(block, block, seq=z_down)
+            spread(block, ahead, False)
+        pass_on(before)
+    yield
+    pass_on(len(waiting))
+    yield
+    for copy in rest:
         copy.wait_recv()
 
 
@@ -202,10 +220,13 @@
 
 
 def gather_kernel(
-    resid, weights, w_out, w_head, full_resid, full_weights, mix, *scratch
+    resid, w_gate, w_x, w_out, w_head, full_resid, full_weights, mix, weights, *scratch
 ):
     *mix_bufs, send, recv, local = scratch
     y, z, c = place()
+    half = w_gate.shape[1]
+    weights[:, pl.ds(0, half)] = w_gate[...]
+    weights[:, pl.ds(half, half)] = w_x[...]
     greet(
         [{"chan": lax.rem(c + d, NCHAN)} for d in range(1, NCHAN)]
         + [{"seq": lax.rem(y + d, NY) * NZ + z} for d in range(1, NY)]
@@ -218,37 +239,38 @@
     own_resid.start()
     rows, first = weights.shape[0], 32
     one, rest = pl.ds(0, first), pl.ds(first, rows - first)
-    b_ring = ring_z_own(wire, weights, full_weights, y, z, first, rows - first)
-    b_lines = exchange_y_lines(wire, full_weights, y, z, rest)
-    a_own = exchange_y(wire, weights, full_weights, y, z, one)
-    a_ring = ring_z_columns(wire, full_weights, y, z, one)
+    lines = gather_z_then_y(wire, weights, full_weights, y, z, rest)
+    own_y = exchange_y(wire, weights, full_weights, y, z, one)
+    columns = ring_z_columns(wire, full_weights, y, z, one)
     chans = gather_chan(wire, resid, full_resid, c, resid.shape[0])
     mixes = gather_mix(wire, w_out, w_head, mix, mix_bufs, y, z, c)
-    in_order(b_ring, a_own, chans, mixes, b_ring, a_own, mixes, b_ring, mixes, b_ring)
+    in_order(own_y, lines, chans, mixes, own_y)
     own_weights.wait()
-    in_order(b_ring, b_lines, a_ring, mixes, chans, a_ring, chans, a_ring, b_lines)
-    in_order(a_ring, chans, a_ring, b_lines, chans)
+    in_order(columns, lines, chans, mixes, lines, columns, mixes, lines, chans)
+    in_order(columns, lines, mixes, columns, chans, columns, lines, lines, chans, chans)
     own_resid.wait()
     wire.finish()
 
 
-def gather_all(resid, weights, w_out, w_head):
+def gather_all(resid, w_gate, w_x, w_out, w_head):
     anywhere = pl.BlockSpec(memory_space=pl.ANY)
     vmem = pl.BlockSpec(memory_space=pltpu.VMEM)
     f32 = jnp.float32
-    copies = 64
+    copies = 96
     block = (VOCAB, 128)
+    rows, half = w_gate.shape
     return pl.pallas_call(
         gather_kernel,
         name="gather_all",
         out_shape=(
             jax.ShapeDtypeStruct((NCHAN, *resid.shape), resid.dtype),
-            jax.ShapeDtypeStruct((NY, NZ, *weights.shape), weights.dtype),
-            jax.ShapeDtypeStruct((VOCAB, resid.shape[1]), f32),
+            jax.ShapeDtypeStruct((NY, NZ, rows, 2 * half), w_gate.dtype),
+            jax.ShapeDtypeStruct((VOCAB, resid.shape[0]), f32),
         ),
-        in_specs=[anywhere] * 2 + [vmem] * 2,
+        in_specs=[anywhere] + [vmem] * 4,
         out_specs=(anywhere, anywhere, vmem),
         scratch_shapes=[
+            pltpu.VMEM((rows, 2 * half), w_gate.dtype),
             pltpu.VMEM(block, f32),
             pltpu.VMEM((NCHAN - 1, *block), f32),
             pltpu.VMEM(block, f32),
@@ -260,7 +282,7 @@
         ],
         compiler_params=pltpu.CompilerParams(collective_id=0, has_side_effects=True),
         cost_estimate=pl.CostEstimate(flops=10**10, bytes_accessed=10**8, transcendentals=0),
-    )(resid, weights, w_out, w_head)
+    )(resid, w_gate, w_x, w_out, w_head)
 
 
 EXACT = lax.Precision.HIGHEST
@@ -278,11 +300,13 @@
     mix_t,
     params,
     targets,
+    w_out,
     dgate,
     dx,
     small,
     gained,
     facts,
+    full_w_out,
     padded,
     prods,
     to_gate,
@@ -296,6 +320,9 @@
     acc_heads,
     send,
     recv,
+    w_send,
+    w_recv,
+    local,
 ):
     f32, bf16 = jnp.float32, jnp.bfloat16
     tokens = gate.shape[0]
@@ -306,7 +333,13 @@
     greet(
         [{"chan": lax.rem(c + d, NCHAN)} for d in range(1, NCHAN)]
         + [{"seq": later}, {"seq": sooner}]
-    )
+        + [{"seq": lax.rem(y + d, NY) * NZ + z} for d in range(1, NY)]
+        + [{"seq": y * NZ + lax.rem(z + d, NZ)} for d in (1, NZ - 1)]
+    )
+    wire = Wire(w_send, w_recv)
+    whole = pl.ds(0, w_out.shape[0])
+    own_w_out = pltpu.make_async_copy(w_out, full_w_out.at[y, z], local.at[0])
+    own_w_out.start()
 
     def copy_of(source, target, at, where):
         return pltpu.make_async_remote_copy(
@@ -320,6 +353,9 @@
 
     edge = copy_of(xs.at[pl.ds(tokens - EDGE, EDGE)], before, 2 * NCHAN, {"seq": later})
     edge.start()
+    own_y = exchange_y(wire, w_out, full_w_out, y, z, whole)
+    columns = ring_z_columns(wire, full_w_out, y, z, whole)
+    in_order(own_y)
     taps = [params[k : k + 1, :] for k in range(KERNEL)]
     bias, skip, gain = params[4:5, :], params[5:6, :], params[6:7, :]
     mix = mix_t[...]
@@ -353,10 +389,13 @@
         to_conv[rows, :] = skip * silu_gate * slope(conv, sig_conv)
         gated = prod * skip
         with_gain = gated * gain
-        gained[rows, :] = with_gain.astype(bf16)
+        gained[:, rows] = with_gain.T.astype(bf16)
         by_lanes = (((1,), (1,)), ((), ()))
         sums[tile, pl.ds(0, VOCAB)] = lax.dot_general(
-            head_t[...], resid[rows, :], by_lanes, preferred_element_type=f32
+            head_t[...],
+            resid[:, rows],
+            (((1,), (0,)), ((), ())),
+            preferred_element_type=f32,
         )
         sums[tile, pl.ds(VOCAB, VOCAB)] = lax.dot_general(
             mix, with_gain, by_lanes, precision=EXACT, preferred_element_type=f32
@@ -370,6 +409,8 @@
         )
 
     edge.wait_recv()
+    own_w_out.wait()
+    in_order(own_y, columns)
     padded[pl.ds(0, EDGE), :] = before[...].astype(f32) * (s > 0).astype(f32)
 
     def forward_step(step, carry):
@@ -379,6 +420,7 @@
 
     lax.fori_loop(0, NCHAN - 1, forward_step, 0)
     forward(c)
+    in_order(columns)
     total = sums[c]
     for step in range(NCHAN - 1):
         share(step).wait_recv()
@@ -410,6 +452,7 @@
     acc_heads[...] = jnp.zeros_like(acc_heads)
     for d in range(1, NCHAN):
         tell(d).wait_recv()
+    in_order(columns)
     second = (
         lax.broadcasted_iota(jnp.int32, (8, mix.shape[1]), 0) == 1
     ).astype(f32)
@@ -439,8 +482,12 @@
         acc_rows[KERNEL] += fold(dconv)
         acc_rows[KERNEL + 1] += fold(dgated * prod)
         acc_heads[0] += jnp.dot(scaled, prod, precision=EXACT, preferred_element_type=f32)
-        acc_heads[1] += jnp.dot(
-            dlogit, resid[rows, :].astype(f32), precision=EXACT, preferred_element_type=f32
+        acc_heads[1] += lax.dot_general(
+            dlogit,
+            resid[:, rows].astype(f32),
+            (((1,), (1,)), ((), ())),
+            precision=EXACT,
+            preferred_element_type=f32,
         )
 
     backward(0)
@@ -452,6 +499,7 @@
         return carry
 
     lax.fori_loop(1, tokens // LANES, backward_step, 0)
+    in_order(columns)
     by_channel = acc_heads[0]
     small[pl.ds(0, VOCAB), :] = by_channel * skip * gain
     small[pl.ds(VOCAB, VOCAB), :] = acc_heads[1]
@@ -472,6 +520,8 @@
         return carry
 
     lax.fori_loop(0, tokens // LANES, spread_step, 0)
+    in_order(columns)
+    wire.finish()
     edge.wait_send()
     first_rows.wait_send()
     for d in range(1, NCHAN):
@@ -479,9 +529,10 @@
         tell(d).wait_send()
 
 
-def middle(gate, xs, resid, head_t, mix_t, params, targets):
+def middle(gate, xs, resid, head_t, mix_t, params, targets, w_out):
     f32, bf16 = jnp.float32, jnp.bfloat16
     vmem = pl.BlockSpec(memory_space=pltpu.VMEM)
+    anywhere = pl.BlockSpec(memory_space=pl.ANY)
     tokens, width = gate.shape
     copies = 2 * NCHAN + 2
     return pl.pallas_call(
@@ -491,11 +542,12 @@
             jax.ShapeDtypeStruct((tokens, width), bf16),
             jax.ShapeDtypeStruct((tokens, width), bf16),
             jax.ShapeDtypeStruct((SUMS, width), f32),
-            jax.ShapeDtypeStruct((tokens, width), bf16),
+            jax.ShapeDtypeStruct((width, tokens), bf16),
             jax.ShapeDtypeStruct((NCHAN, FACTS, LANES), f32),
+            jax.ShapeDtypeStruct((NY, NZ, *w_out.shape), bf16),
         ),
-        in_specs=[vmem] * 7,
-        out_specs=(vmem,) * 5,
+        in_specs=[vmem] * 7 + [anywhere],
+        out_specs=(vmem,) * 5 + (anywhere,),
         scratch_shapes=[
             pltpu.VMEM((tokens + EDGE, width), f32),
             pltpu.VMEM((tokens, width), f32),
@@ -510,27 +562,34 @@
             pltpu.VMEM((2, VOCAB, width), f32),
             pltpu.SemaphoreType.DMA((copies,)),
             pltpu.SemaphoreType.DMA((copies,)),
+            pltpu.SemaphoreType.DMA((NY + NZ,)),
+            pltpu.SemaphoreType.DMA((NY + NZ,)),
+            pltpu.SemaphoreType.DMA((1,)),
         ],
         compiler_params=pltpu.CompilerParams(
             collective_id=1, has_side_effects=True, vmem_limit_bytes=VMEM_BYTES
         ),
         cost_estimate=pl.CostEstimate(flops=10**10, bytes_accessed=10**7, transcendentals=0),
-    )(gate, xs, resid, head_t, mix_t, params, targets)
-
-
-def scatter_seq(wire, grads, bufs, out, y, z, start, count):
+    )(gate, xs, resid, head_t, mix_t, params, targets, w_out)
+
+
+def scatter_seq(wire, grads, ready, bufs, outs, y, z, start, count):
     f32, bf16 = jnp.float32, jnp.bfloat16
     from_below, from_above, via_up, via_down, got_below, got_above, lines, got_z = bufs
     rows = pl.ds(start, count)
     lo, hi = pl.ds(0, NZ // 2), pl.ds(NZ // 2, NZ // 2)
     above, below, across = lax.rem(y + 1, NY), lax.rem(y + 3, NY), lax.rem(y + 2, NY)
     up, down = above * NZ + z, below * NZ + z
+    ready(2 * across)
     half_up = wire.put(grads.at[across, lo, rows], from_below.at[:, rows], seq=up)
+    ready(2 * across + 1)
     half_down = wire.put(grads.at[across, hi, rows], from_above.at[:, rows], seq=down)
-    moves = [
-        wire.put(grads.at[above, hi, rows], got_below.at[hi, rows], seq=up),
-        wire.put(grads.at[below, lo, rows], got_above.at[lo, rows], seq=down),
-    ]
+    ready(2 * above + 1)
+    moves = [wire.put(grads.at[above, hi, rows], got_below.at[hi, rows], seq=up)]
+    ready(2 * below)
+    moves.append(wire.put(grads.at[below, lo, rows], got_above.at[lo, rows], seq=down))
+    ready(2 * above)
+    ready(2 * below + 1)
     yield
     half_up.wait_recv()
     via_up[:, rows] = (
@@ -542,6 +601,8 @@
         grads[below, hi, rows].astype(f32) + from_above[:, rows].astype(f32)
     ).astype(bf16)
     moves.append(wire.put(via_down.at[:, rows], got_above.at[hi, rows], seq=down))
+    ready(2 * y)
+    ready(2 * y + 1)
     yield
     for copy in moves[:2]:
         copy.wait_recv()
@@ -566,7 +627,9 @@
     for d in range(1, NZ):
         puts[d - 1].wait_recv()
         acc = acc + got_z[d - 1, rows].astype(f32)
-    out[rows] = acc
+    half = acc.shape[1] // 2
+    outs[0][rows] = acc[:, :half]
+    outs[1][rows] = acc[:, half:]
 
 
 def sum_small(wire, small, got_y, part, got_z, total, heads, y, z, c):
@@ -604,49 +667,150 @@
 
 
 def grads_kernel(
-    grads, small, gained, out, total, heads, full_gained, *scratch
+    features,
+    dgate,
+    dx,
+    small,
+    gained,
+    w_out,
+    resid,
+    facts,
+    head_t,
+    grad_gate,
+    grad_x,
+    total,
+    grad_out,
+    grad_head,
+    new_resid,
+    *scratch,
 ):
-    *bufs, small_y, small_part, small_z, send, recv, local = scratch
+    f32, bf16 = jnp.float32, jnp.bfloat16
+    feats, both, grads, full_gained, out_cols, heads, *rest = scratch
+    *bufs, small_y, small_part, small_z, send, recv, local = rest
     y, z, c = place()
+    width = dgate.shape[1]
+    order = [
+        2 * lax.rem(y + 2, NY),
+        2 * lax.rem(y + 2, NY) + 1,
+        2 * lax.rem(y + 1, NY) + 1,
+        2 * lax.rem(y + 3, NY),
+        2 * lax.rem(y + 1, NY),
+        2 * lax.rem(y + 3, NY) + 1,
+        2 * y,
+        2 * y + 1,
+    ]
+    loads = [
+        pltpu.make_async_copy(features.at[at], feats.at[step], local.at[step])
+        for step, at in enumerate(order)
+    ]
+    for load in loads:
+        load.start()
+    own = pltpu.make_async_copy(gained, full_gained.at[c], local.at[NCHAN])
+    own.start()
+    weights = pltpu.make_async_copy(w_out, out_cols, local.at[NCHAN + 1])
+    weights.start()
+    both[:, pl.ds(0, width)] = dgate[...]
+    both[:, pl.ds(width, width)] = dx[...]
     greet(
         [{"chan": lax.rem(c + d, NCHAN)} for d in range(1, NCHAN)]
         + [{"seq": lax.rem(y + d, NY) * NZ + z} for d in range(1, NY)]
         + [{"seq": y * NZ + lax.rem(z + d, NZ)} for d in range(1, NZ)]
     )
     wire = Wire(send, recv)
-    own = pltpu.make_async_copy(gained, full_gained.at[c], local.at[0])
-    own.start()
-    rows = out.shape[0]
+    steps = iter(range(NCHAN))
+
+    def ready(block):
+        step = next(steps)
+        loads[step].wait()
+        product = jnp.dot(feats[step], both[...], preferred_element_type=f32)
+        lines = product.reshape(NZ // 2, product.shape[0] // (NZ // 2), product.shape[1])
+        first = lax.rem(block, 2) * (NZ // 2)
+        grads[block // 2, pl.ds(first, NZ // 2)] = lines.astype(bf16)
+
+    rows = grad_gate.shape[0]
+    outs = (grad_gate, grad_x)
     smalls = sum_small(wire, small, small_y, small_part, small_z, total, heads, y, z, c)
-    one = scatter_seq(wire, grads, bufs, out, y, z, 0, 48)
-    two = scatter_seq(wire, grads, bufs, out, y, z, 48, rows - 48)
+    one = scatter_seq(wire, grads, ready, bufs, outs, y, z, 0, 48)
+    two = scatter_seq(wire, grads, lambda block: None, bufs, outs, y, z, 48, rows - 48)
     chans = gather_chan(wire, gained, full_gained, c, gained.shape[0])
-    in_order(smalls, one, chans, smalls, one, chans, one, two, one)
-    in_order(smalls, chans, two, two, two, chans, smalls, one, two, chans)
+    in_order(smalls, chans, one, chans, smalls, one, chans, one, two, one, chans)
+    in_order(two, smalls, two, two, chans, smalls, chans)
     own.wait()
+    weights.wait()
+
+    def project_back(step, carry):
+        cols = pl.ds(pl.multiple_of(step * 256, 256), 256)
+        acc = 0.0
+        for at in range(NCHAN):
+            acc = acc + lax.dot_general(
+                out_cols[at], full_gained[at, :, cols], BY_ROWS, preferred_element_type=f32
+            )
+        for at in range(2):
+            tile = 2 * step + at
+            lanes = pl.ds(pl.multiple_of(tile * LANES, LANES), LANES)
+            scale = facts[tile, VOCAB : VOCAB + 1]
+            summed = resid[:, lanes].astype(f32) + scale * acc[:, at * LANES : (at + 1) * LANES]
+            new_resid[:, lanes] = summed.astype(bf16)
+        return carry
+
+    lax.fori_loop(0, new_resid.shape[1] // 256, project_back, 0)
+    acc = 0.0
+    for at in range(NCHAN):
+        head = heads[at]
+        high = head.astype(bf16)
+        low = (head - high.astype(f32)).astype(bf16)
+        acc = acc + jnp.dot(
+            jnp.concatenate([high, low], axis=0), out_cols[at], preferred_element_type=f32
+        )
+    grad_head[...] = total[pl.ds(VOCAB, VOCAB), :] + acc[:VOCAB] + acc[VOCAB:]
+    s = y * NZ + z
+    per_chan = width // rows
+    mine = heads[s // per_chan]
+    here = jnp.zeros((VOCAB, rows), f32)
+    for at in range(per_chan):
+        chosen = (lax.rem(s, per_chan) == at).astype(f32)
+        here = here + chosen * mine[:, at * rows : (at + 1) * rows]
+    grad_out[...] = lax.dot_general(
+        here, head_t[...].astype(f32), BY_ROWS, precision=EXACT, preferred_element_type=f32
+    )
+    in_order(one, two)
     wire.finish()
 
 
-def finish_grads(grads, small, gained):
+def finish_grads(features, dgate, dx, small, gained, w_out, resid, facts, head_t):
     f32, bf16 = jnp.float32, jnp.bfloat16
     anywhere = pl.BlockSpec(memory_space=pl.ANY)
     vmem = pl.BlockSpec(memory_space=pltpu.VMEM)
-    _, _, rows, cols = grads.shape
-    copies = 64
+    tokens, width = dgate.shape
+    _, depth, _ = w_out.shape
+    rows = INNER // (NY * NZ)
+    copies = 80
+    cols = 2 * width
     half = (NZ // 2, rows, cols)
     line = (NZ, rows, cols)
+    block = jax.ShapeDtypeStruct((rows, width), f32)
     return pl.pallas_call(
         grads_kernel,
         name="finish_grads",
         out_shape=(
-            jax.ShapeDtypeStruct((rows, cols), f32),
+            block,
+            block,
             jax.ShapeDtypeStruct(small.shape, f32),
-            jax.ShapeDtypeStruct((NCHAN, VOCAB, small.shape[1]), f32),
-            jax.ShapeDtypeStruct((NCHAN, *gained.shape), bf16),
+            block,
+            jax.ShapeDtypeStruct((VOCAB, width), f32),
+            jax.ShapeDtypeStruct(resid.shape, bf16),
         ),
-        in_specs=[vmem, vmem, anywhere],
-        out_specs=(vmem, vmem, vmem, anywhere),
-        scratch_shapes=[pltpu.VMEM(half, bf16)] * 4
+        in_specs=[anywhere, vmem, vmem, vmem, anywhere, anywhere, vmem, vmem, vmem],
+        out_specs=(vmem,) * 6,
+        scratch_shapes=[
+            pltpu.VMEM(features.shape, bf16),
+            pltpu.VMEM((tokens, cols), bf16),
+            pltpu.VMEM((NY, NZ, rows, cols), bf16),
+            pltpu.VMEM((NCHAN, *gained.shape), bf16),
+            pltpu.VMEM(w_out.shape, bf16),
+            pltpu.VMEM((NCHAN, VOCAB, width), f32),
+        ]
+        + [pltpu.VMEM(half, bf16)] * 4
         + [pltpu.VMEM(line, bf16)] * 3
         + [
             pltpu.VMEM((NZ - 1, rows, cols), bf16),
@@ -655,21 +819,23 @@
             pltpu.VMEM((NZ, *small.shape), f32),
             pltpu.SemaphoreType.DMA((copies,)),
             pltpu.SemaphoreType.DMA((copies,)),
-            pltpu.SemaphoreType.DMA((1,)),
+            pltpu.SemaphoreType.DMA((NCHAN + 2,)),
         ],
         compiler_params=pltpu.CompilerParams(
             collective_id=2, has_side_effects=True, vmem_limit_bytes=VMEM_BYTES
         ),
         cost_estimate=pl.CostEstimate(flops=10**10, bytes_accessed=10**8, transcendentals=0),
-    )(grads, small, gained)
+    )(features, dgate, dx, small, gained, w_out, resid, facts, head_t)
+
+
+BY_ROWS = (((0,), (0,)), ((), ()))
 
 
 def sum_of_dots(left, right):
-    depth = left.shape[2]
-    acc = jnp.dot(left[0], right[pl.ds(0, depth), :], preferred_element_type=jnp.float32)
-    for at in range(1, left.shape[0]):
-        acc = acc + jnp.dot(
-            left[at], right[pl.ds(at * depth, depth), :], preferred_element_type=jnp.float32
+    acc = 0.0
+    for at in range(left.shape[0]):
+        acc = acc + lax.dot_general(
+            left[at], right[at], BY_ROWS, preferred_element_type=jnp.float32
         )
     return acc
 
@@ -682,8 +848,8 @@
 
 
 def project(left, right):
-    parts, tokens, depth = left.shape
-    tile, width = 256, right.shape[1] // 2
+    parts, depth, tokens = left.shape
+    tile, width = 256, right.shape[2] // 2
     half = pl.BlockSpec((tile, width), lambda i: (i, 0))
     return pl.pallas_call(
         project_kernel,
@@ -691,93 +857,16 @@
         grid=(tokens // tile,),
         out_shape=(jax.ShapeDtypeStruct((tokens, width), jnp.bfloat16),) * 2,
         in_specs=[
-            pl.BlockSpec((parts, tile, depth), lambda i: (0, i, 0)),
-            pl.BlockSpec(right.shape, lambda i: (0, 0), pipeline_mode=pl.Buffered(1)),
+            pl.BlockSpec((parts, depth, tile), lambda i: (0, 0, i)),
+            pl.BlockSpec(right.shape, lambda i: (0, 0, 0), pipeline_mode=pl.Buffered(1)),
         ],
         out_specs=(half, half),
         compiler_params=pltpu.CompilerParams(vmem_limit_bytes=VMEM_BYTES),
     )(left, right)
 
 
-def residual_kernel(left, right, resid, facts, out):
-    acc = sum_of_dots(left, right)
-    inverse = (
-        lax.broadcasted_iota(jnp.int32, (8, out.shape[1]), 0) == 0
-    ).astype(jnp.float32)
-    for at in range(facts.shape[0]):
-        rows = pl.ds(at * LANES, LANES)
-        scale = lax.dot_general(
-            facts[at, pl.ds(VOCAB, 8)],
-            inverse,
-            (((0,), (0,)), ((), ())),
-            precision=EXACT,
-            preferred_element_type=jnp.float32,
-        )
-        summed = resid[rows, :].astype(jnp.float32) + scale * acc[at * LANES : at * LANES + LANES]
-        out[rows, :] = summed.astype(out.dtype)
-
-
-def add_projected(left, right, resid, facts):
-    parts, tokens, depth = left.shape
-    tile, width = 256, right.shape[1]
-    rows = pl.BlockSpec((tile, width), lambda i: (i, 0))
-    return pl.pallas_call(
-        residual_kernel,
-        name="add_projected",
-        grid=(tokens // tile,),
-        out_shape=jax.ShapeDtypeStruct((tokens, width), jnp.bfloat16),
-        in_specs=[
-            pl.BlockSpec((parts, tile, depth), lambda i: (0, i, 0)),
-            pl.BlockSpec(right.shape, lambda i: (0, 0), pipeline_mode=pl.Buffered(1)),
-            rows,
-            pl.BlockSpec((tile // LANES, FACTS, LANES), lambda i: (i, 0, 0)),
-        ],
-        out_specs=rows,
-        compiler_params=pltpu.CompilerParams(vmem_limit_bytes=VMEM_BYTES),
-    )(left, right, resid, facts)
-
-
-def outer_kernel(left, dgate, dx, out, both):
-    width = dgate.shape[1]
-
-    @pl.when(pl.program_id(0) == 0)
-    def _():
-        both[:, pl.ds(0, width)] = dgate[...]
-        both[:, pl.ds(width, width)] = dx[...]
-
-    out[0] = lax.dot_general(
-        left[0], both[...], (((0,), (0,)), ((), ())), preferred_element_type=jnp.float32
-    ).astype(out.dtype)
-
-
-def stacked_outer(left, dgate, dx):
-    parts, tokens, depth = left.shape
-    width = 2 * dgate.shape[1]
-    whole = pl.BlockSpec(dgate.shape, lambda i: (0, 0), pipeline_mode=pl.Buffered(1))
-    return pl.pallas_call(
-        outer_kernel,
-        name="stacked_outer",
-        grid=(parts,),
-        out_shape=jax.ShapeDtypeStruct((parts, depth, width), jnp.bfloat16),
-        in_specs=[pl.BlockSpec((1, tokens, depth), lambda i: (i, 0, 0)), whole, whole],
-        out_specs=pl.BlockSpec((1, depth, width), lambda i: (i, 0, 0)),
-        scratch_shapes=[pltpu.VMEM((tokens, width), jnp.bfloat16)],
-        compiler_params=pltpu.CompilerParams(vmem_limit_bytes=VMEM_BYTES),
-    )(left, dgate, dx)
-
-
 def slope(value, sig):
     return sig * (1.0 + value * (1.0 - sig))
-
-
-def inner_rows(left, right, precision=None):
-    return lax.dot_general(
-        left,
-        right,
-        (((0,), (0,)), ((), ())),
-        preferred_element_type=jnp.float32,
-        precision=precision,
-    )
 
 
 def per_device(
@@ -785,13 +874,9 @@
 ):
     f32 = jnp.float32
     local_inner = w_gate_in.shape[1]
-    row_count = w_out.shape[0]
-    out_cols = lax.all_gather(w_out, "seq", axis=0, tiled=True)
-    head_t = w_head.T
-    features, full, mix_t = gather_all(
-        resid, jnp.concatenate([w_gate_in, w_x_in], axis=1), w_out, head_t
-    )
-    gate_pre, x_pre = project(features, full.reshape(INNER, 2 * local_inner))
+    head_t, resid_t = w_head.T, resid.T
+    features, full, mix_t = gather_all(resid_t, w_gate_in, w_x_in, w_out, head_t)
+    gate_pre, x_pre = project(features, full.reshape(NCHAN, local_inner, 2 * local_inner))
     params = jnp.concatenate(
         [
             conv_weight,
@@ -802,33 +887,38 @@
         ],
         axis=0,
     )
-    dgate, dx_pre, small, gained, facts = middle(
-        gate_pre, x_pre, resid, head_t, mix_t, params, targets.reshape(NCHAN, 1, LANES)
-    )
-    grads = stacked_outer(features, dgate, dx_pre).reshape(NY, NZ, row_count, 2 * local_inner)
-    grad_both, total, mix_grads, full_gained = finish_grads(grads, small, gained)
-    grad_gate_in = grad_both[:, :local_inner]
-    grad_x_in = grad_both[:, local_inner:]
+    dgate, dx_pre, small, gained, facts, out_cols = middle(
+        gate_pre,
+        x_pre,
+        resid_t,
+        head_t,
+        mix_t,
+        params,
+        targets.reshape(NCHAN, 1, LANES),
+        w_out,
+    )
+    grad_gate_in, grad_x_in, total, grad_out, grad_head_t, new_resid_t = finish_grads(
+        features,
+        dgate,
+        dx_pre,
+        small,
+        gained,
+        out_cols.reshape(NCHAN, local_inner, local_inner),
+        resid_t,
+        facts,
+        head_t,
+    )
     at = 2 * VOCAB
     grad_conv_weight = total[at : at + KERNEL]
     grad_conv_bias = total[at + KERNEL]
     grad_gain = total[at + KERNEL + 1]
     grad_skip = total[at + KERNEL + 2].reshape(-1, HEADDIM).sum(axis=1)
-    new_resid = add_projected(full_gained, out_cols, resid, facts)
-    mix_grads = mix_grads.transpose(1, 0, 2).reshape(VOCAB, INNER)
-    grad_head = total[VOCAB : 2 * VOCAB].T + inner_rows(
-        out_cols.astype(f32), mix_grads.T, EXACT
-    )
-    mix_grad_rows = lax.dynamic_slice_in_dim(
-        mix_grads, lax.axis_index("seq") * row_count, row_count, 1
-    )
-    grad_out = inner_rows(mix_grad_rows, w_head.astype(f32).T, EXACT)
     return (
-        new_resid,
+        new_resid_t.T,
         grad_gate_in,
         grad_x_in,
         grad_out,
-        grad_head,
+        grad_head_t.T,
         grad_conv_weight,
         grad_conv_bias,
         grad_skip,

time: 208 us -> 161 us (0.77)
  Pallas kernels: 174 us -> 143 us
  between operations: 14.1 us -> 0.67 us
  matrix products: 3.21 us -> 0 us
    pallas_call x3 -> x1, Pallas kernels: 68 us -> 48.2 us  [finish_grads(): pl.pallas_call(grads_kernel, name='finish_grads', out_shape=(block, block...]
    pallas_call x1, Pallas kernels: 63.1 us -> 48.1 us  [gather_all(): pl.pallas_call(gather_kernel, name='gather_all', out_shape=(jax.ShapeDtyp...]
    pallas_call x1, Pallas kernels: 33.1 us -> 36.8 us  [middle(): pl.pallas_call(middle_kernel, name='middle', out_shape=(jax.ShapeDtypeStr...]
    unnamed x8 -> x5, local copies, waits for them, and re-layouts: 4.49 us -> 7.98 us
    dot_general x2 -> x0, matrix products: 3.21 us -> none  [inner_rows(): lax.dot_general(left, right, (((0,), (0,)), ((), ())), preferred_element_...]
  transfers between devices with their start and end apart: 1 -> 0, of which waited for: 0 -> 0; matrix products, arithmetic and copies ran while one was open for 7% -> 0% of each run, Pallas kernels for 80% -> 0%
where the time goes in v4:
time: 161 us; the launch traced here: 159 us
  Pallas kernels  143 us (89%)
  local copies, waits for them, and re-layouts  14.3 us (9%)
    pallas_call x1, Pallas kernels, finish_grads(): pl.pallas_call(grads_kernel, name='finish_grads', out_shape=(block, block...  48.2 us
    pallas_call x1, Pallas kernels, gather_all(): pl.pallas_call(gather_kernel, name='gather_all', out_shape=(jax.ShapeDtyp...  48.1 us
    pallas_call x1, Pallas kernels, middle(): pl.pallas_call(middle_kernel, name='middle', out_shape=(jax.ShapeDtypeStr...  36.8 us
    pallas_call x1, Pallas kernels, project(): pl.pallas_call(project_kernel, name='project', grid=(tokens // tile,), ou...  10.2 us
    unnamed x5, local copies, waits for them, and re-layouts  7.98 us

profile of v4, /device:TPU:1, one launch (start us, length us, event | category | flops | bytes accessed | tf_op | source)
XLA Modules:
  0.0 158.8 jit_solution(8462473371732967467)
XLA Ops:
  0.6 0.7 broadcast_in_dim.12
  1.3 0.7 broadcast_in_dim.14
  2.0 0.7 broadcast_in_dim.13
  2.7 0.1 broadcast_in_dim_reshape.3
  2.8 1.3 concatenate.3.params
  4.1 48.1 %gather_all.1 = (bf16[8,320,1024]{2,1,0:T(8,128)(2,1)}, bf16[4,8,80,640]{3,2,1,0:T(8,128)(2,1)}, f32[16,320]{1,0:T(8,128)}) custom-call(bf16[320,1024]{1,0:T(8,128)(2,1)} %bitcast.10, bf16[80,320]{1,0:T(8,128)(2,1)} %w_gate.1, bf16[80,320]{1,0:T(8,128)(2,1)} %w_x.1, bf16[80,320]{1,0:T(8,128)(2,1)} %w_out.3, bf16[16,320]{1,0:T(8,128)(2,1)} %bitcast.13), custom_call_target="tpu_custom_call" | custom-call | flops 10000000000 | bytes 100000000 | tf_op jit(solution)/shard_map/gather_all/pallas_call | solution.py:262
  52.2 10.2 %project.1 = (bf16[1024,320]{1,0:T(8,128)(2,1)}, bf16[1024,320]{1,0:T(8,128)(2,1)}) custom-call(bf16[8,320,1024]{2,1,0:T(8,128)(2,1)} %get-tuple-element.26.left.features, bf16[8,320,640]{2,1,0:T(8,128)(2,1)} %bitcast.7), custom_call_target="tpu_custom_call" | custom-call | tf_op jit(solution)/shard_map/project/pallas_call | solution.py:854
  62.5 36.8 %middle.1 = (bf16[1024,320]{1,0:T(8,128)(2,1)}, bf16[1024,320]{1,0:T(8,128)(2,1)}, f32[40,320]{1,0:T(8,128)}, bf16[320,1024]{1,0:T(8,128)(2,1)}, f32[8,24,128]{2,1,0:T(8,128)}, /*index=5*/bf16[4,8,80,320]{3,2,1,0:T(8,128)(2,1)}) custom-call(bf16[1024,320]{1,0:T(8,128)(2,1)} %get-tuple-element.28.gate, bf16[1024,320]{1,0:T(8,128)(2,1)} %get-tuple-element.29.xs, ...), custom_call_target="tpu_custom_call" | custom-call | flops 10000000000 | bytes 10000000 | tf_op jit(solution)/shard_map/middle/pallas_call | solution.py:538
  99.2 48.2 %finish_grads.1 = (f32[80,320]{1,0:T(8,128)}, f32[80,320]{1,0:T(8,128)}, f32[40,320]{1,0:T(8,128)}, f32[80,320]{1,0:T(8,128)}, f32[16,320]{1,0:T(8,128)}, /*index=5*/bf16[320,1024]{1,0:T(8,128)(2,1)}) custom-call(bf16[8,320,1024]{2,1,0:T(8,128)(2,1)} %get-tuple-element.26.left.features, bf16[1024,320]{1,0:T(8,128)(2,1)} %get-tuple-element.31.dgate, ...), custom_call_target="tpu_custom_call" | custom-call | flops 10000000000 | bytes 100000000 | tf_op jit(solution)/shard_map/finish_grads/pallas_call | solution.py:792
  147.4 1.3 slice.12
  148.7 1.4 slice_reduce_fusion
  150.1 0.1 reshape_squeeze.3
  150.2 0.6 reduce_sum.9
  150.9 2.0 %copy.24 = bf16[1024,320]{0,1:T(8,128)(2,1)} copy(bf16[1024,320]{0,1:T(8,128)(2,1)} %bitcast.8) | data formatting | bytes 1310720
  152.8 1.6 copy.25
  154.4 1.6 copy.26
  155.9 1.6 copy.27
  157.5 1.3 copy.28
  (1 shorter events, 0.0 us)

commit v5 on v4

--- a/solution.py
+++ b/solution.py
@@ -1,5 +1,3 @@
-import functools
-
 import jax
 import jax.numpy as jnp
 from jax import lax
@@ -220,7 +218,21 @@
 
 
 def gather_kernel(
-    resid, w_gate, w_x, w_out, w_head, full_resid, full_weights, mix, weights, *scratch
+    resid,
+    w_gate,
+    w_x,
+    w_out,
+    w_head,
+    features,
+    gate,
+    xs,
+    out_lines,
+    mix,
+    full_resid,
+    full_weights,
+    acc,
+    weights,
+    *scratch,
 ):
     *mix_bufs, send, recv, local = scratch
     y, z, c = place()
@@ -247,8 +259,50 @@
     in_order(own_y, lines, chans, mixes, own_y)
     own_weights.wait()
     in_order(columns, lines, chans, mixes, lines, columns, mixes, lines, chans)
-    in_order(columns, lines, mixes, columns, chans, columns, lines, lines, chans, chans)
+    out_lines[y] = w_out[...]
+    out_puts = [
+        wire.put(w_out, out_lines.at[y], seq=lax.rem(y + d, NY) * NZ + z) for d in (1, 3, 2)
+    ]
+    in_order(columns, lines, mixes, columns, chans, columns, lines, lines)
     own_resid.wait()
+    tile = 256
+    width = gate.shape[1]
+    x, core = c // 2, c % 2
+
+    def project(blocks, first, last):
+        def step(at, carry):
+            cols = pl.ds(pl.multiple_of(at * tile, tile), tile)
+            total = 0.0 if first else acc[cols, :]
+            for block in blocks:
+                part = full_weights[block // 2, pl.ds((block % 2) * (NZ // 2), NZ // 2)]
+                total = total + lax.dot_general(
+                    full_resid[block, :, cols],
+                    part.reshape(part.shape[0] * part.shape[1], part.shape[2]),
+                    BY_ROWS,
+                    preferred_element_type=jnp.float32,
+                )
+            if last:
+                gate[cols, :] = total[:, :width].astype(gate.dtype)
+                xs[cols, :] = total[:, width:].astype(xs.dtype)
+            else:
+                acc[cols, :] = total
+            return carry
+
+        lax.fori_loop(0, acc.shape[0] // tile, step, 0)
+
+    mate = c + 1 - 2 * core
+    left = lax.rem(x + NX - 1, NX) * 2 + core
+    right = lax.rem(x + 1, NX) * 2 + core
+    project([c, left, right], True, False)
+    in_order(chans, chans)
+    out = pltpu.make_async_copy(full_resid, features, local.at[1])
+    out.start()
+    across = lax.rem(x + 2, NX) * 2 + core
+    flip = 1 - 2 * core
+    project([mate, left + flip, right + flip, across, across + flip], False, True)
+    for copy in out_puts:
+        copy.wait_recv()
+    out.wait()
     wire.finish()
 
 
@@ -259,17 +313,23 @@
     copies = 96
     block = (VOCAB, 128)
     rows, half = w_gate.shape
+    tokens = resid.shape[1]
     return pl.pallas_call(
         gather_kernel,
         name="gather_all",
         out_shape=(
             jax.ShapeDtypeStruct((NCHAN, *resid.shape), resid.dtype),
-            jax.ShapeDtypeStruct((NY, NZ, rows, 2 * half), w_gate.dtype),
+            jax.ShapeDtypeStruct((tokens, half), resid.dtype),
+            jax.ShapeDtypeStruct((tokens, half), resid.dtype),
+            jax.ShapeDtypeStruct((NY, *w_out.shape), w_out.dtype),
             jax.ShapeDtypeStruct((VOCAB, resid.shape[0]), f32),
         ),
-        in_specs=[anywhere] + [vmem] * 4,
-        out_specs=(anywhere, anywhere, vmem),
+        in_specs=[vmem] * 5,
+        out_specs=(anywhere, vmem, vmem, vmem, vmem),
         scratch_shapes=[
+            pltpu.VMEM((NCHAN, *resid.shape), resid.dtype),
+            pltpu.VMEM((NY, NZ, rows, 2 * half), w_gate.dtype),
+            pltpu.VMEM((tokens, 2 * half), f32),
             pltpu.VMEM((rows, 2 * half), w_gate.dtype),
             pltpu.VMEM(block, f32),
             pltpu.VMEM((NCHAN - 1, *block), f32),
@@ -280,7 +340,9 @@
             pltpu.SemaphoreType.DMA((copies,)),
             pltpu.SemaphoreType.DMA((2,)),
         ],
-        compiler_params=pltpu.CompilerParams(collective_id=0, has_side_effects=True),
+        compiler_params=pltpu.CompilerParams(
+            collective_id=0, has_side_effects=True, vmem_limit_bytes=VMEM_BYTES
+        ),
         cost_estimate=pl.CostEstimate(flops=10**10, bytes_accessed=10**8, transcendentals=0),
     )(resid, w_gate, w_x, w_out, w_head)
 
@@ -298,9 +360,12 @@
     resid,
     head_t,
     mix_t,
-    params,
+    conv_weight,
+    conv_bias,
+    norm_gain,
+    skip_d,
     targets,
-    w_out,
+    out_lines,
     dgate,
     dx,
     small,
@@ -333,13 +398,19 @@
     greet(
         [{"chan": lax.rem(c + d, NCHAN)} for d in range(1, NCHAN)]
         + [{"seq": later}, {"seq": sooner}]
-        + [{"seq": lax.rem(y + d, NY) * NZ + z} for d in range(1, NY)]
         + [{"seq": y * NZ + lax.rem(z + d, NZ)} for d in (1, NZ - 1)]
     )
     wire = Wire(w_send, w_recv)
-    whole = pl.ds(0, w_out.shape[0])
-    own_w_out = pltpu.make_async_copy(w_out, full_w_out.at[y, z], local.at[0])
-    own_w_out.start()
+    own_lines = pltpu.make_async_copy(out_lines, full_w_out.at[:, z], local.at[0])
+    own_lines.start()
+    columns = ring_z(
+        wire,
+        out_lines,
+        lambda at: full_w_out.at[:, at],
+        lambda at: (full_w_out.at[pl.ds(0, 2), at], full_w_out.at[pl.ds(2, 2), at]),
+        y,
+        z,
+    )
 
     def copy_of(source, target, at, where):
         return pltpu.make_async_remote_copy(
@@ -353,11 +424,13 @@
 
     edge = copy_of(xs.at[pl.ds(tokens - EDGE, EDGE)], before, 2 * NCHAN, {"seq": later})
     edge.start()
-    own_y = exchange_y(wire, w_out, full_w_out, y, z, whole)
-    columns = ring_z_columns(wire, full_w_out, y, z, whole)
-    in_order(own_y)
-    taps = [params[k : k + 1, :] for k in range(KERNEL)]
-    bias, skip, gain = params[4:5, :], params[5:6, :], params[6:7, :]
+    in_order(columns)
+    taps = [conv_weight[k : k + 1, :] for k in range(KERNEL)]
+    bias, gain = conv_bias[...], norm_gain[...]
+    head = lax.broadcasted_iota(jnp.int32, bias.shape, 1) // HEADDIM
+    skip = jnp.zeros(bias.shape, f32)
+    for at in range(skip_d.shape[0]):
+        skip = jnp.where(head == at, skip_d[at], skip)
     mix = mix_t[...]
     padded[pl.ds(EDGE, tokens), :] = xs[...].astype(f32)
 
@@ -409,8 +482,6 @@
         )
 
     edge.wait_recv()
-    own_w_out.wait()
-    in_order(own_y, columns)
     padded[pl.ds(0, EDGE), :] = before[...].astype(f32) * (s > 0).astype(f32)
 
     def forward_step(step, carry):
@@ -522,6 +593,7 @@
     lax.fori_loop(0, tokens // LANES, spread_step, 0)
     in_order(columns)
     wire.finish()
+    own_lines.wait()
     edge.wait_send()
     first_rows.wait_send()
     for d in range(1, NCHAN):
@@ -529,7 +601,7 @@
         tell(d).wait_send()
 
 
-def middle(gate, xs, resid, head_t, mix_t, params, targets, w_out):
+def middle(gate, xs, *others):
     f32, bf16 = jnp.float32, jnp.bfloat16
     vmem = pl.BlockSpec(memory_space=pltpu.VMEM)
     anywhere = pl.BlockSpec(memory_space=pl.ANY)
@@ -544,9 +616,9 @@
             jax.ShapeDtypeStruct((SUMS, width), f32),
             jax.ShapeDtypeStruct((width, tokens), bf16),
             jax.ShapeDtypeStruct((NCHAN, FACTS, LANES), f32),
-            jax.ShapeDtypeStruct((NY, NZ, *w_out.shape), bf16),
+            jax.ShapeDtypeStruct((NY, NZ, *others[-1].shape[1:]), bf16),
         ),
-        in_specs=[vmem] * 7 + [anywhere],
+        in_specs=[vmem] * 8 + [pl.BlockSpec(memory_space=pltpu.SMEM), vmem, anywhere],
         out_specs=(vmem,) * 5 + (anywhere,),
         scratch_shapes=[
             pltpu.VMEM((tokens + EDGE, width), f32),
@@ -562,15 +634,15 @@
             pltpu.VMEM((2, VOCAB, width), f32),
             pltpu.SemaphoreType.DMA((copies,)),
             pltpu.SemaphoreType.DMA((copies,)),
-            pltpu.SemaphoreType.DMA((NY + NZ,)),
-            pltpu.SemaphoreType.DMA((NY + NZ,)),
+            pltpu.SemaphoreType.DMA((NZ,)),
+            pltpu.SemaphoreType.DMA((NZ,)),
             pltpu.SemaphoreType.DMA((1,)),
         ],
         compiler_params=pltpu.CompilerParams(
             collective_id=1, has_side_effects=True, vmem_limit_bytes=VMEM_BYTES
         ),
         cost_estimate=pl.CostEstimate(flops=10**10, bytes_accessed=10**7, transcendentals=0),
-    )(gate, xs, resid, head_t, mix_t, params, targets, w_out)
+    )(gate, xs, *others)
 
 
 def scatter_seq(wire, grads, ready, bufs, outs, y, z, start, count):
@@ -615,7 +687,7 @@
         + got_above[:, rows].astype(f32)
     ).astype(bf16)
     puts = []
-    for d in range(1, NZ):
+    for d in (4, 3, 5, 2, 6, 1, 7):
         peer = lax.rem(z + d, NZ)
         puts.append(wire.put(lines.at[peer, rows], got_z.at[d - 1, rows], seq=y * NZ + peer))
     yield
@@ -624,8 +696,9 @@
         + got_below[z, rows].astype(f32)
         + got_above[z, rows].astype(f32)
     )
+    for copy in puts:
+        copy.wait_recv()
     for d in range(1, NZ):
-        puts[d - 1].wait_recv()
         acc = acc + got_z[d - 1, rows].astype(f32)
     half = acc.shape[1] // 2
     outs[0][rows] = acc[:, :half]
@@ -730,11 +803,12 @@
     rows = grad_gate.shape[0]
     outs = (grad_gate, grad_x)
     smalls = sum_small(wire, small, small_y, small_part, small_z, total, heads, y, z, c)
-    one = scatter_seq(wire, grads, ready, bufs, outs, y, z, 0, 48)
-    two = scatter_seq(wire, grads, lambda block: None, bufs, outs, y, z, 48, rows - 48)
+    one = scatter_seq(wire, grads, ready, bufs, outs, y, z, 0, 32)
+    two = scatter_seq(wire, grads, lambda block: None, bufs, outs, y, z, 32, 32)
+    three = scatter_seq(wire, grads, lambda block: None, bufs, outs, y, z, 64, rows - 64)
     chans = gather_chan(wire, gained, full_gained, c, gained.shape[0])
-    in_order(smalls, chans, one, chans, smalls, one, chans, one, two, one, chans)
-    in_order(two, smalls, two, two, chans, smalls, chans)
+    in_order(smalls, chans, one, chans, smalls, one, chans, one, two, one, chans, two, smalls)
+    in_order(two, three, two, three, chans, three, three, smalls, chans)
     own.wait()
     weights.wait()
 
@@ -760,7 +834,9 @@
         high = head.astype(bf16)
         low = (head - high.astype(f32)).astype(bf16)
         acc = acc + jnp.dot(
-            jnp.concatenate([high, low], axis=0), out_cols[at], preferred_element_type=f32
+            jnp.concatenate([high, low], axis=0),
+            out_cols[at],
+            preferred_element_type=f32,
         )
     grad_head[...] = total[pl.ds(VOCAB, VOCAB), :] + acc[:VOCAB] + acc[VOCAB:]
     s = y * NZ + z
@@ -773,7 +849,7 @@
     grad_out[...] = lax.dot_general(
         here, head_t[...].astype(f32), BY_ROWS, precision=EXACT, preferred_element_type=f32
     )
-    in_order(one, two)
+    in_order(one, two, three)
     wire.finish()
 
 
@@ -782,7 +858,6 @@
     anywhere = pl.BlockSpec(memory_space=pl.ANY)
     vmem = pl.BlockSpec(memory_space=pltpu.VMEM)
     tokens, width = dgate.shape
-    _, depth, _ = w_out.shape
     rows = INNER // (NY * NZ)
     copies = 80
     cols = 2 * width
@@ -831,38 +906,25 @@
 BY_ROWS = (((0,), (0,)), ((), ()))
 
 
-def sum_of_dots(left, right):
-    acc = 0.0
-    for at in range(left.shape[0]):
-        acc = acc + lax.dot_general(
-            left[at], right[at], BY_ROWS, preferred_element_type=jnp.float32
-        )
-    return acc
-
-
-def project_kernel(left, right, gate, xs):
-    acc = sum_of_dots(left, right)
-    width = gate.shape[1]
-    gate[...] = acc[:, :width].astype(gate.dtype)
-    xs[...] = acc[:, width:].astype(xs.dtype)
-
-
-def project(left, right):
-    parts, depth, tokens = left.shape
-    tile, width = 256, right.shape[2] // 2
-    half = pl.BlockSpec((tile, width), lambda i: (i, 0))
+def hand_out_kernel(total, *refs):
+    count = len(refs) // 2
+    for at in range(count):
+        refs[at + count][...] = refs[at][...]
+    refs[-1][...] = total[pl.ds(2 * VOCAB, KERNEL), :]
+
+
+def hand_out(total, *arrays):
+    vmem = pl.BlockSpec(memory_space=pltpu.VMEM)
+    shapes = [jax.ShapeDtypeStruct(array.shape, array.dtype) for array in arrays]
+    shapes.append(jax.ShapeDtypeStruct((KERNEL, total.shape[1]), total.dtype))
     return pl.pallas_call(
-        project_kernel,
-        name="project",
-        grid=(tokens // tile,),
-        out_shape=(jax.ShapeDtypeStruct((tokens, width), jnp.bfloat16),) * 2,
-        in_specs=[
-            pl.BlockSpec((parts, depth, tile), lambda i: (0, 0, i)),
-            pl.BlockSpec(right.shape, lambda i: (0, 0, 0), pipeline_mode=pl.Buffered(1)),
-        ],
-        out_specs=(half, half),
+        hand_out_kernel,
+        name="hand_out",
+        out_shape=tuple(shapes),
+        in_specs=[vmem] * (len(arrays) + 1),
+        out_specs=(vmem,) * len(shapes),
         compiler_params=pltpu.CompilerParams(vmem_limit_bytes=VMEM_BYTES),
-    )(left, right)
+    )(total, *arrays)
 
 
 def slope(value, sig):
@@ -875,17 +937,8 @@
     f32 = jnp.float32
     local_inner = w_gate_in.shape[1]
     head_t, resid_t = w_head.T, resid.T
-    features, full, mix_t = gather_all(resid_t, w_gate_in, w_x_in, w_out, head_t)
-    gate_pre, x_pre = project(features, full.reshape(NCHAN, local_inner, 2 * local_inner))
-    params = jnp.concatenate(
-        [
-            conv_weight,
-            conv_bias[None],
-            jnp.repeat(skip_d, HEADDIM)[None],
-            norm_gain[None],
-            jnp.zeros((1, local_inner), f32),
-        ],
-        axis=0,
+    features, gate_pre, x_pre, out_lines, mix_t = gather_all(
+        resid_t, w_gate_in, w_x_in, w_out, head_t
     )
     dgate, dx_pre, small, gained, facts, out_cols = middle(
         gate_pre,
@@ -893,11 +946,14 @@
         resid_t,
         head_t,
         mix_t,
-        params,
+        conv_weight,
+        conv_bias[None],
+        norm_gain[None],
+        skip_d,
         targets.reshape(NCHAN, 1, LANES),
-        w_out,
-    )
-    grad_gate_in, grad_x_in, total, grad_out, grad_head_t, new_resid_t = finish_grads(
+        out_lines,
+    )
+    grad_gate_in, grad_x_in, total, *others = finish_grads(
         features,
         dgate,
         dx_pre,
@@ -908,8 +964,10 @@
         facts,
         head_t,
     )
+    grad_gate_in, grad_x_in, grad_out, grad_head_t, new_resid_t, grad_conv_weight = hand_out(
+        total, grad_gate_in, grad_x_in, *others
+    )
     at = 2 * VOCAB
-    grad_conv_weight = total[at : at + KERNEL]
     grad_conv_bias = total[at + KERNEL]
     grad_gain = total[at + KERNEL + 1]
     grad_skip = total[at + KERNEL + 2].reshape(-1, HEADDIM).sum(axis=1)

time: 161 us -> 143 us (0.89); the launches traced: 159 us -> 143 us
  local copies, waits for them, and re-layouts: 14.3 us -> 3.98 us
  Pallas kernels: 143 us -> 137 us
    unnamed x5 -> x0, local copies, waits for them, and re-layouts: 7.98 us -> none
    pallas_call x1, Pallas kernels: 10.2 us -> 2.3 us  [hand_out(): pl.pallas_call(hand_out_kernel, name='hand_out', out_shape=tuple(shapes),...]
    pallas_call x1, Pallas kernels: 48.1 us -> 55.9 us  [gather_all(): pl.pallas_call(gather_kernel, name='gather_all', out_shape=(jax.ShapeDtyp...]
    pallas_call x1, Pallas kernels: 48.2 us -> 45.2 us  [finish_grads(): pl.pallas_call(grads_kernel, name='finish_grads', out_shape=(block, block...]
    pallas_call x1, Pallas kernels: 36.8 us -> 34.1 us  [middle(): pl.pallas_call(middle_kernel, name='middle', out_shape=(jax.ShapeDtypeStr...]
where the time goes in v5:
time: 143 us
  Pallas kernels  137 us (96%)
  local copies, waits for them, and re-layouts  3.98 us (3%)
    pallas_call x1, Pallas kernels, gather_all(): pl.pallas_call(gather_kernel, name='gather_all', out_shape=(jax.ShapeDtyp...  55.9 us
    pallas_call x1, Pallas kernels, finish_grads(): pl.pallas_call(grads_kernel, name='finish_grads', out_shape=(block, block...  45.2 us
    pallas_call x1, Pallas kernels, middle(): pl.pallas_call(middle_kernel, name='middle', out_shape=(jax.ShapeDtypeStr...  34.1 us

profile of v5, /device:TPU:1, one launch (start us, length us, event | category | flops | bytes accessed | tf_op | source)
XLA Modules:
  0.0 142.8 jit_solution(5536773918033026747)
XLA Ops:
  0.6 1.2 broadcast_in_dim.6.conv_bias
  1.9 1.2 broadcast_in_dim.7.norm_gain
  3.1 55.9 %gather_all.1 = (bf16[8,320,1024]{2,1,0:T(8,128)(2,1)}, bf16[1024,320]{1,0:T(8,128)(2,1)}, bf16[1024,320]{1,0:T(8,128)(2,1)}, bf16[4,80,320]{2,1,0:T(8,128)(2,1)}, f32[16,320]{1,0:T(8,128)}) custom-call(bf16[320,1024]{1,0:T(8,128)(2,1)} %bitcast.6, bf16[80,320]{1,0:T(8,128)(2,1)} %w_gate.1, bf16[80,320]{1,0:T(8,128)(2,1)} %w_x.1, bf16[80,320]{1,0:T(8,128)(2,1)} %w_out.1, ...), custom_call_target="tpu_custom_call" | custom-call | flops 10000000000 | bytes 100000000 | tf_op jit(solution)/shard_map/gather_all/pallas_call | solution.py:317
  59.0 34.1 %middle.1 = (bf16[1024,320]{1,0:T(8,128)(2,1)}, bf16[1024,320]{1,0:T(8,128)(2,1)}, f32[40,320]{1,0:T(8,128)}, bf16[320,1024]{1,0:T(8,128)(2,1)}, f32[8,24,128]{2,1,0:T(8,128)}, /*index=5*/bf16[4,8,80,320]{3,2,1,0:T(8,128)(2,1)}) custom-call(bf16[1024,320]{1,0:T(8,128)(2,1)} %get-tuple-element.33.gate, bf16[1024,320]{1,0:T(8,128)(2,1)} %get-tuple-element.34.xs, ...), custom_call_target="tpu_custom_call" | custom-call | flops 10000000000 | bytes 10000000 | tf_op jit(solution)/shard_map/middle/pallas_call | solution.py:610
  93.1 45.2 %finish_grads.1 = (f32[80,320]{1,0:T(8,128)}, f32[80,320]{1,0:T(8,128)}, f32[40,320]{1,0:T(8,128)}, f32[80,320]{1,0:T(8,128)}, f32[16,320]{1,0:T(8,128)}, /*index=5*/bf16[320,1024]{1,0:T(8,128)(2,1)}) custom-call(bf16[8,320,1024]{2,1,0:T(8,128)(2,1)} %get-tuple-element.32.features, bf16[1024,320]{1,0:T(8,128)(2,1)} %get-tuple-element.37.dgate, ...), custom_call_target="tpu_custom_call" | custom-call | flops 10000000000 | bytes 100000000 | tf_op jit(solution)/shard_map/finish_grads/pallas_call | solution.py:867
  138.3 2.3 %hand_out.1 = (f32[80,320]{1,0:T(8,128)}, f32[80,320]{1,0:T(8,128)}, f32[80,320]{1,0:T(8,128)}, f32[16,320]{1,0:T(8,128)}, bf16[320,1024]{1,0:T(8,128)(2,1)}, /*index=5*/f32[4,320]{1,0:T(4,128)}) custom-call(f32[40,320]{1,0:T(8,128)} %get-tuple-element.43.total, f32[80,320]{1,0:T(8,128)} %get-tuple-element.44.refs_0_, f32[80,320]{1,0:T(8,128)} %get-tuple-element.45.refs_1_, ...), custom_call_target="tpu_custom_call" | custom-call | tf_op jit(solution)/shard_map/hand_out/pallas_call | solution.py:920
  140.6 1.4 slice_reduce_fusion
  142.1 0.1 reshape_squeeze.3
  142.1 0.6 reduce_sum.9

commit v6 on v5

--- a/solution.py
+++ b/solution.py
@@ -42,7 +42,7 @@
     barrier = pltpu.get_barrier_semaphore()
     for peer in peers:
         pl.semaphore_signal(barrier, inc=1, device_id=peer, device_id_type=MESH)
-    pl.semaphore_wait(barrier, len(peers))
+    return lambda: pl.semaphore_wait(barrier, len(peers))
 
 
 def in_order(*streams):
@@ -237,18 +237,19 @@
     *mix_bufs, send, recv, local = scratch
     y, z, c = place()
     half = w_gate.shape[1]
-    weights[:, pl.ds(0, half)] = w_gate[...]
-    weights[:, pl.ds(half, half)] = w_x[...]
-    greet(
+    meet = greet(
         [{"chan": lax.rem(c + d, NCHAN)} for d in range(1, NCHAN)]
         + [{"seq": lax.rem(y + d, NY) * NZ + z} for d in range(1, NY)]
         + [{"seq": y * NZ + lax.rem(z + d, NZ)} for d in range(1, NZ)]
     )
+    weights[:, pl.ds(0, half)] = w_gate[...]
+    weights[:, pl.ds(half, half)] = w_x[...]
     wire = Wire(send, recv)
     own_weights = pltpu.make_async_copy(weights, full_weights.at[y, z], local.at[0])
     own_resid = pltpu.make_async_copy(resid, full_resid.at[c], local.at[1])
     own_weights.start()
     own_resid.start()
+    meet()
     rows, first = weights.shape[0], 32
     one, rest = pl.ds(0, first), pl.ds(first, rows - first)
     lines = gather_z_then_y(wire, weights, full_weights, y, z, rest)
@@ -259,9 +260,9 @@
     in_order(own_y, lines, chans, mixes, own_y)
     own_weights.wait()
     in_order(columns, lines, chans, mixes, lines, columns, mixes, lines, chans)
-    out_lines[y] = w_out[...]
+    out_lines[0, y] = w_out[...]
     out_puts = [
-        wire.put(w_out, out_lines.at[y], seq=lax.rem(y + d, NY) * NZ + z) for d in (1, 3, 2)
+        wire.put(w_out, out_lines.at[0, y], seq=lax.rem(y + d, NY) * NZ + z) for d in (1, 3, 2)
     ]
     in_order(columns, lines, mixes, columns, chans, columns, lines, lines)
     own_resid.wait()
@@ -293,6 +294,12 @@
     mate = c + 1 - 2 * core
     left = lax.rem(x + NX - 1, NX) * 2 + core
     right = lax.rem(x + 1, NX) * 2 + core
+    for copy in out_puts:
+        copy.wait_recv()
+    out_puts = [
+        wire.put(out_lines.at[0], out_lines.at[1], seq=y * NZ + lax.rem(z + 1, NZ)),
+        wire.put(out_lines.at[0], out_lines.at[2], seq=y * NZ + lax.rem(z + NZ - 1, NZ)),
+    ]
     project([c, left, right], True, False)
     in_order(chans, chans)
     out = pltpu.make_async_copy(full_resid, features, local.at[1])
@@ -321,7 +328,7 @@
             jax.ShapeDtypeStruct((NCHAN, *resid.shape), resid.dtype),
             jax.ShapeDtypeStruct((tokens, half), resid.dtype),
             jax.ShapeDtypeStruct((tokens, half), resid.dtype),
-            jax.ShapeDtypeStruct((NY, *w_out.shape), w_out.dtype),
+            jax.ShapeDtypeStruct((3, NY, *w_out.shape), w_out.dtype),
             jax.ShapeDtypeStruct((VOCAB, resid.shape[0]), f32),
         ),
         in_specs=[vmem] * 5,
@@ -352,6 +359,25 @@
 EDGE = 16
 SUMS = 40
 FACTS = 24
+
+
+def ring_on(wire, lines, full, y, z):
+    up, down = y * NZ + lax.rem(z + 1, NZ), y * NZ + lax.rem(z + NZ - 1, NZ)
+    plus = wire.put(lines.at[1], full.at[:, lax.rem(z + NZ - 1, NZ)], seq=up)
+    minus = wire.put(lines.at[2], full.at[:, lax.rem(z + 1, NZ)], seq=down)
+    for step in range(2, NZ // 2):
+        yield
+        last = step == NZ // 2 - 1
+        behind, ahead = lax.rem(z + NZ - step, NZ), lax.rem(z + step, NZ)
+        plus.wait_recv()
+        moved = full.at[pl.ds(0, NY // 2) if last else slice(None), behind]
+        plus = wire.put(moved, moved, seq=up)
+        minus.wait_recv()
+        moved = full.at[pl.ds(NY // 2, NY // 2) if last else slice(None), ahead]
+        minus = wire.put(moved, moved, seq=down)
+    yield
+    plus.wait_recv()
+    minus.wait_recv()
 
 
 def middle_kernel(
@@ -395,22 +421,20 @@
     s = y * NZ + z
     last_seq = NY * NZ - 1
     later, sooner = lax.rem(s + 1, NY * NZ), lax.rem(s + last_seq, NY * NZ)
-    greet(
+    meet = greet(
         [{"chan": lax.rem(c + d, NCHAN)} for d in range(1, NCHAN)]
         + [{"seq": later}, {"seq": sooner}]
         + [{"seq": y * NZ + lax.rem(z + d, NZ)} for d in (1, NZ - 1)]
     )
     wire = Wire(w_send, w_recv)
-    own_lines = pltpu.make_async_copy(out_lines, full_w_out.at[:, z], local.at[0])
-    own_lines.start()
-    columns = ring_z(
-        wire,
-        out_lines,
-        lambda at: full_w_out.at[:, at],
-        lambda at: (full_w_out.at[pl.ds(0, 2), at], full_w_out.at[pl.ds(2, 2), at]),
-        y,
-        z,
-    )
+    near = (z, lax.rem(z + NZ - 1, NZ), lax.rem(z + 1, NZ))
+    own_lines = [
+        pltpu.make_async_copy(out_lines.at[at], full_w_out.at[:, near[at]], local.at[at])
+        for at in range(3)
+    ]
+    for copy in own_lines:
+        copy.start()
+    columns = ring_on(wire, out_lines, full_w_out, y, z)
 
     def copy_of(source, target, at, where):
         return pltpu.make_async_remote_copy(
@@ -423,8 +447,6 @@
         )
 
     edge = copy_of(xs.at[pl.ds(tokens - EDGE, EDGE)], before, 2 * NCHAN, {"seq": later})
-    edge.start()
-    in_order(columns)
     taps = [conv_weight[k : k + 1, :] for k in range(KERNEL)]
     bias, gain = conv_bias[...], norm_gain[...]
     head = lax.broadcasted_iota(jnp.int32, bias.shape, 1) // HEADDIM
@@ -433,6 +455,9 @@
         skip = jnp.where(head == at, skip_d[at], skip)
     mix = mix_t[...]
     padded[pl.ds(EDGE, tokens), :] = xs[...].astype(f32)
+    meet()
+    edge.start()
+    in_order(columns)
 
     def window(tile):
         start = pl.multiple_of(tile * LANES, LANES)
@@ -570,7 +595,6 @@
         return carry
 
     lax.fori_loop(1, tokens // LANES, backward_step, 0)
-    in_order(columns)
     by_channel = acc_heads[0]
     small[pl.ds(0, VOCAB), :] = by_channel * skip * gain
     small[pl.ds(VOCAB, VOCAB), :] = acc_heads[1]
@@ -593,7 +617,8 @@
     lax.fori_loop(0, tokens // LANES, spread_step, 0)
     in_order(columns)
     wire.finish()
-    own_lines.wait()
+    for copy in own_lines:
+        copy.wait()
     edge.wait_send()
     first_rows.wait_send()
     for d in range(1, NCHAN):
@@ -616,7 +641,7 @@
             jax.ShapeDtypeStruct((SUMS, width), f32),
             jax.ShapeDtypeStruct((width, tokens), bf16),
             jax.ShapeDtypeStruct((NCHAN, FACTS, LANES), f32),
-            jax.ShapeDtypeStruct((NY, NZ, *others[-1].shape[1:]), bf16),
+            jax.ShapeDtypeStruct((NY, NZ, *others[-1].shape[2:]), bf16),
         ),
         in_specs=[vmem] * 8 + [pl.BlockSpec(memory_space=pltpu.SMEM), vmem, anywhere],
         out_specs=(vmem,) * 5 + (anywhere,),
@@ -636,7 +661,7 @@
             pltpu.SemaphoreType.DMA((copies,)),
             pltpu.SemaphoreType.DMA((NZ,)),
             pltpu.SemaphoreType.DMA((NZ,)),
-            pltpu.SemaphoreType.DMA((1,)),
+            pltpu.SemaphoreType.DMA((3,)),
         ],
         compiler_params=pltpu.CompilerParams(
             collective_id=1, has_side_effects=True, vmem_limit_bytes=VMEM_BYTES
@@ -762,6 +787,11 @@
     *bufs, small_y, small_part, small_z, send, recv, local = rest
     y, z, c = place()
     width = dgate.shape[1]
+    meet = greet(
+        [{"chan": lax.rem(c + d, NCHAN)} for d in range(1, NCHAN)]
+        + [{"seq": lax.rem(y + d, NY) * NZ + z} for d in range(1, NY)]
+        + [{"seq": y * NZ + lax.rem(z + d, NZ)} for d in range(1, NZ)]
+    )
     order = [
         2 * lax.rem(y + 2, NY),
         2 * lax.rem(y + 2, NY) + 1,
@@ -784,22 +814,25 @@
     weights.start()
     both[:, pl.ds(0, width)] = dgate[...]
     both[:, pl.ds(width, width)] = dx[...]
-    greet(
-        [{"chan": lax.rem(c + d, NCHAN)} for d in range(1, NCHAN)]
-        + [{"seq": lax.rem(y + d, NY) * NZ + z} for d in range(1, NY)]
-        + [{"seq": y * NZ + lax.rem(z + d, NZ)} for d in range(1, NZ)]
-    )
     wire = Wire(send, recv)
-    steps = iter(range(NCHAN))
-
-    def ready(block):
-        step = next(steps)
+    steps = []
+
+    def compute(step):
         loads[step].wait()
         product = jnp.dot(feats[step], both[...], preferred_element_type=f32)
         lines = product.reshape(NZ // 2, product.shape[0] // (NZ // 2), product.shape[1])
+        block = order[step]
         first = lax.rem(block, 2) * (NZ // 2)
         grads[block // 2, pl.ds(first, NZ // 2)] = lines.astype(bf16)
 
+    def ready(block):
+        steps.append(block)
+        if len(steps) > 2:
+            compute(len(steps) - 1)
+
+    compute(0)
+    compute(1)
+    meet()
     rows = grad_gate.shape[0]
     outs = (grad_gate, grad_x)
     smalls = sum_small(wire, small, small_y, small_part, small_z, total, heads, y, z, c)

time: 143 us -> 139 us (0.972)
  Pallas kernels: 137 us -> 134 us
    pallas_call x1, Pallas kernels: 34.1 us -> 31 us  [middle(): pl.pallas_call(middle_kernel, name='middle', out_shape=(jax.ShapeDtypeStr...]
where the time goes in v6:
time: 139 us
  Pallas kernels  134 us (96%)
  local copies, waits for them, and re-layouts  3.98 us (3%)
    pallas_call x1, Pallas kernels, gather_all(): pl.pallas_call(gather_kernel, name='gather_all', out_shape=(jax.ShapeDtyp...  55.5 us
    pallas_call x1, Pallas kernels, finish_grads(): pl.pallas_call(grads_kernel, name='finish_grads', out_shape=(block, block...  45 us
    pallas_call x1, Pallas kernels, middle(): pl.pallas_call(middle_kernel, name='middle', out_shape=(jax.ShapeDtypeStr...  31 us

profile of v6, /device:TPU:1, one launch (start us, length us, event | category | flops | bytes accessed | tf_op | source)
XLA Modules:
  0.0 139.1 jit_solution(11088271329420629552)
XLA Ops:
  0.6 1.2 broadcast_in_dim.6.conv_bias
  1.9 1.2 broadcast_in_dim.7.norm_gain
  3.1 55.5 %gather_all.1 = (bf16[8,320,1024]{2,1,0:T(8,128)(2,1)}, bf16[1024,320]{1,0:T(8,128)(2,1)}, bf16[1024,320]{1,0:T(8,128)(2,1)}, bf16[3,4,80,320]{3,2,1,0:T(8,128)(2,1)}, f32[16,320]{1,0:T(8,128)}) custom-call(bf16[320,1024]{1,0:T(8,128)(2,1)} %bitcast.6, bf16[80,320]{1,0:T(8,128)(2,1)} %w_gate.1, bf16[80,320]{1,0:T(8,128)(2,1)} %w_x.1, bf16[80,320]{1,0:T(8,128)(2,1)} %w_out.1, ...), custom_call_target="tpu_custom_call" | custom-call | flops 10000000000 | bytes 100000000 | tf_op jit(solution)/shard_map/gather_all/pallas_call | solution.py:324
  58.6 31.0 %middle.1 = (bf16[1024,320]{1,0:T(8,128)(2,1)}, bf16[1024,320]{1,0:T(8,128)(2,1)}, f32[40,320]{1,0:T(8,128)}, bf16[320,1024]{1,0:T(8,128)(2,1)}, f32[8,24,128]{2,1,0:T(8,128)}, /*index=5*/bf16[4,8,80,320]{3,2,1,0:T(8,128)(2,1)}) custom-call(bf16[1024,320]{1,0:T(8,128)(2,1)} %get-tuple-element.33.gate, bf16[1024,320]{1,0:T(8,128)(2,1)} %get-tuple-element.34.xs, ...), custom_call_target="tpu_custom_call" | custom-call | flops 10000000000 | bytes 10000000 | tf_op jit(solution)/shard_map/middle/pallas_call | solution.py:635
  89.7 45.0 %finish_grads.1 = (f32[80,320]{1,0:T(8,128)}, f32[80,320]{1,0:T(8,128)}, f32[40,320]{1,0:T(8,128)}, f32[80,320]{1,0:T(8,128)}, f32[16,320]{1,0:T(8,128)}, /*index=5*/bf16[320,1024]{1,0:T(8,128)(2,1)}) custom-call(bf16[8,320,1024]{2,1,0:T(8,128)(2,1)} %get-tuple-element.32.features, bf16[1024,320]{1,0:T(8,128)(2,1)} %get-tuple-element.37.dgate, ...), custom_call_target="tpu_custom_call" | custom-call | flops 10000000000 | bytes 100000000 | tf_op jit(solution)/shard_map/finish_grads/pallas_call | solution.py:900
  134.6 2.3 %hand_out.1 = (f32[80,320]{1,0:T(8,128)}, f32[80,320]{1,0:T(8,128)}, f32[80,320]{1,0:T(8,128)}, f32[16,320]{1,0:T(8,128)}, bf16[320,1024]{1,0:T(8,128)(2,1)}, /*index=5*/f32[4,320]{1,0:T(4,128)}) custom-call(f32[40,320]{1,0:T(8,128)} %get-tuple-element.43.total, f32[80,320]{1,0:T(8,128)} %get-tuple-element.44.refs_0_, f32[80,320]{1,0:T(8,128)} %get-tuple-element.45.refs_1_, ...), custom_call_target="tpu_custom_call" | custom-call | tf_op jit(solution)/shard_map/hand_out/pallas_call | solution.py:953
  137.0 1.4 %slice_reduce_fusion = (f32[320]{0:T(512)}, f32[320]{0:T(512)S(1)}, f32[320]{0:T(512)}) fusion(f32[40,320]{1,0:T(8,128)} %get-tuple-element.43.total), kind=kLoop, calls=%fused_computation | loop fusion | bytes 7680 | tf_op jit(solution)/shard_map/slice | solution.py:1005
  138.4 0.1 reshape_squeeze.3
  138.4 0.6 reduce_sum.9

commit v7 on v6

--- a/solution.py
+++ b/solution.py
@@ -730,7 +730,7 @@
     outs[1][rows] = acc[:, half:]
 
 
-def sum_small(wire, small, got_y, part, got_z, total, heads, y, z, c):
+def sum_small(wire, small, got_y, part, got_z, mine, sums, total, heads, y, z, c):
     puts = [
         wire.put(small, got_y.at[y], seq=lax.rem(y + d, NY) * NZ + z) for d in range(1, NY)
     ]
@@ -741,18 +741,31 @@
     acc = got_y[0]
     for at in range(1, NY):
         acc = acc + got_y[at]
-    part[...] = acc
-    puts = [
-        wire.put(part, got_z.at[z], seq=y * NZ + lax.rem(z + d, NZ)) for d in range(1, NZ)
-    ]
-    got_z[z] = acc
+    used = small.shape[0] // 8
+    for at in range(NZ):
+        lines = acc[8 * at : 8 * at + 8] if at < used else jnp.zeros_like(acc[:8])
+        part[at] = lines
+    puts = []
+    for d in range(1, NZ):
+        peer = lax.rem(z + d, NZ)
+        puts.append(wire.put(part.at[peer], got_z.at[z], seq=y * NZ + peer))
+    got_z[z] = part[z]
     yield
     for copy in puts:
         copy.wait_recv()
     acc = got_z[0]
     for at in range(1, NZ):
         acc = acc + got_z[at]
-    total[...] = acc
+    mine[...] = acc
+    puts = [
+        wire.put(mine, sums.at[z], seq=y * NZ + lax.rem(z + d, NZ)) for d in range(1, NZ)
+    ]
+    sums[z] = acc
+    yield
+    for copy in puts:
+        copy.wait_recv()
+    for at in range(used):
+        total[pl.ds(8 * at, 8), :] = sums[at]
     first = pl.ds(0, VOCAB)
     puts = [
         wire.put(total.at[first], heads.at[c], chan=lax.rem(c + d, NCHAN))
@@ -783,8 +796,8 @@
     *scratch,
 ):
     f32, bf16 = jnp.float32, jnp.bfloat16
-    feats, both, grads, full_gained, out_cols, heads, *rest = scratch
-    *bufs, small_y, small_part, small_z, send, recv, local = rest
+    feats, both, grads, full_gained, out_cols, heads, back, *rest = scratch
+    *bufs, small_y, small_part, small_z, small_mine, small_sums, send, recv, local = rest
     y, z, c = place()
     width = dgate.shape[1]
     meet = greet(
@@ -835,32 +848,46 @@
     meet()
     rows = grad_gate.shape[0]
     outs = (grad_gate, grad_x)
-    smalls = sum_small(wire, small, small_y, small_part, small_z, total, heads, y, z, c)
+    small_bufs = (small_y, small_part, small_z, small_mine, small_sums)
+    smalls = sum_small(wire, small, *small_bufs, total, heads, y, z, c)
     one = scatter_seq(wire, grads, ready, bufs, outs, y, z, 0, 32)
     two = scatter_seq(wire, grads, lambda block: None, bufs, outs, y, z, 32, 32)
     three = scatter_seq(wire, grads, lambda block: None, bufs, outs, y, z, 64, rows - 64)
     chans = gather_chan(wire, gained, full_gained, c, gained.shape[0])
-    in_order(smalls, chans, one, chans, smalls, one, chans, one, two, one, chans, two, smalls)
-    in_order(two, three, two, three, chans, three, three, smalls, chans)
+    in_order(smalls, chans, one, chans, smalls, one, chans, smalls, one, two, one, chans, two)
+    in_order(smalls, two, three, two, chans)
     own.wait()
     weights.wait()
-
-    def project_back(step, carry):
-        cols = pl.ds(pl.multiple_of(step * 256, 256), 256)
-        acc = 0.0
-        for at in range(NCHAN):
-            acc = acc + lax.dot_general(
-                out_cols[at], full_gained[at, :, cols], BY_ROWS, preferred_element_type=f32
-            )
-        for at in range(2):
-            tile = 2 * step + at
-            lanes = pl.ds(pl.multiple_of(tile * LANES, LANES), LANES)
-            scale = facts[tile, VOCAB : VOCAB + 1]
-            summed = resid[:, lanes].astype(f32) + scale * acc[:, at * LANES : (at + 1) * LANES]
-            new_resid[:, lanes] = summed.astype(bf16)
-        return carry
-
-    lax.fori_loop(0, new_resid.shape[1] // 256, project_back, 0)
+    x, core = c // 2, c % 2
+    near = [2 * lax.rem(x + d, NX) + core for d in range(NX)]
+
+    def project_back(blocks, last):
+        def step(at, carry):
+            cols = pl.ds(pl.multiple_of(at * 256, 256), 256)
+            acc = back[:, cols] if last else 0.0
+            for block in blocks:
+                acc = acc + lax.dot_general(
+                    out_cols[block],
+                    full_gained[block, :, cols],
+                    BY_ROWS,
+                    preferred_element_type=f32,
+                )
+            if not last:
+                back[:, cols] = acc
+                return carry
+            for part in range(2):
+                tile = 2 * at + part
+                lanes = pl.ds(pl.multiple_of(tile * LANES, LANES), LANES)
+                scale = facts[tile, VOCAB : VOCAB + 1]
+                scaled = scale * acc[:, part * LANES : (part + 1) * LANES]
+                new_resid[:, lanes] = (resid[:, lanes].astype(f32) + scaled).astype(bf16)
+            return carry
+
+        lax.fori_loop(0, new_resid.shape[1] // 256, step, 0)
+
+    project_back(near, False)
+    in_order(three, three, three, smalls, chans)
+    project_back([block + 1 - 2 * core for block in near], True)
     acc = 0.0
     for at in range(NCHAN):
         head = heads[at]
@@ -917,14 +944,17 @@
             pltpu.VMEM((NCHAN, *gained.shape), bf16),
             pltpu.VMEM(w_out.shape, bf16),
             pltpu.VMEM((NCHAN, VOCAB, width), f32),
+            pltpu.VMEM(resid.shape, f32),
         ]
         + [pltpu.VMEM(half, bf16)] * 4
         + [pltpu.VMEM(line, bf16)] * 3
         + [
             pltpu.VMEM((NZ - 1, rows, cols), bf16),
             pltpu.VMEM((NY, *small.shape), f32),
-            pltpu.VMEM(small.shape, f32),
-            pltpu.VMEM((NZ, *small.shape), f32),
+            pltpu.VMEM((NZ, 8, width), f32),
+            pltpu.VMEM((NZ, 8, width), f32),
+            pltpu.VMEM((8, width), f32),
+            pltpu.VMEM((NZ, 8, width), f32),
             pltpu.SemaphoreType.DMA((copies,)),
             pltpu.SemaphoreType.DMA((copies,)),
             pltpu.SemaphoreType.DMA((NCHAN + 2,)),

time: 139 us -> 139 us (level)
  no operation moved by 1% of the time
where the time goes in v7:
time: 139 us; the launch traced here: 138 us
  Pallas kernels  133 us (96%)
  local copies, waits for them, and re-layouts  3.98 us (3%)
    pallas_call x1, Pallas kernels, gather_all(): pl.pallas_call(gather_kernel, name='gather_all', out_shape=(jax.ShapeDtyp...  55.5 us
    pallas_call x1, Pallas kernels, finish_grads(): pl.pallas_call(grads_kernel, name='finish_grads', out_shape=(block, block...  44 us
    pallas_call x1, Pallas kernels, middle(): pl.pallas_call(middle_kernel, name='middle', out_shape=(jax.ShapeDtypeStr...  31 us

profile of v7, /device:TPU:1, one launch (start us, length us, event | category | flops | bytes accessed | tf_op | source)
XLA Modules:
  0.0 138.1 jit_solution(14995923235655348740)
XLA Ops:
  0.6 1.2 broadcast_in_dim.6.conv_bias
  1.9 1.2 broadcast_in_dim.7.norm_gain
  3.1 55.5 %gather_all.1 = (bf16[8,320,1024]{2,1,0:T(8,128)(2,1)}, bf16[1024,320]{1,0:T(8,128)(2,1)}, bf16[1024,320]{1,0:T(8,128)(2,1)}, bf16[3,4,80,320]{3,2,1,0:T(8,128)(2,1)}, f32[16,320]{1,0:T(8,128)}) custom-call(bf16[320,1024]{1,0:T(8,128)(2,1)} %bitcast.6, bf16[80,320]{1,0:T(8,128)(2,1)} %w_gate.1, bf16[80,320]{1,0:T(8,128)(2,1)} %w_x.1, bf16[80,320]{1,0:T(8,128)(2,1)} %w_out.1, ...), custom_call_target="tpu_custom_call" | custom-call | flops 10000000000 | bytes 100000000 | tf_op jit(solution)/shard_map/gather_all/pallas_call | solution.py:324
  58.6 31.0 %middle.1 = (bf16[1024,320]{1,0:T(8,128)(2,1)}, bf16[1024,320]{1,0:T(8,128)(2,1)}, f32[40,320]{1,0:T(8,128)}, bf16[320,1024]{1,0:T(8,128)(2,1)}, f32[8,24,128]{2,1,0:T(8,128)}, /*index=5*/bf16[4,8,80,320]{3,2,1,0:T(8,128)(2,1)}) custom-call(bf16[1024,320]{1,0:T(8,128)(2,1)} %get-tuple-element.33.gate, bf16[1024,320]{1,0:T(8,128)(2,1)} %get-tuple-element.34.xs, ...), custom_call_target="tpu_custom_call" | custom-call | flops 10000000000 | bytes 10000000 | tf_op jit(solution)/shard_map/middle/pallas_call | solution.py:635
  89.7 44.0 %finish_grads.1 = (f32[80,320]{1,0:T(8,128)}, f32[80,320]{1,0:T(8,128)}, f32[40,320]{1,0:T(8,128)}, f32[80,320]{1,0:T(8,128)}, f32[16,320]{1,0:T(8,128)}, /*index=5*/bf16[320,1024]{1,0:T(8,128)(2,1)}) custom-call(bf16[8,320,1024]{2,1,0:T(8,128)(2,1)} %get-tuple-element.32.features, bf16[1024,320]{1,0:T(8,128)(2,1)} %get-tuple-element.37.dgate, ...), custom_call_target="tpu_custom_call" | custom-call | flops 10000000000 | bytes 100000000 | tf_op jit(solution)/shard_map/finish_grads/pallas_call | solution.py:927
  133.7 2.3 %hand_out.1 = (f32[80,320]{1,0:T(8,128)}, f32[80,320]{1,0:T(8,128)}, f32[80,320]{1,0:T(8,128)}, f32[16,320]{1,0:T(8,128)}, bf16[320,1024]{1,0:T(8,128)(2,1)}, /*index=5*/f32[4,320]{1,0:T(4,128)}) custom-call(f32[40,320]{1,0:T(8,128)} %get-tuple-element.43.total, f32[80,320]{1,0:T(8,128)} %get-tuple-element.44.refs_0_, f32[80,320]{1,0:T(8,128)} %get-tuple-element.45.refs_1_, ...), custom_call_target="tpu_custom_call" | custom-call | tf_op jit(solution)/shard_map/hand_out/pallas_call | solution.py:983
  136.0 1.4 %slice_reduce_fusion = (f32[320]{0:T(512)}, f32[320]{0:T(512)S(1)}, f32[320]{0:T(512)}) fusion(f32[40,320]{1,0:T(8,128)} %get-tuple-element.43.total), kind=kLoop, calls=%fused_computation | loop fusion | bytes 7680 | tf_op jit(solution)/shard_map/slice | solution.py:1035
  137.4 0.1 reshape_squeeze.3
  137.5 0.6 reduce_sum.9
